TPU v7x, 32 devices: a whole 2x2x4 slice. The times are simulated.
32 devices in a mesh: dp: 16 (over z, x, core), tensor: 2 (over y).
Axes of the slice: x: 2, y: 2, z: 4, core: 2. Of those that a mesh axis runs over, the one named last changes fastest.
Arguments:
- tokens: bfloat16 [16384, 1024], P(('dp', 'tensor')), may hold values from -6 to 6
- cotangent: bfloat16 [16384, 1024], P(('dp', 'tensor')), may hold values from -6 to 6
- segment_ids: int32 [16, 1024], P('dp'), may hold values from 0 to 16, as said below
- w_qkv: float32 [3, 1024, 1024], P(None, 'dp', 'tensor'), may hold values from -0.1875 to 0.1875
- m_qkv: float32 [3, 1024, 1024], P(None, 'dp', 'tensor'), may hold values from -384 to 384
- a_qkv: float32 [3, 1024, 1024], P(None, 'dp', 'tensor'), may hold values from -0.1875 to 0.1875
- w_bqv: float32 [2, 1024], P(None, 'tensor'), may hold values from -6 to 6
- m_bqv: float32 [2, 1024], P(None, 'tensor'), may hold values from -768 to 768
- a_bqv: float32 [2, 1024], P(None, 'tensor'), may hold values from -6 to 6
- w_out: float32 [1024, 1024], P('tensor', 'dp'), may hold values from -1.5 to 1.5
- m_out: float32 [1024, 1024], P('tensor', 'dp'), may hold values from -80 to 80
- a_out: float32 [1024, 1024], P('tensor', 'dp'), may hold values from -1.5 to 1.5
- w_up: float32 [1024, 4096], P('dp', 'tensor'), may hold values from -0.1875 to 0.1875
- m_up: float32 [1024, 4096], P('dp', 'tensor'), may hold values from -224 to 224
- a_up: float32 [1024, 4096], P('dp', 'tensor'), may hold values from -0.1875 to 0.1875
- w_bup: float32 [4096], P('tensor'), may hold values from -6 to 6
- m_bup: float32 [4096], P('tensor'), may hold values from -224 to 224
- a_bup: float32 [4096], P('tensor'), may hold values from -6 to 6
- w_down: float32 [4096, 1024], P('tensor', 'dp'), may hold values from -0.09375 to 0.09375
- m_down: float32 [4096, 1024], P('tensor', 'dp'), may hold values from -384 to 384
- a_down: float32 [4096, 1024], P('tensor', 'dp'), may hold values from -0.09375 to 0.09375
- w_vec: float32 [6, 1024], replicated
- m_vec: float32 [6, 1024], replicated, may hold values from -768 to 768
- a_vec: float32 [6, 1024], replicated
Outputs:
- layer_out: bfloat16 [16384, 1024], P(('dp', 'tensor'))
- grad_tokens: bfloat16 [16384, 1024], P(('dp', 'tensor'))
- newm_qkv: float32 [3, 1024, 1024], P(None, 'dp', 'tensor')
- neww_qkv: float32 [3, 1024, 1024], P(None, 'dp', 'tensor')
- newa_qkv: float32 [3, 1024, 1024], P(None, 'dp', 'tensor')
- newm_bqv: float32 [2, 1024], P(None, 'tensor')
- neww_bqv: float32 [2, 1024], P(None, 'tensor')
- newa_bqv: float32 [2, 1024], P(None, 'tensor')
- newm_out: float32 [1024, 1024], P('tensor', 'dp')
- neww_out: float32 [1024, 1024], P('tensor', 'dp')
- newa_out: float32 [1024, 1024], P('tensor', 'dp')
- newm_up: float32 [1024, 4096], P('dp', 'tensor')
- neww_up: float32 [1024, 4096], P('dp', 'tensor')
- newa_up: float32 [1024, 4096], P('dp', 'tensor')
- newm_bup: float32 [4096], P('tensor')
- neww_bup: float32 [4096], P('tensor')
- newa_bup: float32 [4096], P('tensor')
- newm_down: float32 [4096, 1024], P('tensor', 'dp')
- neww_down: float32 [4096, 1024], P('tensor', 'dp')
- newa_down: float32 [4096, 1024], P('tensor', 'dp')
- newm_vec: float32 [6, 1024], replicated
- neww_vec: float32 [6, 1024], replicated
- newa_vec: float32 [6, 1024], replicated
Inputs may be any that keep to these rules, and one draw needn't show every extreme that they name: `segment_ids`: within each sequence the ids start at 0 and rise by one where a document ends; every document has 60 to 800 tokens; some document has exactly 800, and some sequence reaches the largest id.
All inputs are finite; a program needn't handle non-finite values.
Results may differ from a plain program's by a relative error of at most 0.015.
Values may be sent and summed in bfloat16 or wider, within the bound.
No kernel may reach another device: no remote copies, remote signals or barrier semaphores. Data moves between devices by JAX's collectives and lax.ppermute only.
A program may use at most 192 MiB of HBM per device.

v0:
```python
import math

import jax
import jax.numpy as jnp
from jax import lax
from jax.sharding import PartitionSpec as P

HEAD_DIM = 64
SEQ_LEN = 1024
SEQ_GRP = 1
QBLOCK = 512


NORM_EPS = 1e-05
MOMENTUM = 0.9
AVERAGE = 0.75
MATRIX_RATE = 0.05
FASTER_RATE = 0.25


def layer_norm(values, gain, shift):
    centred = values - jnp.mean(values, axis=-1, keepdims=True)
    spread = jnp.mean(centred * centred, axis=-1, keepdims=True)
    return centred * lax.rsqrt(spread + NORM_EPS) * gain + shift


def gelu_exact(values):
    return jax.nn.gelu(values, approximate=False)


def advance(weight, moment, average, gradient, step_rate):
    new_moment = MOMENTUM * moment + gradient
    new_weight = weight - step_rate * (gradient + MOMENTUM * new_moment)
    new_average = AVERAGE * average + (1.0 - AVERAGE) * new_weight
    return (new_moment, new_weight, new_average)


def attend_forward(packed, segment_ids):
    seq_count, length = segment_ids.shape
    blocks_per = length // QBLOCK
    dev_width = packed.shape[2]
    local_heads = dev_width // HEAD_DIM
    score_scale = HEAD_DIM ** (-0.5)
    shaped = packed.reshape(3, seq_count, length, local_heads, HEAD_DIM)

    def one_sequence(inputs):
        query_all, key_all, value_all, seg_all = inputs

        def one_block(block_index):
            start = block_index * QBLOCK
            query_rows = lax.dynamic_slice_in_dim(query_all, start, QBLOCK, 0)
            row_seg = lax.dynamic_slice_in_dim(seg_all, start, QBLOCK, 0)
            scores = (
                jnp.einsum("qhd,khd->hqk", query_rows, key_all, preferred_element_type=jnp.float32)
                * score_scale
            )
            same_doc = (row_seg[:, None] == seg_all[None, :])[None]
            scores = jnp.where(same_doc, scores, -1e30)
            row_max = jnp.max(scores, axis=-1, keepdims=True)
            exp_scores = jnp.exp(scores - row_max)
            row_total = jnp.sum(exp_scores, axis=-1, keepdims=True)
            probs16 = (exp_scores / row_total).astype(jnp.bfloat16)
            context = jnp.einsum(
                "hqk,khd->qhd", probs16, value_all, preferred_element_type=jnp.float32
            )
            return (
                context.astype(jnp.bfloat16).reshape(QBLOCK, dev_width),
                (row_max + jnp.log(row_total))[..., 0],
            )

        context, logsum = lax.map(one_block, jnp.arange(blocks_per, dtype=jnp.int32))
        return (context.reshape(length, dev_width), logsum)

    context, logsum = lax.map(one_sequence, (shaped[0], shaped[1], shaped[2], segment_ids))
    return (context.reshape(seq_count * length, dev_width), logsum)


def attend_backward(packed, context_grad, logsum, segment_ids):
    seq_count, length = segment_ids.shape
    blocks_per = length // QBLOCK
    dev_width = packed.shape[2]
    local_heads = dev_width // HEAD_DIM
    score_scale = HEAD_DIM ** (-0.5)
    shaped = packed.reshape(3, seq_count, length, local_heads, HEAD_DIM)
    grad_shaped = context_grad.reshape(seq_count, length, local_heads, HEAD_DIM)

    def one_sequence(inputs):
        query_all, key_all, value_all, grad_all, lse_all, seg_all = inputs

        def one_block(carry, block_index):
            key_grad, value_grad = carry
            start = block_index * QBLOCK
            query_rows = lax.dynamic_slice_in_dim(query_all, start, QBLOCK, 0)
            grad_rows = lax.dynamic_slice_in_dim(grad_all, start, QBLOCK, 0)
            row_seg = lax.dynamic_slice_in_dim(seg_all, start, QBLOCK, 0)
            row_lse = lax.dynamic_index_in_dim(lse_all, block_index, 0, keepdims=False)
            scores = (
                jnp.einsum("qhd,khd->hqk", query_rows, key_all, preferred_element_type=jnp.float32)
                * score_scale
            )
            same_doc = (row_seg[:, None] == seg_all[None, :])[None]
            probs = jnp.where(same_doc, jnp.exp(scores - row_lse[..., None]), 0.0)
            value_grad = value_grad + jnp.einsum(
                "hqk,qhd->khd",
                probs.astype(jnp.bfloat16),
                grad_rows,
                preferred_element_type=jnp.float32,
            )
            prob_grad = jnp.einsum(
                "qhd,khd->hqk", grad_rows, value_all, preferred_element_type=jnp.float32
            )
            inner_sum = jnp.sum(probs * prob_grad, axis=-1, keepdims=True)
            score_grad = (probs * (prob_grad - inner_sum)).astype(jnp.bfloat16)
            query_grad = (
                jnp.einsum("hqk,khd->qhd", score_grad, key_all, preferred_element_type=jnp.float32)
                * score_scale
            )
            key_grad = (
                key_grad
                + jnp.einsum(
                    "hqk,qhd->khd", score_grad, query_rows, preferred_element_type=jnp.float32
                )
                * score_scale
            )
            return ((key_grad, value_grad), query_grad)

        zero_grad = jnp.zeros(key_all.shape, jnp.float32)
        (key_grad, value_grad), query_grad = lax.scan(
            one_block, (zero_grad, zero_grad), jnp.arange(blocks_per, dtype=jnp.int32)
        )
        return (query_grad.reshape(key_all.shape), key_grad, value_grad)

    query_grad, key_grad, value_grad = lax.map(
        one_sequence, (shaped[0], shaped[1], shaped[2], grad_shaped, logsum, segment_ids)
    )
    total_rows = seq_count * length
    return jnp.stack(
        [
            query_grad.reshape(total_rows, dev_width),
            key_grad.reshape(total_rows, dev_width),
            value_grad.reshape(total_rows, dev_width),
        ]
    )


def body(
    tokens,
    cotangent,
    segment_ids,
    w_qkv,
    m_qkv,
    a_qkv,
    w_bqv,
    m_bqv,
    a_bqv,
    w_out,
    m_out,
    a_out,
    w_up,
    m_up,
    a_up,
    w_bup,
    m_bup,
    a_bup,
    w_down,
    m_down,
    a_down,
    w_vec,
    m_vec,
    a_vec,
):
    shards16 = (
        w_qkv.astype(jnp.bfloat16),
        w_out.astype(jnp.bfloat16),
        w_up.astype(jnp.bfloat16),
        w_down.astype(jnp.bfloat16),
    )
    qkv16, out16, up16, down16 = (
        lax.all_gather(shards16[0], "dp", axis=1, tiled=True),
        lax.all_gather(shards16[1], "dp", axis=1, tiled=True),
        lax.all_gather(shards16[2], "dp", axis=0, tiled=True),
        lax.all_gather(shards16[3], "dp", axis=1, tiled=True),
    )
    tok_full = lax.all_gather(tokens, "tensor", axis=0, tiled=True)
    bias_rows = jnp.stack([w_bqv[0], jnp.zeros_like(w_bqv[0]), w_bqv[1]])[:, None, :]
    packed = (
        jnp.einsum("nd,kde->kne", tok_full, qkv16, preferred_element_type=jnp.float32) + bias_rows
    ).astype(jnp.bfloat16)
    context, logsum = attend_forward(packed, segment_ids)
    attn_terms = jnp.dot(context, out16, preferred_element_type=jnp.float32)
    attended = lax.psum_scatter(attn_terms, "tensor", scatter_dimension=0, tiled=True)
    first_sum = tokens.astype(jnp.float32) + attended + w_vec[0]
    hidden, first_pull = jax.vjp(layer_norm, first_sum, w_vec[2], w_vec[3])
    hidden_full = lax.all_gather(hidden.astype(jnp.bfloat16), "tensor", axis=0, tiled=True)
    upper = jnp.dot(hidden_full, up16, preferred_element_type=jnp.float32) + w_bup
    active, gelu_pull = jax.vjp(gelu_exact, upper)
    active16 = active.astype(jnp.bfloat16)
    mixed_terms = jnp.dot(active16, down16, preferred_element_type=jnp.float32)
    mixed = lax.psum_scatter(mixed_terms, "tensor", scatter_dimension=0, tiled=True)
    second_sum = hidden + mixed + w_vec[1]
    normed, second_pull = jax.vjp(layer_norm, second_sum, w_vec[4], w_vec[5])
    layer_out = normed.astype(jnp.bfloat16)
    qkv16, out16, up16, down16 = (
        lax.all_gather(shards16[0], "dp", axis=1, tiled=True),
        lax.all_gather(shards16[1], "dp", axis=1, tiled=True),
        lax.all_gather(shards16[2], "dp", axis=0, tiled=True),
        lax.all_gather(shards16[3], "dp", axis=1, tiled=True),
    )
    second_grad, gain2_grad, shift2_grad = second_pull(cotangent.astype(jnp.float32))
    mixed_full = lax.all_gather(second_grad.astype(jnp.bfloat16), "tensor", axis=0, tiled=True)
    active_grad = jnp.einsum("nd,fd->nf", mixed_full, down16, preferred_element_type=jnp.float32)
    down_grad = jnp.einsum("nf,nd->fd", active16, mixed_full, preferred_element_type=jnp.float32)
    upper_grad = gelu_pull(active_grad)[0]
    upper16 = upper_grad.astype(jnp.bfloat16)
    hidden_terms = jnp.einsum("nf,df->nd", upper16, up16, preferred_element_type=jnp.float32)
    up_grad = jnp.einsum("nd,nf->df", hidden_full, upper16, preferred_element_type=jnp.float32)
    hidden_grad = second_grad + lax.psum_scatter(
        hidden_terms, "tensor", scatter_dimension=0, tiled=True
    )
    first_grad, gain1_grad, shift1_grad = first_pull(hidden_grad)
    attended_full = lax.all_gather(first_grad.astype(jnp.bfloat16), "tensor", axis=0, tiled=True)
    context_grad = jnp.einsum(
        "nd,ed->ne", attended_full, out16, preferred_element_type=jnp.float32
    ).astype(jnp.bfloat16)
    out_grad = jnp.einsum("ne,nd->ed", context, attended_full, preferred_element_type=jnp.float32)
    packed_grad = attend_backward(packed, context_grad, logsum, segment_ids)
    bqv_local = jnp.stack([jnp.sum(packed_grad[0], axis=0), jnp.sum(packed_grad[2], axis=0)])
    packed16 = packed_grad.astype(jnp.bfloat16)
    token_terms = jnp.einsum("kne,kde->nd", packed16, qkv16, preferred_element_type=jnp.float32)
    qkv_grad = jnp.einsum("nd,kne->kde", tok_full, packed16, preferred_element_type=jnp.float32)
    grad_tokens = (
        first_grad
        + lax.psum_scatter(
            token_terms.astype(jnp.bfloat16), "tensor", scatter_dimension=0, tiled=True
        ).astype(jnp.float32)
    ).astype(jnp.bfloat16)
    qkv_part, out_part, up_part, down_part = (
        lax.psum_scatter(qkv_grad, "dp", scatter_dimension=1, tiled=True),
        lax.psum_scatter(out_grad, "dp", scatter_dimension=1, tiled=True),
        lax.psum_scatter(up_grad, "dp", scatter_dimension=0, tiled=True),
        lax.psum_scatter(down_grad, "dp", scatter_dimension=1, tiled=True),
    )
    tensor_index = lax.axis_index("tensor")
    tensor_count = lax.axis_size("tensor")
    dev_width = w_bqv.shape[1]
    unit_width = w_bup.shape[0]
    bqv_full = lax.dynamic_update_slice(
        jnp.zeros((2, dev_width * tensor_count), jnp.float32),
        bqv_local,
        (0, tensor_index * dev_width),
    )
    bup_full = lax.dynamic_update_slice(
        jnp.zeros((unit_width * tensor_count,), jnp.float32),
        jnp.sum(upper_grad, axis=0),
        (tensor_index * unit_width,),
    )
    vec_local = jnp.stack(
        [
            jnp.sum(first_grad, axis=0),
            jnp.sum(second_grad, axis=0),
            gain1_grad,
            shift1_grad,
            gain2_grad,
            shift2_grad,
        ]
    )
    bqv_sum, bup_sum, vec_grad = lax.psum((bqv_full, bup_full, vec_local), ("dp", "tensor"))
    bqv_grad = lax.dynamic_slice_in_dim(bqv_sum, tensor_index * dev_width, dev_width, 1)
    bup_grad = lax.dynamic_slice_in_dim(bup_sum, tensor_index * unit_width, unit_width, 0)
    base_rate = 1.0 / math.sqrt(SEQ_GRP * SEQ_LEN * lax.axis_size("dp"))
    slow_rate = MATRIX_RATE * base_rate
    fast_rate = FASTER_RATE * base_rate
    nm_qkv, nw_qkv, na_qkv = advance(w_qkv, m_qkv, a_qkv, qkv_part, slow_rate)
    nm_bqv, nw_bqv, na_bqv = advance(w_bqv, m_bqv, a_bqv, bqv_grad, slow_rate)
    nm_out, nw_out, na_out = advance(w_out, m_out, a_out, out_part, fast_rate)
    nm_up, nw_up, na_up = advance(w_up, m_up, a_up, up_part, slow_rate)
    nm_bup, nw_bup, na_bup = advance(w_bup, m_bup, a_bup, bup_grad, fast_rate)
    nm_down, nw_down, na_down = advance(w_down, m_down, a_down, down_part, slow_rate)
    nm_vec, nw_vec, na_vec = advance(w_vec, m_vec, a_vec, vec_grad, slow_rate)
    return (
        layer_out,
        grad_tokens,
        nm_qkv,
        nw_qkv,
        na_qkv,
        nm_bqv,
        nw_bqv,
        na_bqv,
        nm_out,
        nw_out,
        na_out,
        nm_up,
        nw_up,
        na_up,
        nm_bup,
        nw_bup,
        na_bup,
        nm_down,
        nw_down,
        na_down,
        nm_vec,
        nw_vec,
        na_vec,
    )


def solution(mesh):
    in_specs = (
        P(("dp", "tensor"), None),
        P(("dp", "tensor"), None),
        P("dp", None),
        P(None, "dp", "tensor"),
        P(None, "dp", "tensor"),
        P(None, "dp", "tensor"),
        P(None, "tensor"),
        P(None, "tensor"),
        P(None, "tensor"),
        P("tensor", "dp"),
        P("tensor", "dp"),
        P("tensor", "dp"),
        P("dp", "tensor"),
        P("dp", "tensor"),
        P("dp", "tensor"),
        P("tensor"),
        P("tensor"),
        P("tensor"),
        P("tensor", "dp"),
        P("tensor", "dp"),
        P("tensor", "dp"),
        P(),
        P(),
        P(),
    )
    out_specs = (
        P(("dp", "tensor"), None),
        P(("dp", "tensor"), None),
        P(None, "dp", "tensor"),
        P(None, "dp", "tensor"),
        P(None, "dp", "tensor"),
        P(None, "tensor"),
        P(None, "tensor"),
        P(None, "tensor"),
        P("tensor", "dp"),
        P("tensor", "dp"),
        P("tensor", "dp"),
        P("dp", "tensor"),
        P("dp", "tensor"),
        P("dp", "tensor"),
        P("tensor"),
        P("tensor"),
        P("tensor"),
        P("tensor", "dp"),
        P("tensor", "dp"),
        P("tensor", "dp"),
        P(),
        P(),
        P(),
    )
    return jax.shard_map(body, mesh=mesh, in_specs=in_specs, out_specs=out_specs, check_vma=False)
```

profile of v0, /device:TPU:1, one launch (start us, length us, event | category | flops | bytes accessed | tf_op | source)
XLA Modules:
  0.0 1052.0 jit_solution(267220995793951752)
XLA Ops:
  12.3 32.3 %all-gather.11.cloned.1.call-done = bf16[1024,1024]{1,0:T(8,128)(2,1)} async-done(((bf16[512,1024]{1,0:T(8,128)(2,1)}), bf16[1024,1024]{1,0:T(8,128)(2,1)}) %all-gather.11.cloned.1.call-update) | async-done | bytes 2097168 | tf_op jit(solution)/shard_map/all_gather | solution.py:184
  44.6 48.9 %all-gather.9.cloned.1.call-done = bf16[3,1024,512]{2,1,0:T(8,128)(2,1)} async-done(((bf16[3,64,512]{2,1,0:T(8,128)(2,1)}), bf16[3,1024,512]{2,1,0:T(8,128)(2,1)}) %all-gather.9.cloned.1.call-update) | async-done | bytes 3145744 | tf_op jit(solution)/shard_map/all_gather | solution.py:179
  101.2 32.9 %while.47 = (s32[]{:T(128)}, bf16[2,512,512]{2,1,0:T(8,128)(2,1)}, f32[2,8,512]{2,1,0:T(8,128)S(1)}, s32[2]{0:T(128)S(1)}, s32[1024]{0:T(1024)S(1)}, /*index=5*/...) while((s32[]{:T(128)}, bf16[2,512,512]{2,1,0:T(8,128)(2,1)}, ...), condition=%wide.region_3.4_spmd, body=%wide.region_0.3_spmd.sunk | while | flops 1124855808 | bytes 57813192 | solution.py:71
  141.1 50.1 %reduce-scatter.8.cloned.1.call-done = f32[512,1024]{1,0:T(8,128)} async-done(((f32[1024,1024]{1,0:T(8,128)}), f32[512,1024]{1,0:T(8,128)}) %reduce-scatter.8.cloned.1.call-update) | async-done | bytes 2097168 | tf_op jit(solution)/shard_map/reduce_scatter | solution.py:191
  196.7 48.0 %all-gather.17.cloned.1.call-done = bf16[1024,2048]{1,0:T(8,128)(2,1)} async-done(((bf16[64,2048]{1,0:T(8,128)(2,1)}), bf16[1024,2048]{1,0:T(8,128)(2,1)}) %all-gather.17.cloned.1.call-update) | async-done | bytes 4194320 | tf_op jit(solution)/shard_map/all_gather | solution.py:181
  244.7 33.1 %all-gather.15.cloned.1.call-done = bf16[1024,1024]{1,0:T(8,128)(2,1)} async-done(((bf16[512,1024]{1,0:T(8,128)(2,1)}), bf16[1024,1024]{1,0:T(8,128)(2,1)}) %all-gather.15.cloned.1.call-update) | async-done | bytes 2097168 | tf_op jit(solution)/shard_map/all_gather | solution.py:194
  277.8 26.2 %multiply_convert_fusion.1 = (bf16[1024,2048]{1,0:T(8,128)(2,1)}, f32[1024,2048]{1,0:T(8,128)}, f32[1024,2048]{1,0:T(8,128)}) fusion(f32[2048]{0:T(1024)S(1)} %copy-done.32, bf16[1024,1024]{1,0:T(8,128)(2,1)} %all-gather.15.cloned.1.call-done, bf16[1024,2048]{1,0:T(8,128)(2,1)} %all-gather.17.cloned.1.call-done), kind=kOutput, calls=%fused_computation.39 | convolution fusion | flops 4433379328 | bytes 27271168 | tf_op jit(solution)/shard_map/dot_general | solution.py:195
  304.0 27.5 %all-gather.19.cloned.1.call-done = bf16[2048,1024]{0,1:T(8,128)(2,1)} async-done(((bf16[2048,64]{0,1:T(8,128)(2,1)}), bf16[2048,1024]{0,1:T(8,128)(2,1)}) %all-gather.19.cloned.1.call-update) | async-done | bytes 4194320 | tf_op jit(solution)/shard_map/all_gather | solution.py:182
  331.5 10.0 fusion.58
  342.0 52.0 %reduce-scatter.10.cloned.1.call-done = f32[512,1024]{1,0:T(8,128)} async-done(((f32[1024,1024]{1,0:T(8,128)}), f32[512,1024]{1,0:T(8,128)}) %reduce-scatter.10.cloned.1.call-update) | async-done | bytes 2097168 | tf_op jit(solution)/shard_map/reduce_scatter | solution.py:199
  403.9 33.2 %all-gather.21.cloned.1.call-done = bf16[1024,1024]{1,0:T(8,128)(2,1)} async-done(((bf16[512,1024]{1,0:T(8,128)(2,1)}), bf16[1024,1024]{1,0:T(8,128)(2,1)}) %all-gather.21.cloned.1.call-update) | async-done | bytes 2097168 | tf_op jit(solution)/shard_map/all_gather | solution.py:210
  437.1 13.9 %fusion.46 = (f32[2048]{0:T(1024)}, bf16[1024,2048]{1,0:T(8,128)(2,1)S(1)}) fusion(f32[1024,2048]{1,0:T(8,128)} %get-tuple-element.364, f32[1024,2048]{1,0:T(8,128)} %get-tuple-element.391, f32[2048]{0:T(1024)S(1)} %copy-done.32, bf16[1024,1024]{1,0:T(8,128)(2,1)} %all-gather.21.cloned.1.call-done, bf16[2048,1024]{0,1:T(8,128)(2,1)} %all-gather.19.cloned.1.call-done), kind=kOutput, calls=%fused_computation.125 | convolution fusion | flops 4328519680 | bytes 27279360 | tf_op jit(solution)/shard_map/nd,fd->nf/dot_general | solution.py:211
  459.2 54.5 %reduce-scatter.12.cloned.1.call-done = f32[512,1024]{1,0:T(8,128)} async-done(((f32[1024,1024]{1,0:T(8,128)}), f32[512,1024]{1,0:T(8,128)}) %reduce-scatter.12.cloned.1.call-update) | async-done | bytes 2097168 | tf_op jit(solution)/shard_map/reduce_scatter | solution.py:217
  522.3 10.8 %fusion.37 = f32[1024,2048]{1,0:T(8,128)} fusion(bf16[1024,1024]{1,0:T(8,128)(2,1)} %all-gather.15.cloned.1.call-done, bf16[1024,2048]{1,0:T(8,128)(2,1)} %copy-done.35), kind=kOutput, calls=%fused_computation.72 | convolution fusion | flops 4294967296 | bytes 14680064 | tf_op jit(solution)/shard_map/nd,nf->df/dot_general | solution.py:216
  533.1 10.7 %fusion.60 = f32[2048,1024]{0,1:T(8,128)} fusion(bf16[1024,2048]{1,0:T(8,128)(2,1)} %get-tuple-element.363, bf16[1024,1024]{1,0:T(8,128)(2,1)} %all-gather.21.cloned.1.call-done), kind=kOutput, calls=%fused_computation.138 | convolution fusion | flops 4294967296 | bytes 14680064 | tf_op jit(solution)/shard_map/nf,nd->fd/dot_general | solution.py:212
  543.9 11.4 %all-gather.23.cloned.1.call-done = bf16[1024,1024]{1,0:T(8,128)(2,1)} async-done(((bf16[512,1024]{1,0:T(8,128)(2,1)}), bf16[1024,1024]{1,0:T(8,128)(2,1)}) %all-gather.23.cloned.1.call-update) | async-done | bytes 2097168 | tf_op jit(solution)/shard_map/all_gather | solution.py:221
  559.1 95.9 %while.48 = (s32[]{:T(128)}, f32[1024,8,64]{0,2,1:T(8,128)}, f32[1024,8,64]{0,2,1:T(8,128)}, f32[2,512,8,64]{1,3,2,0:T(8,128)}, s32[2]{0:T(128)S(1)}, /*index=5*...) while((s32[]{:T(128)}, f32[1024,8,64]{0,2,1:T(8,128)}, ...), condition=%wide.region_17.18_spmd.clone, body=%wide.region_15.17_spmd.clone.sunk | while | flops 2725507072 | bytes 221604432 | solution.py:128
  568.1 12.9 %multiply_reduce_fusion.6 = (f32[8,512]{1,0:T(8,128)}, f32[8,512,1024]{2,1,0:T(8,128)}) fusion(f32[8,512,1024]{2,1,0:T(8,128)S(1)} %fusion.118, f32[8,512]{1,0:T(8,128)} %dynamic-slice_bitcast_fusion.2, bf16[1024,8,64]{0,2,1:T(8,128)(2,1)} %copy-done.1, bf16[1024,8,64]{0,2,1:T(8,128)(2,1)} %get-tuple-element.591, s32[]{:T(128)S(6)} %select_n.56, ...), kind=kOutput, calls=%fused_computation.16.clone.1 | convolution fusion | flops 557838336 | bytes 35684356 | tf_op jit(solution)/shard_map/while/body/eval_jaxpr/while/body/eval_jaxpr/qhd,khd->hqk/dot_general | solution.py:98
  616.3 11.9 %multiply_reduce_fusion.6 = (f32[8,512]{1,0:T(8,128)}, f32[8,512,1024]{2,1,0:T(8,128)}) fusion(f32[8,512,1024]{2,1,0:T(8,128)S(1)} %fusion.118, f32[8,512]{1,0:T(8,128)} %dynamic-slice_bitcast_fusion.2, bf16[1024,8,64]{0,2,1:T(8,128)(2,1)} %copy-done.1, bf16[1024,8,64]{0,2,1:T(8,128)(2,1)} %get-tuple-element.591, s32[]{:T(128)S(6)} %select_n.56, ...), kind=kOutput, calls=%fused_computation.16.clone.1 | convolution fusion | flops 557838336 | bytes 35684356 | tf_op jit(solution)/shard_map/while/body/eval_jaxpr/while/body/eval_jaxpr/qhd,khd->hqk/dot_general | solution.py:98
  704.8 41.8 %all-reduce.1 = (f32[2,1024]{1,0:T(2,128)S(1)}, f32[4096]{0:T(1024)S(1)}, f32[6,1024]{1,0:T(8,128)S(1)}) all-reduce(f32[2,1024]{1,0:T(2,128)S(1)} %maximum_dynamic-update-slice_fusion, f32[4096]{0:T(1024)S(1)} %dynamic_update_slice.32, f32[6,1024]{1,0:T(8,128)S(1)} %stack.36), channel_id=1, replica_groups=mesh['dp'=16,'tensor'=2] {'dp','tensor'}, use_global_device_ids=true, to_apply=%region_22.23 | all-reduce | flops 12288 | bytes 98304 | tf_op jit(solution)/shard_map/psum | solution.py:267
  753.3 17.4 %reduce-scatter.20.cloned.1.call-done = f32[2048,64]{0,1:T(8,128)} async-done(((f32[2048,1024]{0,1:T(8,128)}), f32[2048,64]{0,1:T(8,128)}) %reduce-scatter.20.cloned.1.call-update) | async-done | bytes 524304 | tf_op jit(solution)/shard_map/reduce_scatter | solution.py:241
  773.2 171.2 %all-reduce.4.cloned.1.call-done = f32[3,1024,512]{2,0,1:T(4,128)} async-done(((f32[3,1024,512]{2,0,1:T(4,128)}), f32[3,1024,512]{2,0,1:T(4,128)}) %all-reduce.4.cloned.1.call-update) | async-done | bytes 6291472
  945.5 62.3 %reduce-scatter.16.cloned.1.call-done = f32[512,64]{0,1:T(8,128)} async-done(((f32[512,1024]{0,1:T(8,128)}), f32[512,64]{0,1:T(8,128)}) %reduce-scatter.16.cloned.1.call-update) | async-done | bytes 131088 | tf_op jit(solution)/shard_map/reduce_scatter | solution.py:239
  1012.0 30.5 %reduce-scatter.14.cloned.1.call-done = bf16[512,1024]{1,0:T(8,128)(2,1)} async-done(((bf16[1024,1024]{1,0:T(8,128)(2,1)}), bf16[512,1024]{1,0:T(8,128)(2,1)}) %reduce-scatter.14.cloned.1.call-update) | async-done | bytes 1048592 | tf_op jit(solution)/shard_map/reduce_scatter | solution.py:233
  (229 shorter events, 219.2 us)
Async XLA Ops:
  7.2 37.4 %all-gather.11.cloned.1.call-start = ((), (), s32[]{:S(2)}) async-start(), calls=%async_computation.8 | async-start | bytes 3145728 | tf_op jit(solution)/shard_map/all_gather | solution.py:184
  7.9 85.5 %all-gather.9.cloned.1.call-start = ((), (), s32[]{:S(2)}) async-start(), calls=%async_computation.7 | async-start | bytes 3342336 | tf_op jit(solution)/shard_map/all_gather | solution.py:179
  9.7 124.3 %all-gather.13.cloned.1.call-start = ((), (), s32[]{:S(2)}) async-start(), calls=%async_computation.9 | async-start | bytes 1114112 | tf_op jit(solution)/shard_map/all_gather | solution.py:180
  11.3 179.8 %reduce-scatter.8.cloned.1.call-start = ((), (), s32[]{:S(2)}) async-start(), calls=%async_computation.10 | async-start | bytes 6291456 | tf_op jit(solution)/shard_map/reduce_scatter | solution.py:191
  138.8 105.9 %all-gather.17.cloned.1.call-start = ((), (), s32[]{:S(2)}) async-start(), calls=%async_computation.12 | async-start | bytes 4456448 | tf_op jit(solution)/shard_map/all_gather | solution.py:181
  140.8 137.0 %all-gather.15.cloned.1.call-start = ((), (), s32[]{:S(2)}) async-start(), calls=%async_computation.11 | async-start | bytes 3145728 | tf_op jit(solution)/shard_map/all_gather | solution.py:194
  193.1 84.7 %copy-start.32 = (f32[2048]{0:T(1024)S(1)}, f32[2048]{0:T(1024)}, u32[]{:S(2)}) copy-start(f32[2048]{0:T(1024)} %param.43) | copy-start | bytes 24580
  195.8 135.7 %all-gather.19.cloned.1.call-start = ((), (), s32[]{:S(2)}) async-start(), calls=%async_computation.13 | async-start | bytes 4456448 | tf_op jit(solution)/shard_map/all_gather | solution.py:182
  196.6 197.4 %reduce-scatter.10.cloned.1.call-start = ((), (), s32[]{:S(2)}) async-start(), calls=%async_computation.14 | async-start | bytes 6291456 | tf_op jit(solution)/shard_map/reduce_scatter | solution.py:199
  341.5 95.6 %all-gather.21.cloned.1.call-start = ((), (), s32[]{:S(2)}) async-start(), calls=%async_computation.15 | async-start | bytes 3145728 | tf_op jit(solution)/shard_map/all_gather | solution.py:210
  403.8 109.8 %reduce-scatter.12.cloned.1.call-start = ((), (), s32[]{:S(2)}) async-start(), calls=%async_computation.16 | async-start | bytes 6291456 | tf_op jit(solution)/shard_map/reduce_scatter | solution.py:217
  459.1 96.2 %all-gather.23.cloned.1.call-start = ((), (), s32[]{:S(2)}) async-start(), calls=%async_computation.17 | async-start | bytes 3145728 | tf_op jit(solution)/shard_map/all_gather | solution.py:221
  522.0 228.6 %reduce-scatter.18.cloned.1.call-start = ((), (), s32[]{:S(2)}) async-start(), calls=%async_computation.20 | async-start | bytes 8912896 | tf_op jit(solution)/shard_map/reduce_scatter | solution.py:240
  533.0 237.6 %reduce-scatter.20.cloned.1.call-start = ((), (), s32[]{:S(2)}) async-start(), calls=%async_computation.21 | async-start | bytes 8912896 | tf_op jit(solution)/shard_map/reduce_scatter | solution.py:241
  543.8 400.5 %all-reduce.4.cloned.1.call-start = ((), (), s32[]{:S(2)}) async-start(), calls=%async_computation.22 | async-start | bytes 16777216
  687.4 320.4 %reduce-scatter.16.cloned.1.call-start = ((), (), s32[]{:S(2)}) async-start(), calls=%async_computation.19 | async-start | bytes 2228224 | tf_op jit(solution)/shard_map/reduce_scatter | solution.py:239
  692.4 58.3 %copy-start.13 = (f32[64,2048]{1,0:T(8,128)S(1)}, f32[64,2048]{1,0:T(8,128)}, u32[]{:S(2)}) copy-start(f32[64,2048]{1,0:T(8,128)} %param.40) | copy-start | bytes 1572868
  692.4 58.3 %copy-start.21 = (f32[64,2048]{1,0:T(8,128)S(1)}, f32[64,2048]{1,0:T(8,128)}, u32[]{:S(2)}) copy-start(f32[64,2048]{1,0:T(8,128)} %param.42) | copy-start | bytes 1572868
  692.4 350.1 %reduce-scatter.14.cloned.1.call-start = ((), (), s32[]{:S(2)}) async-start(), calls=%async_computation.18 | async-start | bytes 3145728 | tf_op jit(solution)/shard_map/reduce_scatter | solution.py:233
  699.5 71.2 %copy-start.15 = (f32[2048,64]{0,1:T(8,128)S(1)}, f32[2048,64]{0,1:T(8,128)}, u32[]{:S(2)}) copy-start(f32[2048,64]{0,1:T(8,128)} %param.46) | copy-start | bytes 1572868
  699.5 71.2 %copy-start.22 = (f32[2048,64]{0,1:T(8,128)S(1)}, f32[2048,64]{0,1:T(8,128)}, u32[]{:S(2)}) copy-start(f32[2048,64]{0,1:T(8,128)} %param.48) | copy-start | bytes 1572868
  750.7 259.0 %copy-start.18 = (f32[3,64,512]{2,1,0:T(8,128)S(1)}, f32[3,64,512]{2,1,0:T(8,128)}, u32[]{:S(2)}) copy-start(f32[3,64,512]{2,1,0:T(8,128)} %param.31) | copy-start | bytes 1179652
  753.3 289.2 %copy-start.10 = (f32[512,1024]{1,0:T(8,128)S(1)}, f32[512,1024]{1,0:T(8,128)}, u32[]{:S(2)}) copy-start(f32[512,1024]{1,0:T(8,128)} %copy-done.9) | copy-start | bytes 6291460
  753.3 289.2 %copy-start.27 = (f32[512]{0:T(512)S(1)}, f32[512]{0:T(512)}, u32[]{:S(2)}) copy-start(f32[512]{0:T(512)} %copy-done.26) | copy-start | bytes 6148
  (38 other events, 262.3 us)
Sparse Core Ops, SparseCore 0:
  9.5 34.9 all-gather.10
  47.3 46.0 all-gather.8
  96.2 36.2 all-gather.12
  139.0 52.1 reduce-scatter.7
  193.7 50.9 all-gather.16
  246.7 31.0 all-gather.14
  280.5 50.9 all-gather.18
  341.6 52.3 reduce-scatter.9
  403.9 33.0 all-gather.20
  459.2 54.3 reduce-scatter.11
  522.2 33.0 all-gather.22
  559.2 103.2 reduce-scatter.17
  666.5 104.1 reduce-scatter.19
  774.3 170.0 all-reduce.3
  947.9 59.7 reduce-scatter.15
  1009.9 32.5 reduce-scatter.13
where the time goes:
time: 1060 us; the launch traced here: 1050 us
  waiting for transfers between devices  673 us (63%)
  matrix products  194 us (18%)
  other arithmetic  79.7 us (8%)
  blocking collectives  41.8 us (4%)
  local copies, waits for them, and re-layouts  39.2 us (4%)
  between operations  15.4 us (1%)
    unnamed x17, waiting for transfers between devices  172 us
    reduce_scatter x1, waiting for transfers between devices, body(): lax.psum_scatter(out_grad, 'dp', scatter_dimension=1, tiled=True)  62.3 us
    reduce_scatter x1, waiting for transfers between devices, body(): lax.psum_scatter(hidden_terms, 'tensor', scatter_dimension=0, tiled=True)  54.5 us
    reduce_scatter x1, waiting for transfers between devices, body(): lax.psum_scatter(mixed_terms, 'tensor', scatter_dimension=0, tiled=True)  52 us
    reduce_scatter x1, waiting for transfers between devices, body(): lax.psum_scatter(attn_terms, 'tensor', scatter_dimension=0, tiled=True)  50.1 us
    all_gather x1, waiting for transfers between devices, body(): lax.all_gather(shards16[0], 'dp', axis=1, tiled=True)  48.9 us
    all_gather x1, waiting for transfers between devices, body(): lax.all_gather(shards16[2], 'dp', axis=0, tiled=True)  48 us
    psum x1, blocking collectives, body(): lax.psum((bqv_full, bup_full, vec_local), ('dp', 'tensor'))  41.8 us
  transfers between devices with their start and end apart: 16, of which 14 were waited for; matrix products, arithmetic and copies ran while one was open for 24% of the time, Pallas kernels for 0%

commit v1 on v0

--- a/solution.py
+++ b/solution.py
@@ -3,7 +3,7 @@
 import jax
 import jax.numpy as jnp
 from jax import lax
-from jax.sharding import PartitionSpec as P
+from jax.sharding import Mesh, PartitionSpec as P
 
 HEAD_DIM = 64
 SEQ_LEN = 1024
@@ -141,6 +141,97 @@
             value_grad.reshape(total_rows, dev_width),
         ]
     )
+
+SWAP = [(core * 2 + side, side * 2 + core) for core in range(2) for side in range(2)]
+FLIP = [(0, 1), (1, 0)]
+
+
+def swap(values):
+    return lax.ppermute(values, ("core", "tensor"), SWAP)
+
+
+def core_exchange(values):
+    return lax.ppermute(values, "core", FLIP)
+
+
+def y_exchange(values):
+    return lax.ppermute(values, "tensor", FLIP)
+
+
+def chip_exchange(values, mask):
+    count = lax.axis_size("chip")
+    return lax.ppermute(values, "chip", [(k, k ^ mask) for k in range(count)])
+
+
+def bits():
+    chip = lax.axis_index("chip")
+    return (lax.axis_index("tensor"), chip & 1, (chip >> 1) & 1, (chip >> 2) & 1)
+
+
+STAGES = (
+    y_exchange,
+    lambda values: chip_exchange(values, 1),
+    lambda values: chip_exchange(values, 2),
+    lambda values: chip_exchange(values, 4),
+)
+Y, X, Z1, Z2 = range(4)
+
+
+def join(mine, stage, axis):
+    other = STAGES[stage](mine)
+    first = bits()[stage] == 0
+    return jnp.where(
+        first, jnp.stack([mine, other], axis), jnp.stack([other, mine], axis)
+    )
+
+
+def gather_pair(left, right):
+    rows, width = left.shape
+    if lax.axis_size("chip") != 8:
+        return tuple(
+            lax.all_gather(part, ("chip", "tensor"), axis=0, tiled=True) for part in (left, right)
+        )
+    both = jnp.stack([left, right])
+    both = join(both, Z1, 1)
+    both = join(both, Z2, 1)
+    left = join(join(both[0], X, 2), Y, 3)
+    right = join(join(both[1], Y, 2), X, 2)
+    return (left.reshape(16 * rows, width), right.reshape(16 * rows, width))
+
+
+def split(values, stage, axis):
+    bit = bits()[stage]
+    keep = lax.dynamic_index_in_dim(values, bit, axis, keepdims=False)
+    send = lax.dynamic_index_in_dim(values, 1 - bit, axis, keepdims=False)
+    other = STAGES[stage](send)
+    return (keep.astype(jnp.float32) + other.astype(jnp.float32)).astype(values.dtype)
+
+
+def reduce_pair(left, right):
+    width = left.shape[1]
+    if lax.axis_size("chip") != 8:
+        left, right = tuple(
+            lax.psum_scatter(part, ("chip", "tensor"), scatter_dimension=0, tiled=True)
+            for part in (left, right)
+        )
+        both = jnp.stack([left, right])
+    else:
+        left = left.reshape(2, 2, 2, 2, -1, width)
+        right = right.reshape(2, 2, 2, 2, -1, width)
+        left = split(split(left, Y, 3), X, 2)
+        right = split(split(right, X, 2), Y, 2)
+        both = jnp.stack([left, right])
+        both = split(split(both, Z2, 1), Z1, 1)
+    both = swap(both)
+    return (both[0].astype(jnp.float32), both[1].astype(jnp.float32))
+
+
+def sum_all(values):
+    if lax.axis_size("chip") != 8:
+        return lax.psum(values, ("chip", "tensor"))
+    for stage in (Y, X, Z1, Z2):
+        values = values + STAGES[stage](values)
+    return values
 
 
 def body(
@@ -169,91 +260,111 @@
     m_vec,
     a_vec,
 ):
-    shards16 = (
-        w_qkv.astype(jnp.bfloat16),
-        w_out.astype(jnp.bfloat16),
-        w_up.astype(jnp.bfloat16),
-        w_down.astype(jnp.bfloat16),
-    )
-    qkv16, out16, up16, down16 = (
-        lax.all_gather(shards16[0], "dp", axis=1, tiled=True),
-        lax.all_gather(shards16[1], "dp", axis=1, tiled=True),
-        lax.all_gather(shards16[2], "dp", axis=0, tiled=True),
-        lax.all_gather(shards16[3], "dp", axis=1, tiled=True),
-    )
-    tok_full = lax.all_gather(tokens, "tensor", axis=0, tiled=True)
-    bias_rows = jnp.stack([w_bqv[0], jnp.zeros_like(w_bqv[0]), w_bqv[1]])[:, None, :]
+    f32, bf16 = jnp.float32, jnp.bfloat16
+    core = lax.axis_index("core")
+    dev_width = w_bqv.shape[1]
+    unit_width = w_bup.shape[0]
+    rows = tokens.shape[0]
+    half = dev_width // 2
+    tokens = swap(tokens)
+    qkv_shard = w_qkv.astype(bf16)
+    qkv_halves = swap(
+        jnp.stack([jnp.concatenate([qkv_shard[k, :, h * half : (h + 1) * half] for k in range(3)], 1) for h in range(2)])
+    )
+    segments = swap(segment_ids)
+    biases = swap(jnp.concatenate([w_bqv.reshape(-1), w_bup]))
+    b_qv = biases[: 2 * dev_width].reshape(2, dev_width)
+    b_up = biases[2 * dev_width :]
+    out_shard = w_out.T.astype(bf16)
+    up_shard = w_up.astype(bf16)
+    down_shard = w_down.T.astype(bf16)
+    up_out = swap(
+        jnp.stack(
+            [
+                jnp.concatenate([out_shard[:, h * half : (h + 1) * half], up_shard[:, h * unit_width // 2 : (h + 1) * unit_width // 2]], 1)
+                for h in range(2)
+            ]
+        )
+    )
+    down_halves = swap(
+        jnp.stack([down_shard[:, h * unit_width // 2 : (h + 1) * unit_width // 2] for h in range(2)])
+    )
+    cotangent = swap(cotangent)
+    tok_full = jnp.concatenate([tokens, core_exchange(tokens)])
+    segments = jnp.where(core == 1, jnp.roll(segments, rows, axis=1), segments)
+    qkv_a, qkv_b = gather_pair(qkv_halves[0], qkv_halves[1])
+    uo_a, uo_b = gather_pair(up_out[0], up_out[1])
+    down_a, down_b = gather_pair(down_halves[0], down_halves[1])
+    qkv16 = jnp.stack(
+        [jnp.concatenate([part[:, k * half : (k + 1) * half] for part in (qkv_a, qkv_b)], 1) for k in range(3)]
+    )
+    out_t = jnp.concatenate([uo_a[:, :half], uo_b[:, :half]], 1)
+    up16 = jnp.concatenate([uo_a[:, half:], uo_b[:, half:]], 1)
+    down_t = jnp.concatenate([down_a, down_b], 1)
+
+    bias_rows = jnp.stack([b_qv[0], jnp.zeros_like(b_qv[0]), b_qv[1]])[:, None, :]
     packed = (
-        jnp.einsum("nd,kde->kne", tok_full, qkv16, preferred_element_type=jnp.float32) + bias_rows
-    ).astype(jnp.bfloat16)
-    context, logsum = attend_forward(packed, segment_ids)
-    attn_terms = jnp.dot(context, out16, preferred_element_type=jnp.float32)
-    attended = lax.psum_scatter(attn_terms, "tensor", scatter_dimension=0, tiled=True)
-    first_sum = tokens.astype(jnp.float32) + attended + w_vec[0]
+        jnp.einsum("nd,kde->kne", tok_full, qkv16, preferred_element_type=f32) + bias_rows
+    ).astype(bf16)
+    context, logsum = attend_forward(packed, segments)
+
+    def summed(left, right, form):
+        away = jnp.einsum(form, left[rows:], right, preferred_element_type=f32)
+        other = core_exchange(away.astype(bf16))
+        return jnp.einsum(form, left[:rows], right, preferred_element_type=f32) + other.astype(f32)
+
+    attended = summed(context, out_t, "ne,de->nd")
+    first_sum = tokens.astype(f32) + attended + w_vec[0]
     hidden, first_pull = jax.vjp(layer_norm, first_sum, w_vec[2], w_vec[3])
-    hidden_full = lax.all_gather(hidden.astype(jnp.bfloat16), "tensor", axis=0, tiled=True)
-    upper = jnp.dot(hidden_full, up16, preferred_element_type=jnp.float32) + w_bup
+    hidden16 = hidden.astype(bf16)
+    hidden_full = jnp.concatenate([hidden16, core_exchange(hidden16)])
+    upper = jnp.dot(hidden_full, up16, preferred_element_type=f32) + b_up
     active, gelu_pull = jax.vjp(gelu_exact, upper)
-    active16 = active.astype(jnp.bfloat16)
-    mixed_terms = jnp.dot(active16, down16, preferred_element_type=jnp.float32)
-    mixed = lax.psum_scatter(mixed_terms, "tensor", scatter_dimension=0, tiled=True)
+    active16 = active.astype(bf16)
+    mixed = summed(active16, down_t, "nf,df->nd")
     second_sum = hidden + mixed + w_vec[1]
     normed, second_pull = jax.vjp(layer_norm, second_sum, w_vec[4], w_vec[5])
-    layer_out = normed.astype(jnp.bfloat16)
-    qkv16, out16, up16, down16 = (
-        lax.all_gather(shards16[0], "dp", axis=1, tiled=True),
-        lax.all_gather(shards16[1], "dp", axis=1, tiled=True),
-        lax.all_gather(shards16[2], "dp", axis=0, tiled=True),
-        lax.all_gather(shards16[3], "dp", axis=1, tiled=True),
-    )
-    second_grad, gain2_grad, shift2_grad = second_pull(cotangent.astype(jnp.float32))
-    mixed_full = lax.all_gather(second_grad.astype(jnp.bfloat16), "tensor", axis=0, tiled=True)
-    active_grad = jnp.einsum("nd,fd->nf", mixed_full, down16, preferred_element_type=jnp.float32)
-    down_grad = jnp.einsum("nf,nd->fd", active16, mixed_full, preferred_element_type=jnp.float32)
+    layer_out = swap(normed.astype(bf16))
+    second_grad, gain2_grad, shift2_grad = second_pull(cotangent.astype(f32))
+    second16 = second_grad.astype(bf16)
+    mixed_full = jnp.concatenate([second16, core_exchange(second16)])
+    active_grad = jnp.einsum("nd,df->nf", mixed_full, down_t, preferred_element_type=f32)
+    down_grad = jnp.einsum("nd,nf->df", mixed_full, active16, preferred_element_type=f32).astype(bf16)
     upper_grad = gelu_pull(active_grad)[0]
-    upper16 = upper_grad.astype(jnp.bfloat16)
-    hidden_terms = jnp.einsum("nf,df->nd", upper16, up16, preferred_element_type=jnp.float32)
-    up_grad = jnp.einsum("nd,nf->df", hidden_full, upper16, preferred_element_type=jnp.float32)
-    hidden_grad = second_grad + lax.psum_scatter(
-        hidden_terms, "tensor", scatter_dimension=0, tiled=True
-    )
+    upper16 = upper_grad.astype(bf16)
+    up_grad = jnp.einsum("nd,nf->df", hidden_full, upper16, preferred_element_type=f32).astype(bf16)
+    hidden_grad = second_grad + summed(upper16, up16, "nf,df->nd")
     first_grad, gain1_grad, shift1_grad = first_pull(hidden_grad)
-    attended_full = lax.all_gather(first_grad.astype(jnp.bfloat16), "tensor", axis=0, tiled=True)
-    context_grad = jnp.einsum(
-        "nd,ed->ne", attended_full, out16, preferred_element_type=jnp.float32
-    ).astype(jnp.bfloat16)
-    out_grad = jnp.einsum("ne,nd->ed", context, attended_full, preferred_element_type=jnp.float32)
-    packed_grad = attend_backward(packed, context_grad, logsum, segment_ids)
+    first16 = first_grad.astype(bf16)
+    attended_full = jnp.concatenate([first16, core_exchange(first16)])
+    context_grad = jnp.einsum("nd,de->ne", attended_full, out_t, preferred_element_type=f32).astype(bf16)
+    out_grad = jnp.einsum("nd,ne->de", attended_full, context, preferred_element_type=f32).astype(bf16)
+    packed_grad = attend_backward(packed, context_grad, logsum, segments)
     bqv_local = jnp.stack([jnp.sum(packed_grad[0], axis=0), jnp.sum(packed_grad[2], axis=0)])
-    packed16 = packed_grad.astype(jnp.bfloat16)
-    token_terms = jnp.einsum("kne,kde->nd", packed16, qkv16, preferred_element_type=jnp.float32)
-    qkv_grad = jnp.einsum("nd,kne->kde", tok_full, packed16, preferred_element_type=jnp.float32)
-    grad_tokens = (
-        first_grad
-        + lax.psum_scatter(
-            token_terms.astype(jnp.bfloat16), "tensor", scatter_dimension=0, tiled=True
-        ).astype(jnp.float32)
-    ).astype(jnp.bfloat16)
-    qkv_part, out_part, up_part, down_part = (
-        lax.psum_scatter(qkv_grad, "dp", scatter_dimension=1, tiled=True),
-        lax.psum_scatter(out_grad, "dp", scatter_dimension=1, tiled=True),
-        lax.psum_scatter(up_grad, "dp", scatter_dimension=0, tiled=True),
-        lax.psum_scatter(down_grad, "dp", scatter_dimension=1, tiled=True),
-    )
-    tensor_index = lax.axis_index("tensor")
-    tensor_count = lax.axis_size("tensor")
-    dev_width = w_bqv.shape[1]
-    unit_width = w_bup.shape[0]
-    bqv_full = lax.dynamic_update_slice(
-        jnp.zeros((2, dev_width * tensor_count), jnp.float32),
-        bqv_local,
-        (0, tensor_index * dev_width),
-    )
-    bup_full = lax.dynamic_update_slice(
-        jnp.zeros((unit_width * tensor_count,), jnp.float32),
-        jnp.sum(upper_grad, axis=0),
-        (tensor_index * unit_width,),
-    )
+    packed16 = packed_grad.astype(bf16)
+    qkv_grad = jnp.einsum("nd,kne->kde", tok_full, packed16, preferred_element_type=f32).astype(bf16)
+    away = jnp.einsum("kne,kde->nd", packed16[:, rows:], qkv16, preferred_element_type=f32)
+    other = core_exchange(away.astype(bf16))
+    near = jnp.einsum("kne,kde->nd", packed16[:, :rows], qkv16, preferred_element_type=f32)
+    grad_tokens = swap((first_grad + near + other.astype(f32)).astype(bf16))
+
+    down_l, down_r = reduce_pair(down_grad[:, : unit_width // 2], down_grad[:, unit_width // 2 :])
+    uo_l, uo_r = reduce_pair(
+        *(
+            jnp.concatenate([out_grad[:, h * half : (h + 1) * half], up_grad[:, h * unit_width // 2 : (h + 1) * unit_width // 2]], 1)
+            for h in range(2)
+        )
+    )
+    qkv_l, qkv_r = reduce_pair(
+        *(jnp.concatenate([qkv_grad[k, :, h * half : (h + 1) * half] for k in range(3)], 1) for h in range(2))
+    )
+    qkv_part = jnp.stack(
+        [jnp.concatenate([part[:, k * half : (k + 1) * half] for part in (qkv_l, qkv_r)], 1) for k in range(3)]
+    )
+    out_part = jnp.concatenate([uo_l[:, :half], uo_r[:, :half]], 1).T
+    up_part = jnp.concatenate([uo_l[:, half:], uo_r[:, half:]], 1)
+    down_part = jnp.concatenate([down_l, down_r], 1).T
+
     vec_local = jnp.stack(
         [
             jnp.sum(first_grad, axis=0),
@@ -264,10 +375,12 @@
             shift2_grad,
         ]
     )
-    bqv_sum, bup_sum, vec_grad = lax.psum((bqv_full, bup_full, vec_local), ("dp", "tensor"))
-    bqv_grad = lax.dynamic_slice_in_dim(bqv_sum, tensor_index * dev_width, dev_width, 1)
-    bup_grad = lax.dynamic_slice_in_dim(bup_sum, tensor_index * unit_width, unit_width, 0)
-    base_rate = 1.0 / math.sqrt(SEQ_GRP * SEQ_LEN * lax.axis_size("dp"))
+    vec_local = vec_local + core_exchange(vec_local)
+    early = sum_all(jnp.concatenate([vec_local.reshape(-1), jnp.sum(upper_grad, axis=0)]))
+    vec_grad = early[: vec_local.size].reshape(vec_local.shape)
+    bup_grad = swap(early[vec_local.size :])
+    bqv_grad = swap(sum_all(bqv_local))
+    base_rate = 1.0 / math.sqrt(SEQ_LEN * lax.axis_size(("chip", "core")))
     slow_rate = MATRIX_RATE * base_rate
     fast_rate = FASTER_RATE * base_rate
     nm_qkv, nw_qkv, na_qkv = advance(w_qkv, m_qkv, a_qkv, qkv_part, slow_rate)
@@ -305,55 +418,15 @@
 
 
 def solution(mesh):
-    in_specs = (
-        P(("dp", "tensor"), None),
-        P(("dp", "tensor"), None),
-        P("dp", None),
-        P(None, "dp", "tensor"),
-        P(None, "dp", "tensor"),
-        P(None, "dp", "tensor"),
-        P(None, "tensor"),
-        P(None, "tensor"),
-        P(None, "tensor"),
-        P("tensor", "dp"),
-        P("tensor", "dp"),
-        P("tensor", "dp"),
-        P("dp", "tensor"),
-        P("dp", "tensor"),
-        P("dp", "tensor"),
-        P("tensor"),
-        P("tensor"),
-        P("tensor"),
-        P("tensor", "dp"),
-        P("tensor", "dp"),
-        P("tensor", "dp"),
-        P(),
-        P(),
-        P(),
-    )
-    out_specs = (
-        P(("dp", "tensor"), None),
-        P(("dp", "tensor"), None),
-        P(None, "dp", "tensor"),
-        P(None, "dp", "tensor"),
-        P(None, "dp", "tensor"),
-        P(None, "tensor"),
-        P(None, "tensor"),
-        P(None, "tensor"),
-        P("tensor", "dp"),
-        P("tensor", "dp"),
-        P("tensor", "dp"),
-        P("dp", "tensor"),
-        P("dp", "tensor"),
-        P("dp", "tensor"),
-        P("tensor"),
-        P("tensor"),
-        P("tensor"),
-        P("tensor", "dp"),
-        P("tensor", "dp"),
-        P("tensor", "dp"),
-        P(),
-        P(),
-        P(),
-    )
-    return jax.shard_map(body, mesh=mesh, in_specs=in_specs, out_specs=out_specs, check_vma=False)
+    devices = mesh.devices.reshape(-1, 2, 2)
+    split_mesh = Mesh(devices, ("chip", "core", "tensor"))
+    dp = ("chip", "core")
+    row = P(("chip", "core", "tensor"), None)
+    deep = P(None, dp, "tensor")
+    wide = P("tensor", dp)
+    tall = P(dp, "tensor")
+    qv = P(None, "tensor")
+    unit = P("tensor")
+    in_specs = (row, row, P(dp, None)) + (deep,) * 3 + (qv,) * 3 + (wide,) * 3 + (tall,) * 3 + (unit,) * 3 + (wide,) * 3 + (P(),) * 3
+    out_specs = (row, row) + in_specs[3:]
+    return jax.shard_map(body, mesh=split_mesh, in_specs=in_specs, out_specs=out_specs, check_vma=False)

time: 1060 us -> 698 us (0.66)
  waiting for transfers between devices: 673 us -> 206 us
  starting transfers between devices: 1.45 us -> 109 us
  blocking collectives: 41.8 us -> 0 us
  local copies, waits for them, and re-layouts: 39.2 us -> 73.9 us
  other arithmetic: 79.7 us -> 94.1 us
  between operations: 15.4 us -> 3.4 us
    reduce_scatter x7 -> x0, waiting for transfers between devices: 267 us -> none  [the longest x1 62.3 us: body(): lax.psum_scatter(out_grad, 'dp', scatter_dimension=1, tiled=True)]
    all_gather x8 -> x0, waiting for transfers between devices: 234 us -> none  [the longest x1 48.9 us: body(): lax.all_gather(shards16[0], 'dp', axis=1, tiled=True)]
    ppermute x0 -> x67, waiting for transfers between devices: none -> 206 us  [the longest x30 142 us: chip_exchange(): return lax.ppermute(values, 'chip', [(k, k ^ mask) for k in range(count)])]
    unnamed x17 -> x0, waiting for transfers between devices: 172 us -> none
    ppermute x0 -> x67, starting transfers between devices: none -> 109 us  [the longest x14 59.9 us: swap(): return lax.ppermute(values, ('core', 'tensor'), SWAP)]
    psum x1 -> x0, blocking collectives: 41.8 us -> none  [body(): lax.psum((bqv_full, bup_full, vec_local), ('dp', 'tensor'))]
    dot_general x12 -> x16, matrix products: 113 us -> 90.5 us  [the longest x1 25.9 us: body(): upper = jnp.dot(hidden_full, up16, preferred_element_type=f32) + b_up]
    select_n x0 -> x28, other arithmetic: none -> 21.8 us  [the longest x27 21.8 us: join(): jnp.where(first, jnp.stack([mine, other], axis), jnp.stack([other, mine],...]
  transfers between devices with their start and end apart: 16 -> 67, of which waited for: 14 -> 30; matrix products, arithmetic and copies ran while one was open for 24% -> 45% of each run, Pallas kernels for 0% -> 0%
where the time goes in v1:
time: 698 us; the launch traced here: 687 us
  waiting for transfers between devices  206 us (30%)
  matrix products  193 us (28%)
  starting transfers between devices  109 us (16%)
  other arithmetic  94.1 us (13%)
  local copies, waits for them, and re-layouts  73.9 us (11%)
  loops' own time  7.05 us (1%)
    ppermute x30, waiting for transfers between devices, chip_exchange(): return lax.ppermute(values, 'chip', [(k, k ^ mask) for k in range(count)])  142 us
    ppermute x14, starting transfers between devices, swap(): return lax.ppermute(values, ('core', 'tensor'), SWAP)  59.9 us
    dot_general x4, matrix products, one_block(): jnp.einsum('qhd,khd->hqk', query_rows, key_all, preferred_element_type=jn...  38.1 us
    ppermute x14, waiting for transfers between devices, y_exchange(): return lax.ppermute(values, 'tensor', FLIP)  32.8 us
    ppermute x14, waiting for transfers between devices, swap(): return lax.ppermute(values, ('core', 'tensor'), SWAP)  31.1 us
    dot_general x1, matrix products, body(): upper = jnp.dot(hidden_full, up16, preferred_element_type=f32) + b_up  25.9 us
    ppermute x30, starting transfers between devices, chip_exchange(): return lax.ppermute(values, 'chip', [(k, k ^ mask) for k in range(count)])  23.9 us
    unnamed x204, local copies, waits for them, and re-layouts  23.3 us
  transfers between devices with their start and end apart: 67, of which 30 were waited for; matrix products, arithmetic and copies ran while one was open for 45% of the time, Pallas kernels for 0%

profile of v1, /device:TPU:1, one launch (start us, length us, event | category | flops | bytes accessed | tf_op | source)
XLA Modules:
  0.0 686.9 jit_solution(1060040446680101107)
XLA Ops:
  32.8 8.0 %collective-permute-done.3 = bf16[2,64,768]{2,1,0:T(8,128)(2,1)S(1)} collective-permute-done((bf16[2,64,768]{2,1,0:T(8,128)(2,1)S(1)}, bf16[2,64,768]{2,1,0:T(8,128)(2,1)S(1)}, u32[]{:S(2)}, u32[]{:S(2)}) %collective-permute-start.3) | collective-permute-done | bytes 196640 | tf_op jit(solution)/shard_map/ppermute | solution.py:163
  50.7 30.0 %collective-permute-done.4 = bf16[2,2,64,768]{3,2,1,0:T(8,128)(2,1)S(1)} collective-permute-done((bf16[2,2,64,768]{3,2,1,0:T(8,128)(2,1)S(1)}, bf16[2,2,64,768]{3,2,1,0:T(8,128)(2,1)S(1)}, u32[]{:S(2)}, u32[]{:S(2)}) %collective-permute-start.4) | collective-permute-done | bytes 393248 | tf_op jit(solution)/shard_map/ppermute | solution.py:163
  98.9 11.2 %collective-permute-done.6 = bf16[2,2,2,64,768]{4,3,2,1,0:T(8,128)(2,1)S(1)} collective-permute-done((bf16[2,2,2,64,768]{4,3,2,1,0:T(8,128)(2,1)S(1)}, bf16[2,2,2,64,768]{4,3,2,1,0:T(8,128)(2,1)S(1)}, u32[]{:S(2)}, u32[]{:S(2)}) %collective-permute-start.6) | collective-permute-done | bytes 786464 | tf_op jit(solution)/shard_map/ppermute | solution.py:158
  145.1 30.2 %while.47 = (s32[]{:T(128)}, bf16[2,512,512]{1,2,0:T(8,128)(2,1)}, f32[2,8,512]{2,1,0:T(8,128)S(1)}, s32[2]{0:T(128)S(1)}, s32[1024]{0:T(1024)S(1)}, /*index=5*/...) while((s32[]{:T(128)}, bf16[2,512,512]{1,2,0:T(8,128)(2,1)}, ...), condition=%wide.region_3.4_spmd, body=%wide.region_0.3_spmd.sunk | while | flops 1124855808 | bytes 56765116 | solution.py:71
  187.5 11.6 %collective-permute-done.23 = bf16[2,2,64,1024]{3,2,1,0:T(8,128)(2,1)S(1)} collective-permute-done((bf16[2,2,64,1024]{3,2,1,0:T(8,128)(2,1)S(1)}, bf16[2,2,64,1024]{3,2,1,0:T(8,128)(2,1)S(1)}, u32[]{:S(2)}, u32[]{:S(2)}) %collective-permute-start.23) | collective-permute-done | bytes 524320 | tf_op jit(solution)/shard_map/ppermute | solution.py:163
  206.5 18.4 %collective-permute-done.26 = bf16[2,2,2,64,1024]{4,3,1,0,2:T(8,128)(2,1)S(1)} collective-permute-done((bf16[2,2,2,64,1024]{4,3,1,0,2:T(8,128)(2,1)S(1)}, bf16[2,2,2,64,1024]{4,3,1,0,2:T(8,128)(2,1)S(1)}, u32[]{:S(2)}, u32[]{:S(2)}) %collective-permute-start.26) | collective-permute-done | bytes 1048608 | tf_op jit(solution)/shard_map/ppermute | solution.py:163
  227.6 25.9 %multiply_convert_fusion.1 = (bf16[1024,2048]{1,0:T(8,128)(2,1)S(1)}, f32[1024,2048]{1,0:T(8,128)}, f32[1024,2048]{1,0:T(8,128)}) fusion(f32[2048]{0:T(1024)S(1)} %slice.398, bf16[1024,1024]{1,0:T(8,128)(2,1)S(1)} %slice.397, bf16[1024,1024]{1,0:T(8,128)(2,1)S(1)} %slice.396, bf16[512,1024]{1,0:T(8,128)(2,1)S(1)} %collective-permute-done.19, ...), kind=kOutput, calls=%fused_computation.39 | convolution fusion | flops 4445962240 | bytes 27271168 | tf_op jit(solution)/shard_map/dot_general | solution.py:321
  263.5 10.7 %collective-permute-done.29 = bf16[512,1024]{1,0:T(8,128)(2,1)S(1)} collective-permute-done((bf16[512,1024]{1,0:T(8,128)(2,1)S(1)}, bf16[512,1024]{1,0:T(8,128)(2,1)S(1)}, u32[]{:S(2)}, u32[]{:S(2)}) %collective-permute-start.29) | collective-permute-done | bytes 1048608 | tf_op jit(solution)/shard_map/ppermute | solution.py:150
  293.9 13.3 %fusion.131 = (f32[2048]{0:T(1024)S(1)}, bf16[1024,2048]{1,0:T(8,128)(2,1)}) fusion(f32[1024,2048]{1,0:T(8,128)} %get-tuple-element.287, bf16[1024,1024]{1,0:T(8,128)(2,1)S(1)} %bitcast.426, bf16[1024,1024]{1,0:T(8,128)(2,1)S(1)} %bitcast.429, bf16[512,1024]{1,0:T(8,128)(2,1)} %collective-permute-done.30, bf16[512,1024]{1,0:T(8,128)(2,1)S(1)} %get-tuple-element.313, ...), kind=kOutput, calls=%fused_computation.366 | convolution fusion | flops 4341102592 | bytes 27279360 | tf_op jit(solution)/shard_map/nd,df->nf/dot_general | solution.py:331
  311.2 8.0 %collective-permute-start.31 = (bf16[512,1024]{1,0:T(8,128)(2,1)S(1)}, bf16[512,1024]{1,0:T(8,128)(2,1)S(1)}, u32[]{:S(2)}, u32[]{:S(2)}) collective-permute-start(bf16[512,1024]{1,0:T(8,128)(2,1)S(1)} %fusion.61), channel_id=1, source_target_pairs={{0,2},{2,0},{1,3},{3,1},{4,6},{6,4},{5,7},{7,5},{8,10},{10,8},{9,1... | collective-permute-start | bytes 3145736 | tf_op jit(solution)/shard_map/ppermute | solution.py:154
  385.6 116.4 %while.48 = (s32[]{:T(128)}, f32[1024,8,64]{0,2,1:T(8,128)}, f32[1024,8,64]{0,2,1:T(8,128)}, f32[2,512,8,64]{1,3,2,0:T(8,128)}, s32[2]{0:T(128)S(1)}, /*index=5*...) while((s32[]{:T(128)}, f32[1024,8,64]{0,2,1:T(8,128)}, ...), condition=%wide.region_14.15_spmd.clone, body=%wide.region_12.14_spmd.clone.sunk | while | flops 2725507072 | bytes 271674336 | solution.py:128
  387.2 8.2 %fusion.191 = f32[8,512,1024]{2,1,0:T(8,128)} fusion(bf16[1024,8,64]{0,2,1:T(8,128)(2,1)S(1)} %get-tuple-element.611, bf16[1024,8,64]{0,2,1:T(8,128)(2,1)S(1)} %get-tuple-element.610, s32[]{:T(128)S(6)} %select_n.496), kind=kOutput, calls=%fused_computation.27.clone.1 | convolution fusion | flops 536870912 | bytes 18350084 | tf_op jit(solution)/shard_map/while/body/eval_jaxpr/while/body/eval_jaxpr/qhd,khd->hqk/dot_general | solution.py:109
  399.9 16.0 %multiply_reduce_fusion.6 = (f32[8,512]{1,0:T(8,128)}, f32[8,512,1024]{2,1,0:T(8,128)}) fusion(f32[8,512,1024]{2,1,0:T(8,128)} %fusion.191, f32[8,512]{1,0:T(8,128)} %dynamic-slice_bitcast_fusion.12, bf16[1024,8,64]{0,2,1:T(8,128)(2,1)S(1)} %get-tuple-element.608, bf16[1024,8,64]{0,2,1:T(8,128)(2,1)} %get-tuple-element.606, s32[]{:T(128)S(6)} %select_n.496, ...), kind=kOutput, calls=%fused_computation.16.clone.1 | convolution fusion | flops 557838336 | bytes 35684356 | tf_op jit(solution)/shard_map/while/body/eval_jaxpr/while/body/eval_jaxpr/qhd,khd->hqk/dot_general | solution.py:98
  415.9 9.3 %multiply_convert_fusion.3 = bf16[8,512,1024]{2,1,0:T(8,128)(2,1)} fusion(f32[8,512,1024]{2,1,0:T(8,128)} %get-tuple-element.531, f32[8,512,1024]{2,1,0:T(8,128)S(1)} %bitcast.404, f32[8,512]{1,0:T(8,128)} %get-tuple-element.532), kind=kLoop, calls=%fused_computation.15.clone.1 | loop fusion | flops 12582912 | bytes 41959424 | tf_op jit(solution)/shard_map/while/body/eval_jaxpr/while/body/eval_jaxpr/convert_element_type | solution.py:113
  444.2 8.2 %fusion.191 = f32[8,512,1024]{2,1,0:T(8,128)} fusion(bf16[1024,8,64]{0,2,1:T(8,128)(2,1)S(1)} %get-tuple-element.611, bf16[1024,8,64]{0,2,1:T(8,128)(2,1)S(1)} %get-tuple-element.610, s32[]{:T(128)S(6)} %select_n.496), kind=kOutput, calls=%fused_computation.27.clone.1 | convolution fusion | flops 536870912 | bytes 18350084 | tf_op jit(solution)/shard_map/while/body/eval_jaxpr/while/body/eval_jaxpr/qhd,khd->hqk/dot_general | solution.py:109
  456.9 16.0 %multiply_reduce_fusion.6 = (f32[8,512]{1,0:T(8,128)}, f32[8,512,1024]{2,1,0:T(8,128)}) fusion(f32[8,512,1024]{2,1,0:T(8,128)} %fusion.191, f32[8,512]{1,0:T(8,128)} %dynamic-slice_bitcast_fusion.12, bf16[1024,8,64]{0,2,1:T(8,128)(2,1)S(1)} %get-tuple-element.608, bf16[1024,8,64]{0,2,1:T(8,128)(2,1)} %get-tuple-element.606, s32[]{:T(128)S(6)} %select_n.496, ...), kind=kOutput, calls=%fused_computation.16.clone.1 | convolution fusion | flops 557838336 | bytes 35684356 | tf_op jit(solution)/shard_map/while/body/eval_jaxpr/while/body/eval_jaxpr/qhd,khd->hqk/dot_general | solution.py:98
  472.9 9.3 %multiply_convert_fusion.3 = bf16[8,512,1024]{2,1,0:T(8,128)(2,1)} fusion(f32[8,512,1024]{2,1,0:T(8,128)} %get-tuple-element.531, f32[8,512,1024]{2,1,0:T(8,128)S(1)} %bitcast.404, f32[8,512]{1,0:T(8,128)} %get-tuple-element.532), kind=kLoop, calls=%fused_computation.15.clone.1 | loop fusion | flops 12582912 | bytes 41959424 | tf_op jit(solution)/shard_map/while/body/eval_jaxpr/while/body/eval_jaxpr/convert_element_type | solution.py:113
  537.7 10.1 %collective-permute-done.43 = f32[2,512]{1,0:T(2,128)S(1)} collective-permute-done((f32[2,512]{1,0:T(2,128)S(1)}, f32[2,512]{1,0:T(2,128)S(1)}, u32[]{:S(2)}, u32[]{:S(2)}) %collective-permute-start.43) | collective-permute-done | bytes 4128 | tf_op jit(solution)/shard_map/ppermute | solution.py:163
  555.3 8.3 %collective-permute-start.46 = (f32[2,512]{1,0:T(2,128)S(1)}, f32[2,512]{1,0:T(2,128)S(1)}, u32[]{:S(2)}, u32[]{:S(2)}) collective-permute-start(f32[2,512]{1,0:T(2,128)S(1)} %add.406), channel_id=1, source_target_pairs={{0,0},{1,2},{2,1},{3,3},{4,4},{5,6},{6,5},{7,7},{8,8},{9,10},{10,9... | collective-permute-start | bytes 12296 | tf_op jit(solution)/shard_map/ppermute | solution.py:150
  576.6 10.1 %collective-permute-done.35 = bf16[2,2,2,64,768]{4,3,2,1,0:T(8,128)(2,1)S(1)} collective-permute-done((bf16[2,2,2,64,768]{4,3,2,1,0:T(8,128)(2,1)S(1)}, bf16[2,2,2,64,768]{4,3,2,1,0:T(8,128)(2,1)S(1)}, u32[]{:S(2)}, u32[]{:S(2)}) %collective-permute-start.35) | collective-permute-done | bytes 786464 | tf_op jit(solution)/shard_map/ppermute | solution.py:158
  602.8 11.5 %collective-permute-done.39 = bf16[2,2,64,768]{3,2,1,0:T(8,128)(2,1)S(1)} collective-permute-done((bf16[2,2,64,768]{3,2,1,0:T(8,128)(2,1)S(1)}, bf16[2,2,64,768]{3,2,1,0:T(8,128)(2,1)S(1)}, u32[]{:S(2)}, u32[]{:S(2)}) %collective-permute-start.39) | collective-permute-done | bytes 393248 | tf_op jit(solution)/shard_map/ppermute | solution.py:163
  632.7 8.0 %collective-permute-start.34 = (bf16[512,1024]{1,0:T(8,128)(2,1)S(1)}, bf16[512,1024]{1,0:T(8,128)(2,1)S(1)}, u32[]{:S(2)}, u32[]{:S(2)}) collective-permute-start(bf16[512,1024]{1,0:T(8,128)(2,1)S(1)} %fusion.48), channel_id=1, source_target_pairs={{0,0},{1,2},{2,1},{3,3},{4,4},{5,6},{6,5},{7,7},{8,8},{9,10},{10,9... | collective-permute-start | bytes 3145736 | tf_op jit(solution)/shard_map/ppermute | solution.py:150
  640.8 19.1 %collective-permute-done.51 = bf16[2,2,64,1280]{3,2,0,1:T(8,128)(2,1)S(1)} collective-permute-done((bf16[2,2,64,1280]{3,2,0,1:T(8,128)(2,1)S(1)}, bf16[2,2,64,1280]{3,2,0,1:T(8,128)(2,1)S(1)}, u32[]{:S(2)}, u32[]{:S(2)}) %collective-permute-start.51) | collective-permute-done | bytes 655392 | tf_op jit(solution)/shard_map/ppermute | solution.py:163
  668.2 8.0 %collective-permute-start.53 = (bf16[2,64,1280]{2,1,0:T(8,128)(2,1)S(1)}, bf16[2,64,1280]{2,1,0:T(8,128)(2,1)S(1)}, u32[]{:S(2)}, u32[]{:S(2)}) collective-permute-start(bf16[2,64,1280]{2,1,0:T(8,128)(2,1)S(1)} %fusion.81), channel_id=1, source_target_pairs={{0,0},{1,2},{2,1},{3,3},{4,4},{5,6},{6,5},{7,7},{8,8},{9,10},{10,9... | collective-permute-start | bytes 983048 | tf_op jit(solution)/shard_map/ppermute | solution.py:150
  (597 shorter events, 397.0 us)
Async XLA Ops:
  6.5 74.9 %collective-permute-start = (bf16[512,1024]{1,0:T(8,128)(2,1)}, bf16[512,1024]{1,0:T(8,128)(2,1)}, u32[]{:S(2)}, u32[]{:S(2)}) collective-permute-start(bf16[512,1024]{1,0:T(8,128)(2,1)} %param.28), channel_id=1, source_target_pairs={{0,0},{1,2},{2,1},{3,3},{4,4},{5,6},{6,5},{7,7},{8,8},{9,10},{10,9... | collective-permute-start | bytes 3145736 | tf_op jit(solution)/shard_map/ppermute | solution.py:150
  40.8 39.9 %collective-permute-start.4 = (bf16[2,2,64,768]{3,2,1,0:T(8,128)(2,1)S(1)}, bf16[2,2,64,768]{3,2,1,0:T(8,128)(2,1)S(1)}, u32[]{:S(2)}, u32[]{:S(2)}) collective-permute-start(bf16[2,2,64,768]{3,2,1,0:T(8,128)(2,1)S(1)} %maximum_select_fusion.20), channel_id=1, source_target_pairs={{0,16},{4,20},{8,24},{12,28},{16,0},{20,4},{24,8},{28,12},{1,17},{... | collective-permute-start | bytes 1179656 | tf_op jit(solution)/shard_map/ppermute | solution.py:163
  45.2 44.0 %collective-permute-start.22 = (bf16[2,2,64,1024]{3,2,1,0:T(8,128)(2,1)S(1)}, bf16[2,2,64,1024]{3,2,1,0:T(8,128)(2,1)S(1)}, u32[]{:S(2)}, u32[]{:S(2)}) collective-permute-start(bf16[2,2,64,1024]{3,2,1,0:T(8,128)(2,1)S(1)} %maximum_select_fusion.19), channel_id=1, source_target_pairs={{0,16},{4,20},{8,24},{12,28},{16,0},{20,4},{24,8},{28,12},{1,17},{... | collective-permute-start | bytes 1572872 | tf_op jit(solution)/shard_map/ppermute | solution.py:163
  50.5 45.7 %collective-permute-start.13 = (bf16[2,2,64,1280]{3,2,1,0:T(8,128)(2,1)S(1)}, bf16[2,2,64,1280]{3,2,1,0:T(8,128)(2,1)S(1)}, u32[]{:S(2)}, u32[]{:S(2)}) collective-permute-start(bf16[2,2,64,1280]{3,2,1,0:T(8,128)(2,1)S(1)} %maximum_select_fusion.18), channel_id=1, source_target_pairs={{0,16},{4,20},{8,24},{12,28},{16,0},{20,4},{24,8},{28,12},{1,17},{... | collective-permute-start | bytes 1966088 | tf_op jit(solution)/shard_map/ppermute | solution.py:163
  81.5 58.3 %collective-permute-start.9 = (bf16[512,1024]{1,0:T(8,128)(2,1)}, bf16[512,1024]{1,0:T(8,128)(2,1)}, u32[]{:S(2)}, u32[]{:S(2)}) collective-permute-start(bf16[512,1024]{1,0:T(8,128)(2,1)} %collective-permute-done), channel_id=1, source_target_pairs={{0,2},{2,0},{1,3},{3,1},{4,6},{6,4},{5,7},{7,5},{8,10},{10,8},{9,1... | collective-permute-start | bytes 3145736 | tf_op jit(solution)/shard_map/ppermute | solution.py:154
  97.9 27.7 %collective-permute-start.14 = (bf16[2,2,64,1280]{3,2,1,0:T(8,128)(2,1)}, bf16[2,2,64,1280]{3,2,1,0:T(8,128)(2,1)}, u32[]{:S(2)}, u32[]{:S(2)}) collective-permute-start(bf16[2,2,64,1280]{3,2,1,0:T(8,128)(2,1)} %get-tuple-element.335), channel_id=1, source_target_pairs={{0,4},{4,0},{8,12},{12,8},{16,20},{20,16},{24,28},{28,24},{1,5},{5... | collective-permute-start | bytes 1966088 | tf_op jit(solution)/shard_map/ppermute | solution.py:163
  98.9 29.4 %collective-permute-start.16 = (bf16[2,2,64,1280]{3,2,1,0:T(8,128)(2,1)}, bf16[2,2,64,1280]{3,2,1,0:T(8,128)(2,1)}, u32[]{:S(2)}, u32[]{:S(2)}) collective-permute-start(bf16[2,2,64,1280]{3,2,1,0:T(8,128)(2,1)} %get-tuple-element.337), channel_id=1, source_target_pairs={{0,1},{1,0},{2,3},{3,2},{4,5},{5,4},{6,7},{7,6},{8,9},{9,8},{10,11... | collective-permute-start | bytes 1966088 | tf_op jit(solution)/shard_map/ppermute | solution.py:158
  128.3 47.0 %collective-permute-start.15 = (bf16[2,2,2,64,1280]{4,3,2,1,0:T(8,128)(2,1)}, bf16[2,2,2,64,1280]{4,3,2,1,0:T(8,128)(2,1)}, u32[]{:S(2)}, u32[]{:S(2)}) collective-permute-start(bf16[2,2,2,64,1280]{4,3,2,1,0:T(8,128)(2,1)} %maximum_select_fusion.7), channel_id=1, source_target_pairs={{0,1},{1,0},{2,3},{3,2},{4,5},{5,4},{6,7},{7,6},{8,9},{9,8},{10,11... | collective-permute-start | bytes 3932168 | tf_op jit(solution)/shard_map/ppermute | solution.py:158
  131.0 48.4 %collective-permute-start.17 = (bf16[2,2,2,64,1280]{4,3,1,0,2:T(8,128)(2,1)}, bf16[2,2,2,64,1280]{4,3,1,0,2:T(8,128)(2,1)}, u32[]{:S(2)}, u32[]{:S(2)}) collective-permute-start(bf16[2,2,2,64,1280]{4,3,1,0,2:T(8,128)(2,1)} %maximum_select_fusion.9), channel_id=1, source_target_pairs={{0,4},{4,0},{8,12},{12,8},{16,20},{20,16},{24,28},{28,24},{1,5},{5... | collective-permute-start | bytes 3932168 | tf_op jit(solution)/shard_map/ppermute | solution.py:163
  199.3 26.1 %collective-permute-start.24 = (bf16[2,2,2,64,1024]{4,3,2,1,0:T(8,128)(2,1)S(1)}, bf16[2,2,2,64,1024]{4,3,2,1,0:T(8,128)(2,1)S(1)}, u32[]{:S(2)}, u32[]{:S(2)}) collective-permute-start(bf16[2,2,2,64,1024]{4,3,2,1,0:T(8,128)(2,1)S(1)} %maximum_select_fusion.11), channel_id=1, source_target_pairs={{0,1},{1,0},{2,3},{3,2},{4,5},{5,4},{6,7},{7,6},{8,9},{9,8},{10,11... | collective-permute-start | bytes 3145736 | tf_op jit(solution)/shard_map/ppermute | solution.py:158
  201.2 23.6 %collective-permute-start.26 = (bf16[2,2,2,64,1024]{4,3,1,0,2:T(8,128)(2,1)S(1)}, bf16[2,2,2,64,1024]{4,3,1,0,2:T(8,128)(2,1)S(1)}, u32[]{:S(2)}, u32[]{:S(2)}) collective-permute-start(bf16[2,2,2,64,1024]{4,3,1,0,2:T(8,128)(2,1)S(1)} %maximum_select_fusion.13), channel_id=1, source_target_pairs={{0,4},{4,0},{8,12},{12,8},{16,20},{20,16},{24,28},{28,24},{1,5},{5... | collective-permute-start | bytes 3145736 | tf_op jit(solution)/shard_map/ppermute | solution.py:163
  281.0 58.8 %collective-permute-start.28 = (bf16[512,1024]{1,0:T(8,128)(2,1)}, bf16[512,1024]{1,0:T(8,128)(2,1)}, u32[]{:S(2)}, u32[]{:S(2)}) collective-permute-start(bf16[512,1024]{1,0:T(8,128)(2,1)} %get-tuple-element.311), channel_id=1, source_target_pairs={{0,0},{1,2},{2,1},{3,3},{4,4},{5,6},{6,5},{7,7},{8,8},{9,10},{10,9... | collective-permute-start | bytes 3145736 | tf_op jit(solution)/shard_map/ppermute | solution.py:150
  292.8 47.2 %collective-permute-start.62 = (bf16[2,2,2,64,1024]{4,3,1,0,2:T(8,128)(2,1)}, bf16[2,2,2,64,1024]{4,3,1,0,2:T(8,128)(2,1)}, u32[]{:S(2)}, u32[]{:S(2)}) collective-permute-start(bf16[2,2,2,64,1024]{4,3,1,0,2:T(8,128)(2,1)} %bitcast.370), channel_id=1, source_target_pairs={{0,4},{4,0},{8,12},{12,8},{16,20},{20,16},{24,28},{28,24},{1,5},{5... | collective-permute-start | bytes 3145736 | tf_op jit(solution)/shard_map/ppermute | solution.py:163
  320.5 28.5 %collective-permute-start.60 = (bf16[2,2,2,64,1024]{4,3,1,0,2:T(8,128)(2,1)}, bf16[2,2,2,64,1024]{4,3,1,0,2:T(8,128)(2,1)}, u32[]{:S(2)}, u32[]{:S(2)}) collective-permute-start(bf16[2,2,2,64,1024]{4,3,1,0,2:T(8,128)(2,1)} %bitcast.371), channel_id=1, source_target_pairs={{0,1},{1,0},{2,3},{3,2},{4,5},{5,4},{6,7},{7,6},{8,9},{9,8},{10,11... | collective-permute-start | bytes 3145736 | tf_op jit(solution)/shard_map/ppermute | solution.py:158
  367.8 165.3 %collective-permute-start.64 = (bf16[2,2,64,1024]{3,2,0,1:T(8,128)(2,1)}, bf16[2,2,64,1024]{3,2,0,1:T(8,128)(2,1)}, u32[]{:S(2)}, u32[]{:S(2)}) collective-permute-start(bf16[2,2,64,1024]{3,2,0,1:T(8,128)(2,1)} %fusion.85), channel_id=1, source_target_pairs={{0,16},{4,20},{8,24},{12,28},{16,0},{20,4},{24,8},{28,12},{1,17},{... | collective-permute-start | bytes 1572872 | tf_op jit(solution)/shard_map/ppermute | solution.py:163
  378.5 218.6 %collective-permute-start.49 = (bf16[2,2,2,64,1280]{4,3,1,0,2:T(8,128)(2,1)}, bf16[2,2,2,64,1280]{4,3,1,0,2:T(8,128)(2,1)}, u32[]{:S(2)}, u32[]{:S(2)}) collective-permute-start(bf16[2,2,2,64,1280]{4,3,1,0,2:T(8,128)(2,1)} %bitcast.368), channel_id=1, source_target_pairs={{0,4},{4,0},{8,12},{12,8},{16,20},{20,16},{24,28},{28,24},{1,5},{5... | collective-permute-start | bytes 3932168 | tf_op jit(solution)/shard_map/ppermute | solution.py:163
  382.1 219.1 %collective-permute-start.47 = (bf16[2,2,2,64,1280]{4,3,1,0,2:T(8,128)(2,1)}, bf16[2,2,2,64,1280]{4,3,1,0,2:T(8,128)(2,1)}, u32[]{:S(2)}, u32[]{:S(2)}) collective-permute-start(bf16[2,2,2,64,1280]{4,3,1,0,2:T(8,128)(2,1)} %bitcast.369), channel_id=1, source_target_pairs={{0,1},{1,0},{2,3},{3,2},{4,5},{5,4},{6,7},{7,6},{8,9},{9,8},{10,11... | collective-permute-start | bytes 3932168 | tf_op jit(solution)/shard_map/ppermute | solution.py:158
  506.2 29.3 %collective-permute-start.42 = (f32[2,512]{1,0:T(2,128)S(1)}, f32[2,512]{1,0:T(2,128)S(1)}, u32[]{:S(2)}, u32[]{:S(2)}) collective-permute-start(f32[2,512]{1,0:T(2,128)S(1)} %pad_maximum_fusion.50), channel_id=1, source_target_pairs={{0,1},{1,0},{2,3},{3,2},{4,5},{5,4},{6,7},{7,6},{8,9},{9,8},{10,11... | collective-permute-start | bytes 12296 | tf_op jit(solution)/shard_map/ppermute | solution.py:158
  531.9 43.2 %collective-permute-start.37 = (bf16[2,2,2,64,768]{4,3,1,0,2:T(8,128)(2,1)}, bf16[2,2,2,64,768]{4,3,1,0,2:T(8,128)(2,1)}, u32[]{:S(2)}, u32[]{:S(2)}) collective-permute-start(bf16[2,2,2,64,768]{4,3,1,0,2:T(8,128)(2,1)} %bitcast.372), channel_id=1, source_target_pairs={{0,4},{4,0},{8,12},{12,8},{16,20},{20,16},{24,28},{28,24},{1,5},{5... | collective-permute-start | bytes 2359304 | tf_op jit(solution)/shard_map/ppermute | solution.py:163
  537.2 26.4 %collective-permute-start.65 = (bf16[2,64,1024]{2,1,0:T(8,128)(2,1)}, bf16[2,64,1024]{2,1,0:T(8,128)(2,1)}, u32[]{:S(2)}, u32[]{:S(2)}) collective-permute-start(bf16[2,64,1024]{2,1,0:T(8,128)(2,1)} %dynamic-slice_bitcast_fusion.9), channel_id=1, source_target_pairs={{0,8},{4,12},{8,0},{12,4},{16,24},{20,28},{24,16},{28,20},{1,9},{5... | collective-permute-start | bytes 786440 | tf_op jit(solution)/shard_map/ppermute | solution.py:163
  575.1 55.6 %collective-permute-start.33 = (bf16[512,1024]{1,0:T(8,128)(2,1)S(1)}, bf16[512,1024]{1,0:T(8,128)(2,1)S(1)}, u32[]{:S(2)}, u32[]{:S(2)}) collective-permute-start(bf16[512,1024]{1,0:T(8,128)(2,1)S(1)} %copy-done.98), channel_id=1, source_target_pairs={{0,2},{2,0},{1,3},{3,1},{4,6},{6,4},{5,7},{7,5},{8,10},{10,8},{9,1... | collective-permute-start | bytes 3145736 | tf_op jit(solution)/shard_map/ppermute | solution.py:154
  598.9 28.0 %collective-permute-start.50 = (bf16[2,2,64,1280]{3,2,1,0:T(8,128)(2,1)S(1)}, bf16[2,2,64,1280]{3,2,1,0:T(8,128)(2,1)S(1)}, u32[]{:S(2)}, u32[]{:S(2)}) collective-permute-start(bf16[2,2,64,1280]{3,2,1,0:T(8,128)(2,1)S(1)} %dynamic-slice_bitcast_fusion.2), channel_id=1, source_target_pairs={{0,1},{1,0},{2,3},{3,2},{4,5},{5,4},{6,7},{7,6},{8,9},{9,8},{10,11... | collective-permute-start | bytes 1966088 | tf_op jit(solution)/shard_map/ppermute | solution.py:158
  629.2 30.8 %collective-permute-start.51 = (bf16[2,2,64,1280]{3,2,0,1:T(8,128)(2,1)S(1)}, bf16[2,2,64,1280]{3,2,0,1:T(8,128)(2,1)S(1)}, u32[]{:S(2)}, u32[]{:S(2)}) collective-permute-start(bf16[2,2,64,1280]{3,2,0,1:T(8,128)(2,1)S(1)} %fusion.78), channel_id=1, source_target_pairs={{0,16},{4,20},{8,24},{12,28},{16,0},{20,4},{24,8},{28,12},{1,17},{... | collective-permute-start | bytes 1966088 | tf_op jit(solution)/shard_map/ppermute | solution.py:163
  632.7 44.8 %collective-permute-start.34 = (bf16[512,1024]{1,0:T(8,128)(2,1)S(1)}, bf16[512,1024]{1,0:T(8,128)(2,1)S(1)}, u32[]{:S(2)}, u32[]{:S(2)}) collective-permute-start(bf16[512,1024]{1,0:T(8,128)(2,1)S(1)} %fusion.48), channel_id=1, source_target_pairs={{0,0},{1,2},{2,1},{3,3},{4,4},{5,6},{6,5},{7,7},{8,8},{9,10},{10,9... | collective-permute-start | bytes 3145736 | tf_op jit(solution)/shard_map/ppermute | solution.py:150
  (156 other events, 1624.0 us)

commit v2 on v1

--- a/solution.py
+++ b/solution.py
@@ -1,14 +1,15 @@
+import functools
 import math
 
 import jax
 import jax.numpy as jnp
 from jax import lax
+from jax.experimental import pallas as pl
+from jax.experimental.pallas import tpu as pltpu
 from jax.sharding import Mesh, PartitionSpec as P
 
 HEAD_DIM = 64
 SEQ_LEN = 1024
-SEQ_GRP = 1
-QBLOCK = 512
 
 
 NORM_EPS = 1e-05
@@ -35,112 +36,148 @@
     return (new_moment, new_weight, new_average)
 
 
-def attend_forward(packed, segment_ids):
-    seq_count, length = segment_ids.shape
-    blocks_per = length // QBLOCK
-    dev_width = packed.shape[2]
-    local_heads = dev_width // HEAD_DIM
-    score_scale = HEAD_DIM ** (-0.5)
-    shaped = packed.reshape(3, seq_count, length, local_heads, HEAD_DIM)
-
-    def one_sequence(inputs):
-        query_all, key_all, value_all, seg_all = inputs
-
-        def one_block(block_index):
-            start = block_index * QBLOCK
-            query_rows = lax.dynamic_slice_in_dim(query_all, start, QBLOCK, 0)
-            row_seg = lax.dynamic_slice_in_dim(seg_all, start, QBLOCK, 0)
-            scores = (
-                jnp.einsum("qhd,khd->hqk", query_rows, key_all, preferred_element_type=jnp.float32)
-                * score_scale
-            )
-            same_doc = (row_seg[:, None] == seg_all[None, :])[None]
-            scores = jnp.where(same_doc, scores, -1e30)
-            row_max = jnp.max(scores, axis=-1, keepdims=True)
-            exp_scores = jnp.exp(scores - row_max)
-            row_total = jnp.sum(exp_scores, axis=-1, keepdims=True)
-            probs16 = (exp_scores / row_total).astype(jnp.bfloat16)
-            context = jnp.einsum(
-                "hqk,khd->qhd", probs16, value_all, preferred_element_type=jnp.float32
-            )
-            return (
-                context.astype(jnp.bfloat16).reshape(QBLOCK, dev_width),
-                (row_max + jnp.log(row_total))[..., 0],
-            )
-
-        context, logsum = lax.map(one_block, jnp.arange(blocks_per, dtype=jnp.int32))
-        return (context.reshape(length, dev_width), logsum)
-
-    context, logsum = lax.map(one_sequence, (shaped[0], shaped[1], shaped[2], segment_ids))
-    return (context.reshape(seq_count * length, dev_width), logsum)
-
-
-def attend_backward(packed, context_grad, logsum, segment_ids):
-    seq_count, length = segment_ids.shape
-    blocks_per = length // QBLOCK
-    dev_width = packed.shape[2]
-    local_heads = dev_width // HEAD_DIM
-    score_scale = HEAD_DIM ** (-0.5)
-    shaped = packed.reshape(3, seq_count, length, local_heads, HEAD_DIM)
-    grad_shaped = context_grad.reshape(seq_count, length, local_heads, HEAD_DIM)
-
-    def one_sequence(inputs):
-        query_all, key_all, value_all, grad_all, lse_all, seg_all = inputs
-
-        def one_block(carry, block_index):
-            key_grad, value_grad = carry
-            start = block_index * QBLOCK
-            query_rows = lax.dynamic_slice_in_dim(query_all, start, QBLOCK, 0)
-            grad_rows = lax.dynamic_slice_in_dim(grad_all, start, QBLOCK, 0)
-            row_seg = lax.dynamic_slice_in_dim(seg_all, start, QBLOCK, 0)
-            row_lse = lax.dynamic_index_in_dim(lse_all, block_index, 0, keepdims=False)
-            scores = (
-                jnp.einsum("qhd,khd->hqk", query_rows, key_all, preferred_element_type=jnp.float32)
-                * score_scale
-            )
-            same_doc = (row_seg[:, None] == seg_all[None, :])[None]
-            probs = jnp.where(same_doc, jnp.exp(scores - row_lse[..., None]), 0.0)
-            value_grad = value_grad + jnp.einsum(
-                "hqk,qhd->khd",
-                probs.astype(jnp.bfloat16),
-                grad_rows,
-                preferred_element_type=jnp.float32,
-            )
-            prob_grad = jnp.einsum(
-                "qhd,khd->hqk", grad_rows, value_all, preferred_element_type=jnp.float32
-            )
-            inner_sum = jnp.sum(probs * prob_grad, axis=-1, keepdims=True)
-            score_grad = (probs * (prob_grad - inner_sum)).astype(jnp.bfloat16)
-            query_grad = (
-                jnp.einsum("hqk,khd->qhd", score_grad, key_all, preferred_element_type=jnp.float32)
-                * score_scale
-            )
-            key_grad = (
-                key_grad
-                + jnp.einsum(
-                    "hqk,qhd->khd", score_grad, query_rows, preferred_element_type=jnp.float32
-                )
-                * score_scale
-            )
-            return ((key_grad, value_grad), query_grad)
-
-        zero_grad = jnp.zeros(key_all.shape, jnp.float32)
-        (key_grad, value_grad), query_grad = lax.scan(
-            one_block, (zero_grad, zero_grad), jnp.arange(blocks_per, dtype=jnp.int32)
-        )
-        return (query_grad.reshape(key_all.shape), key_grad, value_grad)
-
-    query_grad, key_grad, value_grad = lax.map(
-        one_sequence, (shaped[0], shaped[1], shaped[2], grad_shaped, logsum, segment_ids)
-    )
-    total_rows = seq_count * length
-    return jnp.stack(
-        [
-            query_grad.reshape(total_rows, dev_width),
-            key_grad.reshape(total_rows, dev_width),
-            value_grad.reshape(total_rows, dev_width),
-        ]
-    )
+NT = (((1,), (1,)), ((), ()))
+TN = (((0,), (0,)), ((), ()))
+FAR = -1e30
+
+
+def dot32(left, right, dims=(((1,), (0,)), ((), ()))):
+    return lax.dot_general(left, right, dims, preferred_element_type=jnp.float32)
+
+
+def three_terms(values):
+    high = values.astype(jnp.bfloat16).astype(jnp.float32)
+    rest = values - high
+    middle = rest.astype(jnp.bfloat16).astype(jnp.float32)
+    return (high, middle, rest - middle)
+
+
+def place(lane, terms, other):
+    high, middle, low = terms
+    return jnp.where(lane == 63, high, jnp.where(lane == 62, middle, jnp.where(lane == 61, low, other)))
+
+
+def forward_kernel(q_ref, k_ref, v_ref, seg_ref, out_ref, lse_ref, *, block):
+    f32, bf16 = jnp.float32, jnp.bfloat16
+    rows = q_ref.shape[0]
+    lanes = lax.broadcasted_iota(jnp.int32, (rows, 128), 1)
+    lower = lanes < HEAD_DIM
+    lane = lanes & 63
+    same = lane == seg_ref[...]
+    q_mark = jnp.where(same, 1.0, 0.0)
+    k_mark = jnp.where(same, 0.0, FAR)
+    query = q_ref[...].astype(f32)
+    keys = k_ref[...].astype(f32) * 0.125
+    value = v_ref[...].astype(f32)
+    q_heads = [jnp.where(lower, query, q_mark).astype(bf16), jnp.where(lower, q_mark, query).astype(bf16)]
+    k_heads = [jnp.where(lower, keys, k_mark).astype(bf16), jnp.where(lower, k_mark, keys).astype(bf16)]
+    v_heads = [jnp.where(lower, value, 1.0).astype(bf16), jnp.where(lower, 1.0, value).astype(bf16)]
+    low = lower[:block]
+    for start in range(0, rows, block):
+        parts = []
+        for head in range(2):
+            scores = dot32(q_heads[head][start : start + block], k_heads[head], NT)
+            top = jnp.max(scores, axis=1, keepdims=True)
+            weights = jnp.exp(scores - top).astype(bf16)
+            parts.append((dot32(weights, v_heads[head]), top))
+        (first, top0), (second, top1) = parts
+        total = pltpu.roll(jnp.where(low, second, first), HEAD_DIM, 1)
+        out_ref[start : start + block, :] = (jnp.where(low, first, second) / total).astype(bf16)
+        lse_ref[start : start + block, :] = jnp.where(low, top0, top1) + jnp.log(total)
+
+
+def backward_kernel(q_ref, k_ref, v_ref, g_ref, o_ref, lse_ref, seg_ref, d_ref, sum_ref, *, block):
+    f32, bf16 = jnp.float32, jnp.bfloat16
+    rows = q_ref.shape[0]
+    lanes = lax.broadcasted_iota(jnp.int32, (rows, 128), 1)
+    lower = lanes < HEAD_DIM
+    lane = lanes & 63
+    same = lane == seg_ref[...]
+    query = q_ref[...].astype(f32)
+    keys = k_ref[...].astype(f32) * 0.125
+    value = v_ref[...].astype(f32)
+    grad = g_ref[...].astype(f32)
+    lse = pltpu.roll(lse_ref[...], HEAD_DIM, 1)
+    q_mark = place(lane, three_terms(-lse), jnp.where(same, 1.0, 0.0))
+    k_mark = jnp.where(lane > 60, 1.0, jnp.where(same, 0.0, FAR))
+    inner = grad * o_ref[...].astype(f32)
+    inner0 = jnp.sum(jnp.where(lower, inner, 0.0), axis=1, keepdims=True)
+    inner1 = jnp.sum(jnp.where(lower, 0.0, inner), axis=1, keepdims=True)
+    g_mark = place(lane, three_terms(-jnp.where(lower, inner1, inner0)), 0.0)
+    v_mark = jnp.where(lane > 60, 1.0, 0.0)
+
+    def heads(values, mark):
+        return [jnp.where(lower, values, mark).astype(bf16), jnp.where(lower, mark, values).astype(bf16)]
+
+    q_heads, k_heads = heads(query, q_mark), heads(keys, k_mark)
+    v_heads, g_heads = heads(value, v_mark), heads(grad, g_mark)
+    q_small = (query * 0.125).astype(bf16)
+    k_small = keys.astype(bf16)
+    grad16 = g_ref[...]
+    low = lower[:block]
+    q_grads = [None, None]
+    v_sum = jnp.zeros((1, 128), f32)
+    for start in range(0, rows, block):
+        stop = start + block
+        dv, dk = [], []
+        for head in range(2):
+            probs = jnp.exp(dot32(k_heads[head][start:stop], q_heads[head], NT))
+            delta = dot32(v_heads[head][start:stop], g_heads[head], NT)
+            dv.append(dot32(probs.astype(bf16), grad16))
+            change = (probs * delta).astype(bf16)
+            dk.append(dot32(change, q_small))
+            part = dot32(change, k_small[start:stop], TN)
+            q_grads[head] = part if q_grads[head] is None else q_grads[head] + part
+        v_grad = jnp.where(low, dv[0], dv[1])
+        v_sum = v_sum + jnp.sum(v_grad, axis=0, keepdims=True)
+        d_ref[1, start:stop, :] = jnp.where(low, dk[0], dk[1]).astype(bf16)
+        d_ref[2, start:stop, :] = v_grad.astype(bf16)
+    q_grad = jnp.where(lower, q_grads[0], q_grads[1])
+    d_ref[0] = q_grad.astype(bf16)
+    sum_ref[0:1, :] = jnp.sum(q_grad, axis=0, keepdims=True)
+    sum_ref[1:2, :] = v_sum
+
+
+def part_spec(index, rows, base):
+    return pl.BlockSpec((None, rows, 128), lambda i: (index, 0, base + i))
+
+
+def attend_forward(packed, seg_col, base, pairs, block=512):
+    rows = packed.shape[1]
+    flat = pl.BlockSpec((rows, 128), lambda i: (0, i))
+    return pl.pallas_call(
+        functools.partial(forward_kernel, block=block),
+        grid=(pairs,),
+        in_specs=[part_spec(k, rows, base) for k in range(3)] + [pl.BlockSpec((rows, 1), lambda i: (0, 0))],
+        out_specs=[flat, flat],
+        out_shape=[
+            jax.ShapeDtypeStruct((rows, pairs * 128), jnp.bfloat16),
+            jax.ShapeDtypeStruct((rows, pairs * 128), jnp.float32),
+        ],
+        compiler_params=pltpu.CompilerParams(vmem_limit_bytes=48 * 2**20),
+        name="attend_forward",
+    )(packed, packed, packed, seg_col)
+
+
+def attend_backward(packed, grad, context, lse, seg_col, base, pairs, block=256):
+    rows = packed.shape[1]
+    shifted = pl.BlockSpec((rows, 128), lambda i: (0, base + i))
+    return pl.pallas_call(
+        functools.partial(backward_kernel, block=block),
+        grid=(pairs,),
+        in_specs=[part_spec(k, rows, base) for k in range(3)] + [shifted] * 3 + [pl.BlockSpec((rows, 1), lambda i: (0, 0))],
+        out_specs=[
+            pl.BlockSpec((3, rows, 128), lambda i: (0, 0, i)),
+            pl.BlockSpec((2, 128), lambda i: (0, i)),
+        ],
+        out_shape=[
+            jax.ShapeDtypeStruct((3, rows, pairs * 128), jnp.bfloat16),
+            jax.ShapeDtypeStruct((2, pairs * 128), jnp.float32),
+        ],
+        compiler_params=pltpu.CompilerParams(vmem_limit_bytes=48 * 2**20),
+        name="attend_backward",
+    )(packed, packed, packed, grad, context, lse, seg_col)
+
 
 SWAP = [(core * 2 + side, side * 2 + core) for core in range(2) for side in range(2)]
 FLIP = [(0, 1), (1, 0)]
@@ -306,7 +343,9 @@
     packed = (
         jnp.einsum("nd,kde->kne", tok_full, qkv16, preferred_element_type=f32) + bias_rows
     ).astype(bf16)
-    context, logsum = attend_forward(packed, segments)
+    seg_col = segments.reshape(-1, 1)
+    pairs = dev_width // 128
+    context, logsum = attend_forward(packed, seg_col, 0, pairs)
 
     def summed(left, right, form):
         away = jnp.einsum(form, left[rows:], right, preferred_element_type=f32)
@@ -339,9 +378,7 @@
     attended_full = jnp.concatenate([first16, core_exchange(first16)])
     context_grad = jnp.einsum("nd,de->ne", attended_full, out_t, preferred_element_type=f32).astype(bf16)
     out_grad = jnp.einsum("nd,ne->de", attended_full, context, preferred_element_type=f32).astype(bf16)
-    packed_grad = attend_backward(packed, context_grad, logsum, segments)
-    bqv_local = jnp.stack([jnp.sum(packed_grad[0], axis=0), jnp.sum(packed_grad[2], axis=0)])
-    packed16 = packed_grad.astype(bf16)
+    packed16, bqv_local = attend_backward(packed, context_grad, context, logsum, seg_col, 0, pairs)
     qkv_grad = jnp.einsum("nd,kne->kde", tok_full, packed16, preferred_element_type=f32).astype(bf16)
     away = jnp.einsum("kne,kde->nd", packed16[:, rows:], qkv16, preferred_element_type=f32)
     other = core_exchange(away.astype(bf16))

time: 698 us -> 577 us (0.83)
  matrix products: 193 us -> 93.3 us
  Pallas kernels: 0 us -> 43.3 us
  other arithmetic: 94.1 us -> 60.2 us
  local copies, waits for them, and re-layouts: 73.9 us -> 54.1 us
  loops' own time: 7.05 us -> 0 us
    dot_general x14 -> x0, matrix products: 102 us -> none  [the longest x4 38.1 us: one_block(): jnp.einsum('qhd,khd->hqk', query_rows, key_all, preferred_element_type=jn...]
    pallas_call x0 -> x2, Pallas kernels: none -> 43.3 us  [the longest x1 28.7 us: attend_backward(): pl.pallas_call(functools.partial(backward_kernel, block=block), grid=(pai...]
    convert_element_type x2 -> x0, other arithmetic: 18.7 us -> none  [one_block(): score_grad = (probs * (prob_grad - inner_sum)).astype(jnp.bfloat16)]
    reduce_sum x4 -> x0, other arithmetic: 12.3 us -> none  [the longest x2 8.48 us: one_block(): row_total = jnp.sum(exp_scores, axis=-1, keepdims=True)]
    another operation x6 -> x0, local copies, waits for them, and re-layouts: 9.69 us -> none  [the longest x4 9.54 us: attend_backward(): jnp.stack([query_grad.reshape(total_rows, dev_width), key_grad.reshape(to...]
    another operation x2 -> x0, loops' own time: 7.05 us -> none  [the longest x1 5.44 us: one_sequence(): lax.scan(one_block, (zero_grad, zero_grad), jnp.arange(blocks_per, dtype=...]
    unnamed x204 -> x174, local copies, waits for them, and re-layouts: 23.3 us -> 21.3 us
  transfers between devices with their start and end apart: 67 -> 67, of which waited for: 30 -> 32; matrix products, arithmetic and copies ran while one was open for 45% -> 27% of each run, Pallas kernels for 0% -> 8%
where the time goes in v2:
time: 577 us; the launch traced here: 568 us
  waiting for transfers between devices  201 us (35%)
  starting transfers between devices  114 us (20%)
  matrix products  93.3 us (16%)
  other arithmetic  60.2 us (10%)
  local copies, waits for them, and re-layouts  54.1 us (9%)
  Pallas kernels  43.3 us (8%)
    ppermute x30, waiting for transfers between devices, chip_exchange(): return lax.ppermute(values, 'chip', [(k, k ^ mask) for k in range(count)])  136 us
    ppermute x14, starting transfers between devices, swap(): return lax.ppermute(values, ('core', 'tensor'), SWAP)  64.2 us
    ppermute x14, waiting for transfers between devices, y_exchange(): return lax.ppermute(values, 'tensor', FLIP)  32.5 us
    ppermute x14, waiting for transfers between devices, swap(): return lax.ppermute(values, ('core', 'tensor'), SWAP)  31.2 us
    pallas_call x1, Pallas kernels, attend_backward(): pl.pallas_call(functools.partial(backward_kernel, block=block), grid=(pai...  28.7 us
    dot_general x1, matrix products, body(): upper = jnp.dot(hidden_full, up16, preferred_element_type=f32) + b_up  25.9 us
    ppermute x30, starting transfers between devices, chip_exchange(): return lax.ppermute(values, 'chip', [(k, k ^ mask) for k in range(count)])  23.7 us
    unnamed x174, local copies, waits for them, and re-layouts  21.3 us
  transfers between devices with their start and end apart: 67, of which 32 were waited for; matrix products, arithmetic and copies ran while one was open for 27% of the time, Pallas kernels for 8%

profile of v2, /device:TPU:1, one launch (start us, length us, event | category | flops | bytes accessed | tf_op | source)
XLA Modules:
  0.0 568.1 jit_solution(11366867395745506067)
XLA Ops:
  32.8 8.4 %collective-permute-done.2 = bf16[2,64,768]{2,1,0:T(8,128)(2,1)S(1)} collective-permute-done((bf16[2,64,768]{2,1,0:T(8,128)(2,1)S(1)}, bf16[2,64,768]{2,1,0:T(8,128)(2,1)S(1)}, u32[]{:S(2)}, u32[]{:S(2)}) %collective-permute-start.2) | collective-permute-done | bytes 196640 | tf_op jit(solution)/shard_map/ppermute | solution.py:200
  50.8 30.4 %collective-permute-done.3 = bf16[2,2,64,768]{3,2,1,0:T(8,128)(2,1)S(1)} collective-permute-done((bf16[2,2,64,768]{3,2,1,0:T(8,128)(2,1)S(1)}, bf16[2,2,64,768]{3,2,1,0:T(8,128)(2,1)S(1)}, u32[]{:S(2)}, u32[]{:S(2)}) %collective-permute-start.3) | collective-permute-done | bytes 393248 | tf_op jit(solution)/shard_map/ppermute | solution.py:200
  99.3 11.2 %collective-permute-done.5 = bf16[2,2,2,64,768]{4,3,2,1,0:T(8,128)(2,1)S(1)} collective-permute-done((bf16[2,2,2,64,768]{4,3,2,1,0:T(8,128)(2,1)S(1)}, bf16[2,2,2,64,768]{4,3,2,1,0:T(8,128)(2,1)S(1)}, u32[]{:S(2)}, u32[]{:S(2)}) %collective-permute-start.5) | collective-permute-done | bytes 786464 | tf_op jit(solution)/shard_map/ppermute | solution.py:195
  119.8 6.0 %collective-permute-done.14 = bf16[2,2,64,1280]{3,2,1,0:T(8,128)(2,1)} collective-permute-done((bf16[2,2,64,1280]{3,2,1,0:T(8,128)(2,1)}, bf16[2,2,64,1280]{3,2,1,0:T(8,128)(2,1)}, u32[]{:S(2)}, u32[]{:S(2)}) %collective-permute-start.14) | collective-permute-done | bytes 655392 | tf_op jit(solution)/shard_map/ppermute | solution.py:200
  143.1 6.8 %fusion.6.q_ref.k_ref.v_ref = bf16[3,1024,512]{2,1,0:T(8,128)(2,1)} fusion(f32[3,512]{1,0:T(4,128)S(1)} %pad_maximum_fusion.48, bf16[512,1024]{1,0:T(8,128)(2,1)} %collective-permute-done.8, bf16[512,1024]{1,0:T(8,128)(2,1)} %collective-permute-done, bf16[1,1024,512]{1,2,0:T(8,128)(2,1)S(1)} %maximum_bitcast_fusion.5, ...), kind=kOutput, calls=%fused_computation.22 | convolution fusion | flops 3231711232 | bytes 8394752 | tf_op jit(solution)/shard_map/nd,kde->kne/dot_general | solution.py:344
  149.8 14.6 %attend_forward.1 = (bf16[1024,512]{1,0:T(8,128)(2,1)S(1)}, f32[1024,512]{1,0:T(8,128)S(1)}) custom-call(bf16[3,1024,512]{2,1,0:T(8,128)(2,1)} %fusion.6.q_ref.k_ref.v_ref, bf16[3,1024,512]{2,1,0:T(8,128)(2,1)} %fusion.6.q_ref.k_ref.v_ref, bf16[3,1024,512]{2,1,0:T(8,128)(2,1)} %fusion.6.q_ref.k_ref.v_ref, s32[1024,1]{1,0:T(8,128)S(1)} %copy.81.seg_ref), custom_call_target="tpu_custom_call" | custom-call | tf_op jit(solution)/shard_map/attend_forward/pallas_call | solution.py:148
  174.0 11.0 %collective-permute-done.23 = bf16[2,2,64,1024]{3,2,1,0:T(8,128)(2,1)S(1)} collective-permute-done((bf16[2,2,64,1024]{3,2,1,0:T(8,128)(2,1)S(1)}, bf16[2,2,64,1024]{3,2,1,0:T(8,128)(2,1)S(1)}, u32[]{:S(2)}, u32[]{:S(2)}) %collective-permute-start.23) | collective-permute-done | bytes 524320 | tf_op jit(solution)/shard_map/ppermute | solution.py:200
  192.9 17.2 %collective-permute-done.26 = bf16[2,2,2,64,1024]{4,3,1,0,2:T(8,128)(2,1)S(1)} collective-permute-done((bf16[2,2,2,64,1024]{4,3,1,0,2:T(8,128)(2,1)S(1)}, bf16[2,2,2,64,1024]{4,3,1,0,2:T(8,128)(2,1)S(1)}, u32[]{:S(2)}, u32[]{:S(2)}) %collective-permute-start.26) | collective-permute-done | bytes 1048608 | tf_op jit(solution)/shard_map/ppermute | solution.py:200
  212.9 25.9 %multiply_convert_fusion = (bf16[1024,2048]{1,0:T(8,128)(2,1)S(1)}, f32[1024,2048]{1,0:T(8,128)}, f32[1024,2048]{1,0:T(8,128)}) fusion(f32[2048]{0:T(1024)S(1)} %slice.369, bf16[1024,1024]{1,0:T(8,128)(2,1)S(1)} %slice.368, bf16[1024,1024]{1,0:T(8,128)(2,1)S(1)} %slice.367, bf16[512,1024]{1,0:T(8,128)(2,1)S(1)} %collective-permute-done.19, ...), kind=kOutput, calls=%fused_computation.3 | convolution fusion | flops 4445962240 | bytes 27271168 | tf_op jit(solution)/shard_map/dot_general | solution.py:360
  249.4 10.7 %collective-permute-done.29 = bf16[512,1024]{1,0:T(8,128)(2,1)S(1)} collective-permute-done((bf16[512,1024]{1,0:T(8,128)(2,1)S(1)}, bf16[512,1024]{1,0:T(8,128)(2,1)S(1)}, u32[]{:S(2)}, u32[]{:S(2)}) %collective-permute-start.29) | collective-permute-done | bytes 1048608 | tf_op jit(solution)/shard_map/ppermute | solution.py:187
  268.4 7.4 %convolution_convert_fusion = bf16[1024,2048]{1,0:T(8,128)(2,1)S(1)} fusion(bf16[1024,2048]{1,0:T(8,128)(2,1)} %copy-done.81, bf16[512,1024]{1,0:T(8,128)(2,1)} %collective-permute-done.30, bf16[512,1024]{1,0:T(8,128)(2,1)} %get-tuple-element.82), kind=kOutput, calls=%fused_computation.20 | convolution fusion | flops 4301258752 | bytes 10485760 | tf_op jit(solution)/shard_map/nd,nf->df/dot_general | solution.py:371
  279.7 13.6 %fusion.105 = (f32[2048]{0:T(1024)S(1)}, bf16[1024,2048]{1,0:T(8,128)(2,1)}) fusion(f32[1024,2048]{1,0:T(8,128)} %get-tuple-element.63, bf16[1024,1024]{1,0:T(8,128)(2,1)S(1)} %bitcast.342, bf16[1024,1024]{1,0:T(8,128)(2,1)S(1)} %bitcast.345, bf16[512,1024]{1,0:T(8,128)(2,1)} %collective-permute-done.30, bf16[512,1024]{1,0:T(8,128)(2,1)} %get-tuple-element.82, ...), kind=kOutput, calls=%fused_computation.326 | convolution fusion | flops 4341102592 | bytes 27279360 | tf_op jit(solution)/shard_map/nd,df->nf/dot_general | solution.py:370
  297.2 7.0 %collective-permute-start.31 = (bf16[512,1024]{1,0:T(8,128)(2,1)S(1)}, bf16[512,1024]{1,0:T(8,128)(2,1)S(1)}, u32[]{:S(2)}, u32[]{:S(2)}) collective-permute-start(bf16[512,1024]{1,0:T(8,128)(2,1)S(1)} %fusion.37), channel_id=1, source_target_pairs={{0,2},{2,0},{1,3},{3,1},{4,6},{6,4},{5,7},{7,5},{8,10},{10,8},{9,1... | collective-permute-start | bytes 3145736 | tf_op jit(solution)/shard_map/ppermute | solution.py:191
  308.0 6.7 %convolution_convert_fusion.1 = bf16[1024,2048]{1,0:T(8,128)(2,1)} fusion(bf16[1024,2048]{1,0:T(8,128)(2,1)S(1)} %copy-done.80, bf16[512,1024]{1,0:T(8,128)(2,1)S(1)} %copy-done.79, bf16[512,1024]{1,0:T(8,128)(2,1)S(1)} %copy-done.51), kind=kOutput, calls=%fused_computation.21 | convolution fusion | flops 4301258752 | bytes 10485760 | tf_op jit(solution)/shard_map/nd,nf->df/dot_general | solution.py:374
  376.6 28.7 %attend_backward.1 = (bf16[3,1024,512]{2,1,0:T(8,128)(2,1)}, f32[2,512]{1,0:T(2,128)S(1)}) custom-call(bf16[3,1024,512]{2,1,0:T(8,128)(2,1)} %fusion.6.q_ref.k_ref.v_ref, bf16[3,1024,512]{2,1,0:T(8,128)(2,1)} %fusion.6.q_ref.k_ref.v_ref, bf16[3,1024,512]{2,1,0:T(8,128)(2,1)} %fusion.6.q_ref.k_ref.v_ref, ...), custom_call_target="tpu_custom_call" | custom-call | tf_op jit(solution)/shard_map/attend_backward/pallas_call | solution.py:165
  435.0 8.7 %collective-permute-start.46 = (f32[2,512]{1,0:T(2,128)S(1)}, f32[2,512]{1,0:T(2,128)S(1)}, u32[]{:S(2)}, u32[]{:S(2)}) collective-permute-start(f32[2,512]{1,0:T(2,128)S(1)} %add.362), channel_id=1, source_target_pairs={{0,0},{1,2},{2,1},{3,3},{4,4},{5,6},{6,5},{7,7},{8,8},{9,10},{10,9... | collective-permute-start | bytes 12296 | tf_op jit(solution)/shard_map/ppermute | solution.py:187
  447.4 7.8 %collective-permute-done.66 = bf16[2,64,1024]{2,1,0:T(8,128)(2,1)S(1)} collective-permute-done((bf16[2,64,1024]{2,1,0:T(8,128)(2,1)S(1)}, bf16[2,64,1024]{2,1,0:T(8,128)(2,1)S(1)}, u32[]{:S(2)}, u32[]{:S(2)}) %collective-permute-start.66) | collective-permute-done | bytes 262176 | tf_op jit(solution)/shard_map/ppermute | solution.py:187
  456.7 10.4 %collective-permute-done.35 = bf16[2,2,2,64,768]{4,3,2,1,0:T(8,128)(2,1)S(1)} collective-permute-done((bf16[2,2,2,64,768]{4,3,2,1,0:T(8,128)(2,1)S(1)}, bf16[2,2,2,64,768]{4,3,2,1,0:T(8,128)(2,1)S(1)}, u32[]{:S(2)}, u32[]{:S(2)}) %collective-permute-start.35) | collective-permute-done | bytes 786464 | tf_op jit(solution)/shard_map/ppermute | solution.py:195
  482.4 11.6 %collective-permute-done.39 = bf16[2,2,64,768]{3,2,1,0:T(8,128)(2,1)S(1)} collective-permute-done((bf16[2,2,64,768]{3,2,1,0:T(8,128)(2,1)S(1)}, bf16[2,2,64,768]{3,2,1,0:T(8,128)(2,1)S(1)}, u32[]{:S(2)}, u32[]{:S(2)}) %collective-permute-start.39) | collective-permute-done | bytes 393248 | tf_op jit(solution)/shard_map/ppermute | solution.py:200
  498.8 8.9 %collective-permute-start.41 = (bf16[2,64,768]{2,1,0:T(8,128)(2,1)S(1)}, bf16[2,64,768]{2,1,0:T(8,128)(2,1)S(1)}, u32[]{:S(2)}, u32[]{:S(2)}) collective-permute-start(bf16[2,64,768]{2,1,0:T(8,128)(2,1)S(1)} %fusion.78), channel_id=1, source_target_pairs={{0,0},{1,2},{2,1},{3,3},{4,4},{5,6},{6,5},{7,7},{8,8},{9,10},{10,9... | collective-permute-start | bytes 589832 | tf_op jit(solution)/shard_map/ppermute | solution.py:187
  512.7 9.5 %collective-permute-start.34 = (bf16[512,1024]{1,0:T(8,128)(2,1)S(1)}, bf16[512,1024]{1,0:T(8,128)(2,1)S(1)}, u32[]{:S(2)}, u32[]{:S(2)}) collective-permute-start(bf16[512,1024]{1,0:T(8,128)(2,1)S(1)} %fusion.24), channel_id=1, source_target_pairs={{0,0},{1,2},{2,1},{3,3},{4,4},{5,6},{6,5},{7,7},{8,8},{9,10},{10,9... | collective-permute-start | bytes 3145736 | tf_op jit(solution)/shard_map/ppermute | solution.py:187
  522.3 17.1 %collective-permute-done.51 = bf16[2,2,64,1280]{3,2,0,1:T(8,128)(2,1)S(1)} collective-permute-done((bf16[2,2,64,1280]{3,2,0,1:T(8,128)(2,1)S(1)}, bf16[2,2,64,1280]{3,2,0,1:T(8,128)(2,1)S(1)}, u32[]{:S(2)}, u32[]{:S(2)}) %collective-permute-start.51) | collective-permute-done | bytes 655392 | tf_op jit(solution)/shard_map/ppermute | solution.py:200
  539.8 7.8 %collective-permute-done.52 = bf16[2,64,1280]{2,1,0:T(8,128)(2,1)S(1)} collective-permute-done((bf16[2,64,1280]{2,1,0:T(8,128)(2,1)S(1)}, bf16[2,64,1280]{2,1,0:T(8,128)(2,1)S(1)}, u32[]{:S(2)}, u32[]{:S(2)}) %collective-permute-start.52) | collective-permute-done | bytes 327712 | tf_op jit(solution)/shard_map/ppermute | solution.py:200
  547.7 9.8 %collective-permute-start.53 = (bf16[2,64,1280]{2,1,0:T(8,128)(2,1)S(1)}, bf16[2,64,1280]{2,1,0:T(8,128)(2,1)S(1)}, u32[]{:S(2)}, u32[]{:S(2)}) collective-permute-start(bf16[2,64,1280]{2,1,0:T(8,128)(2,1)S(1)} %fusion.57), channel_id=1, source_target_pairs={{0,0},{1,2},{2,1},{3,3},{4,4},{5,6},{6,5},{7,7},{8,8},{9,10},{10,9... | collective-permute-start | bytes 983048 | tf_op jit(solution)/shard_map/ppermute | solution.py:187
  (478 shorter events, 268.2 us)
Async XLA Ops:
  1.9 23.7 %collective-permute-start.1 = (bf16[2,64,768]{2,1,0:T(8,128)(2,1)S(1)}, bf16[2,64,768]{2,1,0:T(8,128)(2,1)S(1)}, u32[]{:S(2)}, u32[]{:S(2)}) collective-permute-start(bf16[2,64,768]{2,1,0:T(8,128)(2,1)S(1)} %pad_maximum_fusion.45), channel_id=1, source_target_pairs={{0,0},{1,2},{2,1},{3,3},{4,4},{5,6},{6,5},{7,7},{8,8},{9,10},{10,9... | collective-permute-start | bytes 589832 | tf_op jit(solution)/shard_map/ppermute | solution.py:187
  6.5 75.4 %collective-permute-start = (bf16[512,1024]{1,0:T(8,128)(2,1)}, bf16[512,1024]{1,0:T(8,128)(2,1)}, u32[]{:S(2)}, u32[]{:S(2)}) collective-permute-start(bf16[512,1024]{1,0:T(8,128)(2,1)} %param.24), channel_id=1, source_target_pairs={{0,0},{1,2},{2,1},{3,3},{4,4},{5,6},{6,5},{7,7},{8,8},{9,10},{10,9... | collective-permute-start | bytes 3145736 | tf_op jit(solution)/shard_map/ppermute | solution.py:187
  41.2 39.9 %collective-permute-start.3 = (bf16[2,2,64,768]{3,2,1,0:T(8,128)(2,1)S(1)}, bf16[2,2,64,768]{3,2,1,0:T(8,128)(2,1)S(1)}, u32[]{:S(2)}, u32[]{:S(2)}) collective-permute-start(bf16[2,2,64,768]{3,2,1,0:T(8,128)(2,1)S(1)} %maximum_select_fusion.20), channel_id=1, source_target_pairs={{0,16},{4,20},{8,24},{12,28},{16,0},{20,4},{24,8},{28,12},{1,17},{... | collective-permute-start | bytes 1179656 | tf_op jit(solution)/shard_map/ppermute | solution.py:200
  44.9 44.7 %collective-permute-start.22 = (bf16[2,2,64,1024]{3,2,1,0:T(8,128)(2,1)S(1)}, bf16[2,2,64,1024]{3,2,1,0:T(8,128)(2,1)S(1)}, u32[]{:S(2)}, u32[]{:S(2)}) collective-permute-start(bf16[2,2,64,1024]{3,2,1,0:T(8,128)(2,1)S(1)} %maximum_select_fusion.19), channel_id=1, source_target_pairs={{0,16},{4,20},{8,24},{12,28},{16,0},{20,4},{24,8},{28,12},{1,17},{... | collective-permute-start | bytes 1572872 | tf_op jit(solution)/shard_map/ppermute | solution.py:200
  50.5 46.1 %collective-permute-start.13 = (bf16[2,2,64,1280]{3,2,1,0:T(8,128)(2,1)S(1)}, bf16[2,2,64,1280]{3,2,1,0:T(8,128)(2,1)S(1)}, u32[]{:S(2)}, u32[]{:S(2)}) collective-permute-start(bf16[2,2,64,1280]{3,2,1,0:T(8,128)(2,1)S(1)} %maximum_select_fusion.18), channel_id=1, source_target_pairs={{0,16},{4,20},{8,24},{12,28},{16,0},{20,4},{24,8},{28,12},{1,17},{... | collective-permute-start | bytes 1966088 | tf_op jit(solution)/shard_map/ppermute | solution.py:200
  81.9 59.6 %collective-permute-start.8 = (bf16[512,1024]{1,0:T(8,128)(2,1)}, bf16[512,1024]{1,0:T(8,128)(2,1)}, u32[]{:S(2)}, u32[]{:S(2)}) collective-permute-start(bf16[512,1024]{1,0:T(8,128)(2,1)} %collective-permute-done), channel_id=1, source_target_pairs={{0,2},{2,0},{1,3},{3,1},{4,6},{6,4},{5,7},{7,5},{8,10},{10,8},{9,1... | collective-permute-start | bytes 3145736 | tf_op jit(solution)/shard_map/ppermute | solution.py:191
  98.3 27.5 %collective-permute-start.14 = (bf16[2,2,64,1280]{3,2,1,0:T(8,128)(2,1)}, bf16[2,2,64,1280]{3,2,1,0:T(8,128)(2,1)}, u32[]{:S(2)}, u32[]{:S(2)}) collective-permute-start(bf16[2,2,64,1280]{3,2,1,0:T(8,128)(2,1)} %get-tuple-element.100), channel_id=1, source_target_pairs={{0,4},{4,0},{8,12},{12,8},{16,20},{20,16},{24,28},{28,24},{1,5},{5... | collective-permute-start | bytes 1966088 | tf_op jit(solution)/shard_map/ppermute | solution.py:200
  99.3 29.1 %collective-permute-start.16 = (bf16[2,2,64,1280]{3,2,1,0:T(8,128)(2,1)}, bf16[2,2,64,1280]{3,2,1,0:T(8,128)(2,1)}, u32[]{:S(2)}, u32[]{:S(2)}) collective-permute-start(bf16[2,2,64,1280]{3,2,1,0:T(8,128)(2,1)} %get-tuple-element.102), channel_id=1, source_target_pairs={{0,1},{1,0},{2,3},{3,2},{4,5},{5,4},{6,7},{7,6},{8,9},{9,8},{10,11... | collective-permute-start | bytes 1966088 | tf_op jit(solution)/shard_map/ppermute | solution.py:195
  128.4 36.0 %collective-permute-start.15 = (bf16[2,2,2,64,1280]{4,3,2,1,0:T(8,128)(2,1)}, bf16[2,2,2,64,1280]{4,3,2,1,0:T(8,128)(2,1)}, u32[]{:S(2)}, u32[]{:S(2)}) collective-permute-start(bf16[2,2,2,64,1280]{4,3,2,1,0:T(8,128)(2,1)} %maximum_select_fusion.7), channel_id=1, source_target_pairs={{0,1},{1,0},{2,3},{3,2},{4,5},{5,4},{6,7},{7,6},{8,9},{9,8},{10,11... | collective-permute-start | bytes 3932168 | tf_op jit(solution)/shard_map/ppermute | solution.py:195
  131.0 35.8 %collective-permute-start.17 = (bf16[2,2,2,64,1280]{4,3,1,0,2:T(8,128)(2,1)}, bf16[2,2,2,64,1280]{4,3,1,0,2:T(8,128)(2,1)}, u32[]{:S(2)}, u32[]{:S(2)}) collective-permute-start(bf16[2,2,2,64,1280]{4,3,1,0,2:T(8,128)(2,1)} %maximum_select_fusion.9), channel_id=1, source_target_pairs={{0,4},{4,0},{8,12},{12,8},{16,20},{20,16},{24,28},{28,24},{1,5},{5... | collective-permute-start | bytes 3932168 | tf_op jit(solution)/shard_map/ppermute | solution.py:200
  185.1 25.5 %collective-permute-start.24 = (bf16[2,2,2,64,1024]{4,3,2,1,0:T(8,128)(2,1)S(1)}, bf16[2,2,2,64,1024]{4,3,2,1,0:T(8,128)(2,1)S(1)}, u32[]{:S(2)}, u32[]{:S(2)}) collective-permute-start(bf16[2,2,2,64,1024]{4,3,2,1,0:T(8,128)(2,1)S(1)} %maximum_select_fusion.11), channel_id=1, source_target_pairs={{0,1},{1,0},{2,3},{3,2},{4,5},{5,4},{6,7},{7,6},{8,9},{9,8},{10,11... | collective-permute-start | bytes 3145736 | tf_op jit(solution)/shard_map/ppermute | solution.py:195
  187.0 23.1 %collective-permute-start.26 = (bf16[2,2,2,64,1024]{4,3,1,0,2:T(8,128)(2,1)S(1)}, bf16[2,2,2,64,1024]{4,3,1,0,2:T(8,128)(2,1)S(1)}, u32[]{:S(2)}, u32[]{:S(2)}) collective-permute-start(bf16[2,2,2,64,1024]{4,3,1,0,2:T(8,128)(2,1)S(1)} %maximum_select_fusion.13), channel_id=1, source_target_pairs={{0,4},{4,0},{8,12},{12,8},{16,20},{20,16},{24,28},{28,24},{1,5},{5... | collective-permute-start | bytes 3145736 | tf_op jit(solution)/shard_map/ppermute | solution.py:200
  265.4 60.7 %collective-permute-start.28 = (bf16[512,1024]{1,0:T(8,128)(2,1)}, bf16[512,1024]{1,0:T(8,128)(2,1)}, u32[]{:S(2)}, u32[]{:S(2)}) collective-permute-start(bf16[512,1024]{1,0:T(8,128)(2,1)} %get-tuple-element.80), channel_id=1, source_target_pairs={{0,0},{1,2},{2,1},{3,3},{4,4},{5,6},{6,5},{7,7},{8,8},{9,10},{10,9... | collective-permute-start | bytes 3145736 | tf_op jit(solution)/shard_map/ppermute | solution.py:187
  278.6 47.9 %collective-permute-start.62 = (bf16[2,2,2,64,1024]{4,3,1,0,2:T(8,128)(2,1)}, bf16[2,2,2,64,1024]{4,3,1,0,2:T(8,128)(2,1)}, u32[]{:S(2)}, u32[]{:S(2)}) collective-permute-start(bf16[2,2,2,64,1024]{4,3,1,0,2:T(8,128)(2,1)} %bitcast.325), channel_id=1, source_target_pairs={{0,4},{4,0},{8,12},{12,8},{16,20},{20,16},{24,28},{28,24},{1,5},{5... | collective-permute-start | bytes 3145736 | tf_op jit(solution)/shard_map/ppermute | solution.py:200
  306.6 28.5 %collective-permute-start.60 = (bf16[2,2,2,64,1024]{4,3,1,0,2:T(8,128)(2,1)}, bf16[2,2,2,64,1024]{4,3,1,0,2:T(8,128)(2,1)}, u32[]{:S(2)}, u32[]{:S(2)}) collective-permute-start(bf16[2,2,2,64,1024]{4,3,1,0,2:T(8,128)(2,1)} %bitcast.326), channel_id=1, source_target_pairs={{0,1},{1,0},{2,3},{3,2},{4,5},{5,4},{6,7},{7,6},{8,9},{9,8},{10,11... | collective-permute-start | bytes 3145736 | tf_op jit(solution)/shard_map/ppermute | solution.py:195
  354.4 68.8 %collective-permute-start.64 = (bf16[2,2,64,1024]{3,2,0,1:T(8,128)(2,1)}, bf16[2,2,64,1024]{3,2,0,1:T(8,128)(2,1)}, u32[]{:S(2)}, u32[]{:S(2)}) collective-permute-start(bf16[2,2,64,1024]{3,2,0,1:T(8,128)(2,1)} %fusion.61), channel_id=1, source_target_pairs={{0,16},{4,20},{8,24},{12,28},{16,0},{20,4},{24,8},{28,12},{1,17},{... | collective-permute-start | bytes 1572872 | tf_op jit(solution)/shard_map/ppermute | solution.py:200
  366.2 110.5 %collective-permute-start.49 = (bf16[2,2,2,64,1280]{4,3,1,0,2:T(8,128)(2,1)}, bf16[2,2,2,64,1280]{4,3,1,0,2:T(8,128)(2,1)}, u32[]{:S(2)}, u32[]{:S(2)}) collective-permute-start(bf16[2,2,2,64,1280]{4,3,1,0,2:T(8,128)(2,1)} %bitcast.323), channel_id=1, source_target_pairs={{0,4},{4,0},{8,12},{12,8},{16,20},{20,16},{24,28},{28,24},{1,5},{5... | collective-permute-start | bytes 3932168 | tf_op jit(solution)/shard_map/ppermute | solution.py:200
  373.2 107.5 %collective-permute-start.47 = (bf16[2,2,2,64,1280]{4,3,1,0,2:T(8,128)(2,1)}, bf16[2,2,2,64,1280]{4,3,1,0,2:T(8,128)(2,1)}, u32[]{:S(2)}, u32[]{:S(2)}) collective-permute-start(bf16[2,2,2,64,1280]{4,3,1,0,2:T(8,128)(2,1)} %bitcast.324), channel_id=1, source_target_pairs={{0,1},{1,0},{2,3},{3,2},{4,5},{5,4},{6,7},{7,6},{8,9},{9,8},{10,11... | collective-permute-start | bytes 3932168 | tf_op jit(solution)/shard_map/ppermute | solution.py:195
  429.0 26.3 %collective-permute-start.37 = (bf16[2,2,2,64,768]{4,3,1,0,2:T(8,128)(2,1)}, bf16[2,2,2,64,768]{4,3,1,0,2:T(8,128)(2,1)}, u32[]{:S(2)}, u32[]{:S(2)}) collective-permute-start(bf16[2,2,2,64,768]{4,3,1,0,2:T(8,128)(2,1)} %bitcast.327), channel_id=1, source_target_pairs={{0,4},{4,0},{8,12},{12,8},{16,20},{20,16},{24,28},{28,24},{1,5},{5... | collective-permute-start | bytes 2359304 | tf_op jit(solution)/shard_map/ppermute | solution.py:200
  455.2 55.6 %collective-permute-start.33 = (bf16[512,1024]{1,0:T(8,128)(2,1)S(1)}, bf16[512,1024]{1,0:T(8,128)(2,1)S(1)}, u32[]{:S(2)}, u32[]{:S(2)}) collective-permute-start(bf16[512,1024]{1,0:T(8,128)(2,1)S(1)} %copy-done.77), channel_id=1, source_target_pairs={{0,2},{2,0},{1,3},{3,1},{4,6},{6,4},{5,7},{7,5},{8,10},{10,8},{9,1... | collective-permute-start | bytes 3145736 | tf_op jit(solution)/shard_map/ppermute | solution.py:191
  478.5 29.2 %collective-permute-start.50 = (bf16[2,2,64,1280]{3,2,1,0:T(8,128)(2,1)S(1)}, bf16[2,2,64,1280]{3,2,1,0:T(8,128)(2,1)S(1)}, u32[]{:S(2)}, u32[]{:S(2)}) collective-permute-start(bf16[2,2,64,1280]{3,2,1,0:T(8,128)(2,1)S(1)} %dynamic-slice_bitcast_fusion.1), channel_id=1, source_target_pairs={{0,1},{1,0},{2,3},{3,2},{4,5},{5,4},{6,7},{7,6},{8,9},{9,8},{10,11... | collective-permute-start | bytes 1966088 | tf_op jit(solution)/shard_map/ppermute | solution.py:195
  498.8 23.4 %collective-permute-start.41 = (bf16[2,64,768]{2,1,0:T(8,128)(2,1)S(1)}, bf16[2,64,768]{2,1,0:T(8,128)(2,1)S(1)}, u32[]{:S(2)}, u32[]{:S(2)}) collective-permute-start(bf16[2,64,768]{2,1,0:T(8,128)(2,1)S(1)} %fusion.78), channel_id=1, source_target_pairs={{0,0},{1,2},{2,1},{3,3},{4,4},{5,6},{6,5},{7,7},{8,8},{9,10},{10,9... | collective-permute-start | bytes 589832 | tf_op jit(solution)/shard_map/ppermute | solution.py:187
  508.7 30.8 %collective-permute-start.51 = (bf16[2,2,64,1280]{3,2,0,1:T(8,128)(2,1)S(1)}, bf16[2,2,64,1280]{3,2,0,1:T(8,128)(2,1)S(1)}, u32[]{:S(2)}, u32[]{:S(2)}) collective-permute-start(bf16[2,2,64,1280]{3,2,0,1:T(8,128)(2,1)S(1)} %fusion.54), channel_id=1, source_target_pairs={{0,16},{4,20},{8,24},{12,28},{16,0},{20,4},{24,8},{28,12},{1,17},{... | collective-permute-start | bytes 1966088 | tf_op jit(solution)/shard_map/ppermute | solution.py:200
  512.7 46.0 %collective-permute-start.34 = (bf16[512,1024]{1,0:T(8,128)(2,1)S(1)}, bf16[512,1024]{1,0:T(8,128)(2,1)S(1)}, u32[]{:S(2)}, u32[]{:S(2)}) collective-permute-start(bf16[512,1024]{1,0:T(8,128)(2,1)S(1)} %fusion.24), channel_id=1, source_target_pairs={{0,0},{1,2},{2,1},{3,3},{4,4},{5,6},{6,5},{7,7},{8,8},{9,10},{10,9... | collective-permute-start | bytes 3145736 | tf_op jit(solution)/shard_map/ppermute | solution.py:187
  (125 other events, 1329.8 us)

commit v3 on v2

v3 whole, which is shorter than its diff:
```python
import functools
import math

import jax
import jax.numpy as jnp
from jax import lax
from jax.experimental import pallas as pl
from jax.experimental.pallas import tpu as pltpu
from jax.sharding import Mesh, PartitionSpec as P

HEAD_DIM = 64
SEQ_LEN = 1024


NORM_EPS = 1e-05
MOMENTUM = 0.9
AVERAGE = 0.75
MATRIX_RATE = 0.05
FASTER_RATE = 0.25


def layer_norm(values, gain, shift):
    centred = values - jnp.mean(values, axis=-1, keepdims=True)
    spread = jnp.mean(centred * centred, axis=-1, keepdims=True)
    return centred * lax.rsqrt(spread + NORM_EPS) * gain + shift


def gelu_exact(values):
    return jax.nn.gelu(values, approximate=False)


def advance(weight, moment, average, gradient, step_rate):
    new_moment = MOMENTUM * moment + gradient
    new_weight = weight - step_rate * (gradient + MOMENTUM * new_moment)
    new_average = AVERAGE * average + (1.0 - AVERAGE) * new_weight
    return (new_moment, new_weight, new_average)


NT = (((1,), (1,)), ((), ()))
TN = (((0,), (0,)), ((), ()))
FAR = -1e30


def dot32(left, right, dims=(((1,), (0,)), ((), ()))):
    return lax.dot_general(left, right, dims, preferred_element_type=jnp.float32)


def three_terms(values):
    high = values.astype(jnp.bfloat16).astype(jnp.float32)
    rest = values - high
    middle = rest.astype(jnp.bfloat16).astype(jnp.float32)
    return (high, middle, rest - middle)


def place(lane, terms, other):
    high, middle, low = terms
    return jnp.where(lane == 63, high, jnp.where(lane == 62, middle, jnp.where(lane == 61, low, other)))


def forward_kernel(q_ref, k_ref, v_ref, seg_ref, out_ref, lse_ref, *, block):
    f32, bf16 = jnp.float32, jnp.bfloat16
    rows = q_ref.shape[0]
    lanes = lax.broadcasted_iota(jnp.int32, (rows, 128), 1)
    lower = lanes < HEAD_DIM
    lane = lanes & 63
    same = lane == seg_ref[...]
    q_mark = jnp.where(same, 1.0, 0.0)
    k_mark = jnp.where(same, 0.0, FAR)
    query = q_ref[...].astype(f32)
    keys = k_ref[...].astype(f32) * 0.125
    value = v_ref[...].astype(f32)
    q_heads = [jnp.where(lower, query, q_mark).astype(bf16), jnp.where(lower, q_mark, query).astype(bf16)]
    k_heads = [jnp.where(lower, keys, k_mark).astype(bf16), jnp.where(lower, k_mark, keys).astype(bf16)]
    v_heads = [jnp.where(lower, value, 1.0).astype(bf16), jnp.where(lower, 1.0, value).astype(bf16)]
    low = lower[:block]
    for start in range(0, rows, block):
        parts = []
        for head in range(2):
            scores = dot32(q_heads[head][start : start + block], k_heads[head], NT)
            top = jnp.max(scores, axis=1, keepdims=True)
            weights = jnp.exp(scores - top).astype(bf16)
            parts.append((dot32(weights, v_heads[head]), top))
        (first, top0), (second, top1) = parts
        total = pltpu.roll(jnp.where(low, second, first), HEAD_DIM, 1)
        out_ref[start : start + block, :] = (jnp.where(low, first, second) / total).astype(bf16)
        lse_ref[start : start + block, :] = jnp.where(low, top0, top1) + jnp.log(total)


def backward_kernel(q_ref, k_ref, v_ref, g_ref, o_ref, lse_ref, seg_ref, d_ref, sum_ref, *, block):
    f32, bf16 = jnp.float32, jnp.bfloat16
    rows = q_ref.shape[0]
    lanes = lax.broadcasted_iota(jnp.int32, (rows, 128), 1)
    lower = lanes < HEAD_DIM
    lane = lanes & 63
    same = lane == seg_ref[...]
    query = q_ref[...].astype(f32)
    keys = k_ref[...].astype(f32) * 0.125
    value = v_ref[...].astype(f32)
    grad = g_ref[...].astype(f32)
    lse = pltpu.roll(lse_ref[...], HEAD_DIM, 1)
    q_mark = place(lane, three_terms(-lse), jnp.where(same, 1.0, 0.0))
    k_mark = jnp.where(lane > 60, 1.0, jnp.where(same, 0.0, FAR))
    inner = grad * o_ref[...].astype(f32)
    inner0 = jnp.sum(jnp.where(lower, inner, 0.0), axis=1, keepdims=True)
    inner1 = jnp.sum(jnp.where(lower, 0.0, inner), axis=1, keepdims=True)
    g_mark = place(lane, three_terms(-jnp.where(lower, inner1, inner0)), 0.0)
    v_mark = jnp.where(lane > 60, 1.0, 0.0)

    def heads(values, mark):
        return [jnp.where(lower, values, mark).astype(bf16), jnp.where(lower, mark, values).astype(bf16)]

    q_heads, k_heads = heads(query, q_mark), heads(keys, k_mark)
    v_heads, g_heads = heads(value, v_mark), heads(grad, g_mark)
    q_small = (query * 0.125).astype(bf16)
    k_small = keys.astype(bf16)
    grad16 = g_ref[...]
    low = lower[:block]
    q_grads = [None, None]
    spot = pl.program_id(0) * 128
    places = [pl.ds(pl.multiple_of(k * (d_ref.shape[1] // 3) + spot, 128), 128) for k in range(3)]
    v_sum = jnp.zeros((1, 128), f32)
    for start in range(0, rows, block):
        stop = start + block
        dv, dk = [], []
        for head in range(2):
            probs = jnp.exp(dot32(k_heads[head][start:stop], q_heads[head], NT))
            delta = dot32(v_heads[head][start:stop], g_heads[head], NT)
            dv.append(dot32(probs.astype(bf16), grad16))
            change = (probs * delta).astype(bf16)
            dk.append(dot32(change, q_small))
            part = dot32(change, k_small[start:stop], TN)
            q_grads[head] = part if q_grads[head] is None else q_grads[head] + part
        v_grad = jnp.where(low, dv[0], dv[1])
        v_sum = v_sum + jnp.sum(v_grad, axis=0, keepdims=True)
        d_ref[start:stop, places[1]] = jnp.where(low, dk[0], dk[1]).astype(bf16)
        d_ref[start:stop, places[2]] = v_grad.astype(bf16)
    q_grad = jnp.where(lower, q_grads[0], q_grads[1])
    d_ref[:, places[0]] = q_grad.astype(bf16)
    sum_ref[0:1, :] = jnp.sum(q_grad, axis=0, keepdims=True)
    sum_ref[1:2, :] = v_sum


def part_specs(rows, pairs):
    return [pl.BlockSpec((rows, 128), lambda i, k=k: (0, k * pairs + i)) for k in range(3)]


def attend_forward(packed, seg_col, block=512):
    rows, width = packed.shape
    pairs = width // 384
    flat = pl.BlockSpec((rows, 128), lambda i: (0, i))
    return pl.pallas_call(
        functools.partial(forward_kernel, block=block),
        grid=(pairs,),
        in_specs=part_specs(rows, pairs) + [pl.BlockSpec((rows, 1), lambda i: (0, 0))],
        out_specs=[flat, flat],
        out_shape=[
            jax.ShapeDtypeStruct((rows, pairs * 128), jnp.bfloat16),
            jax.ShapeDtypeStruct((rows, pairs * 128), jnp.float32),
        ],
        compiler_params=pltpu.CompilerParams(vmem_limit_bytes=48 * 2**20),
        name="attend_forward",
    )(packed, packed, packed, seg_col)


def attend_backward(packed, grad, context, lse, seg_col, block=256):
    rows, width = packed.shape
    pairs = width // 384
    flat = pl.BlockSpec((rows, 128), lambda i: (0, i))
    return pl.pallas_call(
        functools.partial(backward_kernel, block=block),
        grid=(pairs,),
        in_specs=part_specs(rows, pairs) + [flat] * 3 + [pl.BlockSpec((rows, 1), lambda i: (0, 0))],
        out_specs=[
            pl.BlockSpec((rows, width), lambda i: (0, 0)),
            pl.BlockSpec((2, 128), lambda i: (0, i)),
        ],
        out_shape=[
            jax.ShapeDtypeStruct((rows, width), jnp.bfloat16),
            jax.ShapeDtypeStruct((2, pairs * 128), jnp.float32),
        ],
        compiler_params=pltpu.CompilerParams(vmem_limit_bytes=48 * 2**20),
        name="attend_backward",
    )(packed, packed, packed, grad, context, lse, seg_col)


SWAP = [(core * 2 + side, side * 2 + core) for core in range(2) for side in range(2)]
FLIP = [(0, 1), (1, 0)]


def swap(values):
    return lax.ppermute(values, ("core", "tensor"), SWAP)


def core_exchange(values):
    return lax.ppermute(values, "core", FLIP)


def y_exchange(values):
    return lax.ppermute(values, "tensor", FLIP)


def chip_exchange(values, mask):
    count = lax.axis_size("chip")
    return lax.ppermute(values, "chip", [(k, k ^ mask) for k in range(count)])


def bits():
    chip = lax.axis_index("chip")
    return (lax.axis_index("tensor"), chip & 1, (chip >> 1) & 1, (chip >> 2) & 1)


STAGES = (
    y_exchange,
    lambda values: chip_exchange(values, 1),
    lambda values: chip_exchange(values, 2),
    lambda values: chip_exchange(values, 4),
)
Y, X, Z1, Z2 = range(4)


def tie(*values):
    return lax.optimization_barrier(values)


def join(mine, other, stage, axis):
    first = bits()[stage] == 0
    return jnp.where(first, jnp.stack([mine, other], axis), jnp.stack([other, mine], axis))


class Gather:
    def __init__(self, both):
        self.rows, self.width = both.shape[1:]
        self.native = lax.axis_size("chip") != 8
        self.flight = ()
        self.held = (both,)
        self.step = 0

    def start(self):
        if self.native:
            return
        if self.step == 0:
            self.flight = (STAGES[Z2](self.held[0]),)
        elif self.step == 1:
            self.flight = (STAGES[Z1](self.held[0]),)
        elif self.step == 2:
            self.flight = (STAGES[X](self.held[0]), STAGES[Y](self.held[1]))
        else:
            self.flight = (STAGES[Y](self.held[0]), STAGES[X](self.held[1]))

    def finish(self):
        if self.native:
            return
        if self.step == 0:
            self.held = (join(self.held[0], self.flight[0], Z2, 1),)
        elif self.step == 1:
            both = join(self.held[0], self.flight[0], Z1, 2)
            self.held = (both[0], both[1])
        elif self.step == 2:
            left, right = self.held
            self.held = (join(left, self.flight[0], X, 2), join(right, self.flight[1], Y, 2))
        else:
            left, right = self.held
            self.held = (join(left, self.flight[0], Y, 3), join(right, self.flight[1], X, 2))
        self.flight = ()
        self.step += 1

    def result(self):
        if self.native:
            return tuple(lax.all_gather(self.held[0][k], ("chip", "tensor"), axis=0, tiled=True) for k in range(2))
        return tuple(part.reshape(16 * self.rows, self.width) for part in self.held)


class Reduce:
    def __init__(self, left, right):
        self.width = left.shape[1]
        self.native = lax.axis_size("chip") != 8
        self.held, self.flight = (left, right), ()
        self.step = 0
        if not self.native:
            self.held = tuple(part.reshape(2, 2, 2, 2, -1, self.width) for part in self.held)

    def start(self):
        if self.native:
            return
        if self.step == 0:
            plan = ((Y, 3), (X, 2))
        elif self.step == 1:
            plan = ((X, 2), (Y, 2))
        elif self.step == 2:
            plan = ((Z1, 2),)
        else:
            plan = ((Z2, 1),)
        self.keep, self.flight = [], []
        for part, (stage, axis) in zip(self.held, plan):
            bit = bits()[stage]
            self.keep.append(lax.dynamic_index_in_dim(part, bit, axis, keepdims=False))
            self.flight.append(STAGES[stage](lax.dynamic_index_in_dim(part, 1 - bit, axis, keepdims=False)))
        self.flight = tuple(self.flight)

    def finish(self):
        if self.native:
            return
        total = tuple(
            (mine.astype(jnp.float32) + other.astype(jnp.float32)).astype(jnp.bfloat16)
            for mine, other in zip(self.keep, self.flight)
        )
        self.held = (jnp.stack(total),) if self.step == 1 else total
        self.flight = ()
        self.step += 1

    def result(self):
        if self.native:
            both = jnp.stack(
                [lax.psum_scatter(p, ("chip", "tensor"), scatter_dimension=0, tiled=True) for p in self.held]
            )
        else:
            both = self.held[0]
        return swap(both)


def arrive(stream, *values):
    count = len(stream.flight)
    out = tie(*stream.flight, *values) if count + len(values) else ()
    stream.flight = out[:count]
    stream.finish()
    return out[count:]


def follow(stream, *values):
    out = tie(*stream.held, *values)
    count = len(stream.held)
    stream.held = out[:count]
    return out[count:]


def sum_all(values):
    if lax.axis_size("chip") != 8:
        return lax.psum(values, ("chip", "tensor"))
    for stage in (Y, X, Z1, Z2):
        values = values + STAGES[stage](values)
    return values


def halves(values, width):
    return (values[:, :width], values[:, width:])


def body(
    tokens,
    cotangent,
    segment_ids,
    w_qkv,
    m_qkv,
    a_qkv,
    w_bqv,
    m_bqv,
    a_bqv,
    w_out,
    m_out,
    a_out,
    w_up,
    m_up,
    a_up,
    w_bup,
    m_bup,
    a_bup,
    w_down,
    m_down,
    a_down,
    w_vec,
    m_vec,
    a_vec,
):
    f32, bf16 = jnp.float32, jnp.bfloat16
    core = lax.axis_index("core")
    dev_width = w_bqv.shape[1]
    unit_width = w_bup.shape[0]
    rows = tokens.shape[0]
    half = dev_width // 2
    unit_half = unit_width // 2
    sides = range(2)

    def full(values):
        return jnp.concatenate([values, core_exchange(values)])

    qkv_shard = w_qkv.astype(bf16)
    qkv_both = swap(
        jnp.stack([jnp.concatenate([qkv_shard[k, :, h * half : (h + 1) * half] for k in range(3)], 1) for h in sides])
    )
    tokens, qkv_order = tie(tokens, qkv_both)
    tokens = swap(tokens)
    out_shard, up_shard, down_shard = w_out.T.astype(bf16), w_up.astype(bf16), w_down.T.astype(bf16)
    rest = jnp.stack(
        [
            jnp.concatenate(
                [
                    out_shard[:, h * half : (h + 1) * half],
                    up_shard[:, h * unit_half : (h + 1) * unit_half],
                    down_shard[:, h * unit_half : (h + 1) * unit_half],
                ],
                1,
            )
            for h in sides
        ]
    )
    small = jnp.concatenate([w_bqv.reshape(-1), w_bup, segment_ids.reshape(-1).astype(f32)])

    qkv = Gather(qkv_order)
    qkv.start()
    tokens, rest, small = arrive(qkv, tokens, rest, small)
    qkv.start()
    rest, small = swap(rest), swap(small)
    tok_full = full(tokens)
    (rest, small, tok_full) = arrive(qkv, rest, small, tok_full)
    qkv.start()
    b_qv = small[: 2 * dev_width].reshape(2, dev_width)
    b_up = small[2 * dev_width : 2 * dev_width + unit_width]
    segments = small[2 * dev_width + unit_width :].astype(jnp.int32).reshape(1, -1)
    segments = jnp.where(core == 1, jnp.roll(segments, rows, axis=1), segments)
    seg_col = segments.reshape(-1, 1)
    upo = Gather(rest[:, :, : half + unit_half])
    down = Gather(rest[:, :, half + unit_half :])
    upo.start()
    arrive(qkv)
    qkv.start()
    (tok_full,) = arrive(upo, tok_full)
    upo.start()
    (tok_full,) = arrive(qkv, tok_full)
    (tok_full,) = arrive(upo, tok_full)
    upo.start()
    down.start()
    qkv_w = qkv.result()

    packed, context, logsum = [], [], []
    for h in sides:
        bias = jnp.concatenate(
            [b_qv[0, h * half : (h + 1) * half], jnp.zeros((half,), f32), b_qv[1, h * half : (h + 1) * half]]
        )
        packed.append((jnp.dot(tok_full, qkv_w[h], preferred_element_type=f32) + bias).astype(bf16))
    for h in sides:
        ctx, lse = attend_forward(packed[h], seg_col)
        context.append(ctx)
        logsum.append(lse)
        if h == 0:
            (packed[1],) = arrive(upo, packed[1])
            upo.start()
            (packed[1],) = arrive(down, packed[1])
            down.start()
    (context[1],) = arrive(upo, context[1])
    uo_w = upo.result()
    out_w = [part[:, :half] for part in uo_w]
    up_w = [part[:, half:] for part in uo_w]
    (context[1],) = arrive(down, context[1])
    down.start()
    cotangent, _ = tie(cotangent, context[1])

    def pair_dot(lefts, rights, form):
        return sum(jnp.einsum(form, left, right, preferred_element_type=f32) for left, right in zip(lefts, rights))

    def summed(lefts, rights, form):
        away = pair_dot([left[rows:] for left in lefts], rights, form)
        other = core_exchange(away.astype(bf16))
        return pair_dot([left[:rows] for left in lefts], rights, form) + other.astype(f32)

    attended = summed(context, out_w, "ne,de->nd")
    first_sum = tokens.astype(f32) + attended + w_vec[0]
    hidden, first_pull = jax.vjp(layer_norm, first_sum, w_vec[2], w_vec[3])
    hidden_full = full(hidden.astype(bf16))
    active16, gelu_pulls = [], []
    for h in sides:
        upper = jnp.dot(hidden_full, up_w[h], preferred_element_type=f32) + b_up[h * unit_half : (h + 1) * unit_half]
        active, pull = jax.vjp(gelu_exact, upper)
        active16.append(active.astype(bf16))
        gelu_pulls.append(pull)
        if h == 0:
            (hidden_full,) = arrive(down, hidden_full)
            down.start()
    (active16[1],) = arrive(down, active16[1])
    down_w = down.result()
    cotangent = swap(cotangent)
    mixed = summed(active16, down_w, "nf,df->nd")
    second_sum = hidden + mixed + w_vec[1]
    normed, second_pull = jax.vjp(layer_norm, second_sum, w_vec[4], w_vec[5])
    layer_out = normed.astype(bf16)
    second_grad, gain2_grad, shift2_grad = second_pull(cotangent.astype(f32))
    second_full = full(second_grad.astype(bf16))
    down_grads = [jnp.einsum("nd,nf->df", second_full, active16[h], preferred_element_type=f32).astype(bf16) for h in sides]
    (second_full, *down_grads) = tie(second_full, *down_grads)
    down_sum = Reduce(*down_grads)
    down_sum.start()
    upper_grads, upper16, up_grads = [], [], []
    for h in sides:
        active_grad = jnp.einsum("nd,df->nf", second_full, down_w[h], preferred_element_type=f32)
        upper_grads.append(gelu_pulls[h](active_grad)[0])
        upper16.append(upper_grads[h].astype(bf16))
    for h in sides:
        up_grads.append(jnp.einsum("nd,nf->df", hidden_full, upper16[h], preferred_element_type=f32).astype(bf16))
    (upper16[0], upper16[1], *up_grads) = arrive(down_sum, *upper16, *up_grads)
    down_sum.start()
    hidden_grad = second_grad + summed(upper16, up_w, "nf,df->nd")
    first_grad, gain1_grad, shift1_grad = first_pull(hidden_grad)
    first_full = full(first_grad.astype(bf16))
    out_grads = [jnp.einsum("nd,ne->de", first_full, context[h], preferred_element_type=f32).astype(bf16) for h in sides]
    (first_full, *out_grads) = arrive(down_sum, first_full, *out_grads)
    upo_sum = Reduce(*(jnp.concatenate([out_grads[h], up_grads[h]], 1) for h in sides))
    (first_full,) = follow(upo_sum, first_full)
    upo_sum.start()
    down_sum.start()
    context_grads = [
        jnp.einsum("nd,de->ne", first_full, out_w[h], preferred_element_type=f32).astype(bf16) for h in sides
    ]
    vec_local = jnp.stack(
        [
            jnp.sum(first_grad, axis=0),
            jnp.sum(second_grad, axis=0),
            gain1_grad,
            shift1_grad,
            gain2_grad,
            shift2_grad,
        ]
    )
    bup_local = jnp.concatenate([jnp.sum(part, axis=0) for part in upper_grads])
    packed16, bias_sums = [None, None], [None, None]
    packed16[0], bias_sums[0] = attend_backward(packed[0], context_grads[0], context[0], logsum[0], seg_col)
    (context_grads[1], packed16[0], vec_local, layer_out) = arrive(
        down_sum, context_grads[1], packed16[0], vec_local, layer_out
    )
    down_sum.start()
    vec_local = vec_local + core_exchange(vec_local)
    early = sum_all(jnp.concatenate([vec_local.reshape(-1), bup_local]))
    vec_grad = early[: vec_local.size].reshape(vec_local.shape)
    packed16[1], bias_sums[1] = attend_backward(packed[1], context_grads[1], context[1], logsum[1], seg_col)
    (packed16[1],) = arrive(upo_sum, packed16[1])
    upo_sum.start()
    (packed16[1], vec_grad) = arrive(down_sum, packed16[1], vec_grad)

    qkv_grads = [
        jnp.dot(tok_full.T, packed16[h], preferred_element_type=f32).astype(bf16) for h in sides
    ]
    layer_out, vec_grad, *qkv_grads = arrive(upo_sum, layer_out, vec_grad, *qkv_grads)
    qkv_sum = Reduce(*qkv_grads)
    qkv_sum.start()
    upo_sum.start()
    bup_grad = early[vec_local.size :]
    away = pair_dot([part[rows:] for part in packed16], qkv_w, "ne,de->nd")
    other = core_exchange(away.astype(bf16))
    near = pair_dot([part[:rows] for part in packed16], qkv_w, "ne,de->nd")
    grad_tokens = (first_grad + near + other.astype(f32)).astype(bf16)
    bqv_local = jnp.concatenate(bias_sums, 1)
    (grad_tokens,) = arrive(upo_sum, grad_tokens)
    upo_sum.start()
    (grad_tokens, bqv_local, bup_grad, layer_out) = arrive(qkv_sum, grad_tokens, bqv_local, bup_grad, layer_out)
    qkv_sum.start()
    layer_out = swap(layer_out)
    bqv_grad = sum_all(bqv_local)
    down_both = down_sum.result()
    (grad_tokens, bqv_grad) = arrive(upo_sum, grad_tokens, bqv_grad)
    arrive(qkv_sum)
    qkv_sum.start()
    grad_tokens = swap(grad_tokens)
    upo_both = upo_sum.result()
    arrive(qkv_sum)
    qkv_sum.start()
    tail = swap(jnp.concatenate([bqv_grad.reshape(-1), bup_grad]))
    bqv_grad = tail[: bqv_grad.size].reshape(bqv_grad.shape)
    bup_grad = tail[bqv_grad.size :]
    arrive(qkv_sum)
    qkv_both = qkv_sum.result().astype(f32)
    upo_both, down_both = upo_both.astype(f32), down_both.astype(f32)
    qkv_part = jnp.stack(
        [jnp.concatenate([qkv_both[h, :, k * half : (k + 1) * half] for h in sides], 1) for k in range(3)]
    )
    out_part = jnp.concatenate([upo_both[h, :, :half] for h in sides], 1).T
    up_part = jnp.concatenate([upo_both[h, :, half:] for h in sides], 1)
    down_part = jnp.concatenate([down_both[h] for h in sides], 1).T
    base_rate = 1.0 / math.sqrt(SEQ_LEN * lax.axis_size(("chip", "core")))
    slow_rate = MATRIX_RATE * base_rate
    fast_rate = FASTER_RATE * base_rate
    nm_qkv, nw_qkv, na_qkv = advance(w_qkv, m_qkv, a_qkv, qkv_part, slow_rate)
    nm_bqv, nw_bqv, na_bqv = advance(w_bqv, m_bqv, a_bqv, bqv_grad, slow_rate)
    nm_out, nw_out, na_out = advance(w_out, m_out, a_out, out_part, fast_rate)
    nm_up, nw_up, na_up = advance(w_up, m_up, a_up, up_part, slow_rate)
    nm_bup, nw_bup, na_bup = advance(w_bup, m_bup, a_bup, bup_grad, fast_rate)
    nm_down, nw_down, na_down = advance(w_down, m_down, a_down, down_part, slow_rate)
    nm_vec, nw_vec, na_vec = advance(w_vec, m_vec, a_vec, vec_grad, slow_rate)
    return (
        layer_out,
        grad_tokens,
        nm_qkv,
        nw_qkv,
        na_qkv,
        nm_bqv,
        nw_bqv,
        na_bqv,
        nm_out,
        nw_out,
        na_out,
        nm_up,
        nw_up,
        na_up,
        nm_bup,
        nw_bup,
        na_bup,
        nm_down,
        nw_down,
        na_down,
        nm_vec,
        nw_vec,
        na_vec,
    )


def solution(mesh):
    devices = mesh.devices.reshape(-1, 2, 2)
    split_mesh = Mesh(devices, ("chip", "core", "tensor"))
    dp = ("chip", "core")
    row = P(("chip", "core", "tensor"), None)
    deep = P(None, dp, "tensor")
    wide = P("tensor", dp)
    tall = P(dp, "tensor")
    qv = P(None, "tensor")
    unit = P("tensor")
    in_specs = (row, row, P(dp, None)) + (deep,) * 3 + (qv,) * 3 + (wide,) * 3 + (tall,) * 3 + (unit,) * 3 + (wide,) * 3 + (P(),) * 3
    out_specs = (row, row) + in_specs[3:]
    return jax.shard_map(body, mesh=split_mesh, in_specs=in_specs, out_specs=out_specs, check_vma=False)
```

time: 577 us -> 506 us (0.88)
  local copies, waits for them, and re-layouts: 54.1 us -> 27.2 us
  starting transfers between devices: 114 us -> 96.8 us
  other arithmetic: 60.2 us -> 43.7 us
    ppermute x30, waiting for transfers between devices: 136 us -> 108 us  [chip_exchange(): return lax.ppermute(values, 'chip', [(k, k ^ mask) for k in range(count)])]
    ppermute x14 -> x11, starting transfers between devices: 64.2 us -> 42.1 us  [swap(): return lax.ppermute(values, ('core', 'tensor'), SWAP)]
    ppermute x14, waiting for transfers between devices: 32.5 us -> 51.3 us  [y_exchange(): return lax.ppermute(values, 'tensor', FLIP)]
    slice x28 -> x8, local copies, waits for them, and re-layouts: 18.5 us -> 0.07 us  [the longest x1 0.02 us: body(): up_shard[:, h * unit_half:(h + 1) * unit_half]]
    select_n x27, other arithmetic: 19.4 us -> 6.55 us  [join(): jnp.where(first, jnp.stack([mine, other], axis), jnp.stack([other, mine],...]
    ppermute x30, starting transfers between devices: 23.7 us -> 32.4 us  [chip_exchange(): return lax.ppermute(values, 'chip', [(k, k ^ mask) for k in range(count)])]
    ppermute x9, starting transfers between devices: 18.5 us -> 10.1 us  [core_exchange(): return lax.ppermute(values, 'core', FLIP)]
    unnamed x174 -> x204, local copies, waits for them, and re-layouts: 21.3 us -> 14.3 us
  transfers between devices with their start and end apart: 67 -> 64, of which waited for: 32 -> 35; matrix products, arithmetic and copies ran while one was open for 27% -> 21% of each run, Pallas kernels for 8% -> 8%
where the time goes in v3:
time: 506 us; the launch traced here: 499 us
  waiting for transfers between devices  196 us (39%)
  starting transfers between devices  96.8 us (19%)
  matrix products  90.6 us (18%)
  other arithmetic  43.7 us (9%)
  Pallas kernels  41.5 us (8%)
  local copies, waits for them, and re-layouts  27.2 us (5%)
    ppermute x30, waiting for transfers between devices, chip_exchange(): return lax.ppermute(values, 'chip', [(k, k ^ mask) for k in range(count)])  108 us
    ppermute x14, waiting for transfers between devices, y_exchange(): return lax.ppermute(values, 'tensor', FLIP)  51.3 us
    ppermute x11, starting transfers between devices, swap(): return lax.ppermute(values, ('core', 'tensor'), SWAP)  42.1 us
    ppermute x30, starting transfers between devices, chip_exchange(): return lax.ppermute(values, 'chip', [(k, k ^ mask) for k in range(count)])  32.4 us
    ppermute x11, waiting for transfers between devices, swap(): return lax.ppermute(values, ('core', 'tensor'), SWAP)  32.1 us
    pallas_call x2, Pallas kernels, attend_backward(): pl.pallas_call(functools.partial(backward_kernel, block=block), grid=(pai...  27.4 us
    dot_general x2, matrix products, body(): jnp.dot(hidden_full, up_w[h], preferred_element_type=f32)  26.6 us
    dot_general x16, matrix products, pair_dot(): jnp.einsum(form, left, right, preferred_element_type=f32)  21.2 us
  transfers between devices with their start and end apart: 64, of which 35 were waited for; matrix products, arithmetic and copies ran while one was open for 21% of the time, Pallas kernels for 8%

profile of v3, /device:TPU:1, one launch (start us, length us, event | category | flops | bytes accessed | tf_op | source)
XLA Modules:
  0.0 499.3 jit_solution(11253115991939439056)
XLA Ops:
  1.9 4.7 collective-permute-start
  16.1 5.1 %collective-permute-done.1 = bf16[2,64,768]{2,1,0:T(8,128)(2,1)S(1)} collective-permute-done((bf16[2,64,768]{2,1,0:T(8,128)(2,1)S(1)}, bf16[2,64,768]{2,1,0:T(8,128)(2,1)S(1)}, u32[]{:S(2)}, u32[]{:S(2)}) %collective-permute-start.1) | collective-permute-done | bytes 196640 | tf_op jit(solution)/shard_map/ppermute | solution.py:204
  21.2 5.1 %collective-permute-done.2 = bf16[512,1024]{1,0:T(8,128)(2,1)S(1)} collective-permute-done((bf16[512,1024]{1,0:T(8,128)(2,1)S(1)}, bf16[512,1024]{1,0:T(8,128)(2,1)S(1)}, u32[]{:S(2)}, u32[]{:S(2)}) %collective-permute-start.2) | collective-permute-done | bytes 1048608 | tf_op jit(solution)/shard_map/ppermute | solution.py:191
  45.8 19.8 %collective-permute-done.8 = bf16[2,64,1280]{2,1,0:T(8,128)(2,1)} collective-permute-done((bf16[2,64,1280]{2,1,0:T(8,128)(2,1)}, bf16[2,64,1280]{2,1,0:T(8,128)(2,1)}, u32[]{:S(2)}, u32[]{:S(2)}) %collective-permute-start.8) | collective-permute-done | bytes 327712 | tf_op jit(solution)/shard_map/ppermute | solution.py:204
  72.0 15.5 %collective-permute-done.13 = bf16[2,2,2,64,768]{4,3,2,1,0:T(8,128)(2,1)S(1)} collective-permute-done((bf16[2,2,2,64,768]{4,3,2,1,0:T(8,128)(2,1)S(1)}, bf16[2,2,2,64,768]{4,3,2,1,0:T(8,128)(2,1)S(1)}, u32[]{:S(2)}, u32[]{:S(2)}) %collective-permute-start.13) | collective-permute-done | bytes 786464 | tf_op jit(solution)/shard_map/ppermute | solution.py:204
  93.8 7.1 %attend_forward.3 = (bf16[1024,256]{1,0:T(8,128)(2,1)S(1)}, f32[1024,256]{1,0:T(8,128)S(1)}) custom-call(bf16[1024,768]{1,0:T(8,128)(2,1)S(1)} %add_convert_fusion.q_ref.k_ref.v_ref, bf16[1024,768]{1,0:T(8,128)(2,1)S(1)} %add_convert_fusion.q_ref.k_ref.v_ref, bf16[1024,768]{1,0:T(8,128)(2,1)S(1)} %add_convert_fusion.q_ref.k_ref.v_ref, ...), custom_call_target="tpu_custom_call" | custom-call | tf_op jit(solution)/shard_map/attend_forward/pallas_call | solution.py:151
  108.3 6.9 %attend_forward.2 = (bf16[1024,256]{1,0:T(8,128)(2,1)S(1)}, f32[1024,256]{1,0:T(8,128)S(1)}) custom-call(bf16[1024,768]{1,0:T(8,128)(2,1)S(1)} %add_convert_fusion.1.q_ref.k_ref.v_ref, bf16[1024,768]{1,0:T(8,128)(2,1)S(1)} %add_convert_fusion.1.q_ref.k_ref.v_ref, bf16[1024,768]{1,0:T(8,128)(2,1)S(1)} %add_convert_fusion.1.q_ref.k_ref.v_ref, ...), custom_call_target="tpu_custom_call" | custom-call | tf_op jit(solution)/shard_map/attend_forward/pallas_call | solution.py:151
  115.3 16.9 %collective-permute-done.18 = bf16[2,2,2,64,1280]{4,3,1,0,2:T(8,128)(2,1)S(1)} collective-permute-done((bf16[2,2,2,64,1280]{4,3,1,0,2:T(8,128)(2,1)S(1)}, bf16[2,2,2,64,1280]{4,3,1,0,2:T(8,128)(2,1)S(1)}, u32[]{:S(2)}, u32[]{:S(2)}) %collective-permute-start.18) | collective-permute-done | bytes 1310752 | tf_op jit(solution)/shard_map/ppermute | solution.py:204
  146.9 10.3 %collective-permute-done.22 = bf16[2,2,64,1024]{3,2,1,0:T(8,128)(2,1)S(1)} collective-permute-done((bf16[2,2,64,1024]{3,2,1,0:T(8,128)(2,1)S(1)}, bf16[2,2,64,1024]{3,2,1,0:T(8,128)(2,1)S(1)}, u32[]{:S(2)}, u32[]{:S(2)}) %collective-permute-start.22) | collective-permute-done | bytes 524320 | tf_op jit(solution)/shard_map/ppermute | solution.py:204
  160.3 12.4 %multiply_convert_fusion = (bf16[1024,1024]{1,0:T(8,128)(2,1)S(1)}, f32[1024,1024]{1,0:T(8,128)}, f32[1024,1024]{1,0:T(8,128)}) fusion(f32[1024]{0:T(1024)S(1)} %get-tuple-element.320, bf16[1024,1024]{1,0:T(8,128)(2,1)S(1)} %pad_maximum_fusion.3, bf16[1024,1280]{1,0:T(8,128)(2,1)S(1)} %bitcast.337), kind=kOutput, calls=%fused_computation.6 | convolution fusion | flops 2216689664 | bytes 14684160 | tf_op jit(solution)/shard_map/dot_general | solution.py:471
  172.6 14.2 %multiply_convert_fusion.1 = (bf16[1024,1024]{1,0:T(8,128)(2,1)S(1)}, f32[1024,1024]{1,0:T(8,128)}, f32[1024,1024]{1,0:T(8,128)}) fusion(f32[1024]{0:T(1024)S(1)} %get-tuple-element.319, bf16[1024,1280]{1,0:T(8,128)(2,1)S(1)} %bitcast.343, bf16[512,1024]{1,0:T(8,128)(2,1)S(1)} %collective-permute-done.21, bf16[512,1024]{1,0:T(8,128)(2,1)S(1)} %fusion.20), kind=kOutput, calls=%fused_computation.19 | convolution fusion | flops 2220883968 | bytes 14684160 | tf_op jit(solution)/shard_map/dot_general | solution.py:471
  198.8 10.6 %collective-permute-done.19 = bf16[512,1024]{1,0:T(8,128)(2,1)S(1)} collective-permute-done((bf16[512,1024]{1,0:T(8,128)(2,1)S(1)}, bf16[512,1024]{1,0:T(8,128)(2,1)S(1)}, u32[]{:S(2)}, u32[]{:S(2)}) %collective-permute-start.19) | collective-permute-done | bytes 1048608 | tf_op jit(solution)/shard_map/ppermute | solution.py:191
  249.1 4.7 collective-permute-done.29
  279.5 5.1 %collective-permute-done.31 = bf16[2,2,64,1024]{3,2,0,1:T(8,128)(2,1)} collective-permute-done((bf16[2,2,64,1024]{3,2,0,1:T(8,128)(2,1)}, bf16[2,2,64,1024]{3,2,0,1:T(8,128)(2,1)}, u32[]{:S(2)}, u32[]{:S(2)}) %collective-permute-start.31) | collective-permute-done | bytes 524320 | tf_op jit(solution)/shard_map/ppermute | solution.py:199
  294.9 13.7 %attend_backward.2 = (bf16[1024,768]{1,0:T(8,128)(2,1)S(1)}, f32[2,256]{1,0:T(2,128)S(1)}) custom-call(bf16[1024,768]{1,0:T(8,128)(2,1)S(1)} %copy-done.3, bf16[1024,768]{1,0:T(8,128)(2,1)S(1)} %copy-done.3, bf16[1024,768]{1,0:T(8,128)(2,1)S(1)} %copy-done.3, bf16[1024,256]{1,0:T(8,128)(2,1)S(1)} %convolution_convert_fusion.6.g_ref, ...), custom_call_target="tpu_custom_call" | custom-call | tf_op jit(solution)/shard_map/attend_backward/pallas_call | solution.py:169
  316.5 28.3 %collective-permute-done.41 = f32[8192]{0:T(1024)S(1)} collective-permute-done((f32[8192]{0:T(1024)S(1)}, f32[8192]{0:T(1024)S(1)}, u32[]{:S(2)}, u32[]{:S(2)}) %collective-permute-start.41) | collective-permute-done | bytes 32800 | tf_op jit(solution)/shard_map/ppermute | solution.py:199
  355.6 13.7 %attend_backward.3 = (bf16[1024,768]{1,0:T(8,128)(2,1)S(1)}, f32[2,256]{1,0:T(2,128)S(1)}) custom-call(bf16[1024,768]{1,0:T(8,128)(2,1)S(1)} %copy-done.1, bf16[1024,768]{1,0:T(8,128)(2,1)S(1)} %copy-done.1, bf16[1024,768]{1,0:T(8,128)(2,1)S(1)} %copy-done.1, bf16[1024,256]{1,0:T(8,128)(2,1)S(1)} %convolution_convert_fusion.7.g_ref, ...), custom_call_target="tpu_custom_call" | custom-call | tf_op jit(solution)/shard_map/attend_backward/pallas_call | solution.py:169
  379.9 6.5 %collective-permute-start.63 = (bf16[2,64,1024]{2,1,0:T(8,128)(2,1)S(1)}, bf16[2,64,1024]{2,1,0:T(8,128)(2,1)S(1)}, u32[]{:S(2)}, u32[]{:S(2)}) collective-permute-start(bf16[2,64,1024]{2,1,0:T(8,128)(2,1)S(1)} %fusion.77), channel_id=1, source_target_pairs={{0,0},{1,2},{2,1},{3,3},{4,4},{5,6},{6,5},{7,7},{8,8},{9,10},{10,9... | collective-permute-start | bytes 786440 | tf_op jit(solution)/shard_map/ppermute | solution.py:191
  395.8 9.7 %collective-permute-done.38 = bf16[2,2,64,1280]{3,2,0,1:T(8,128)(2,1)S(1)} collective-permute-done((bf16[2,2,64,1280]{3,2,0,1:T(8,128)(2,1)S(1)}, bf16[2,2,64,1280]{3,2,0,1:T(8,128)(2,1)S(1)}, u32[]{:S(2)}, u32[]{:S(2)}) %collective-permute-start.38) | collective-permute-done | bytes 655392 | tf_op jit(solution)/shard_map/ppermute | solution.py:199
  414.1 9.0 %collective-permute-done.47 = bf16[2,2,64,1280]{3,2,0,1:T(8,128)(2,1)S(1)} collective-permute-done((bf16[2,2,64,1280]{3,2,0,1:T(8,128)(2,1)S(1)}, bf16[2,2,64,1280]{3,2,0,1:T(8,128)(2,1)S(1)}, u32[]{:S(2)}, u32[]{:S(2)}) %collective-permute-start.47) | collective-permute-done | bytes 655392 | tf_op jit(solution)/shard_map/ppermute | solution.py:204
  439.9 8.6 %collective-permute-start.49 = (bf16[512,1024]{1,0:T(8,128)(2,1)}, bf16[512,1024]{1,0:T(8,128)(2,1)S(1)}, u32[]{:S(2)}, u32[]{:S(2)}) collective-permute-start(bf16[512,1024]{1,0:T(8,128)(2,1)} %get-tuple-element.191), channel_id=1, source_target_pairs={{0,0},{1,2},{2,1},{3,3},{4,4},{5,6},{6,5},{7,7},{8,8},{9,10},{10,9... | collective-permute-start | bytes 3145736 | tf_op jit(solution)/shard_map/ppermute | solution.py:191
  454.9 6.4 %collective-permute-done.61 = f32[3072]{0:T(1024)S(1)} collective-permute-done((f32[3072]{0:T(1024)S(1)}, f32[3072]{0:T(1024)S(1)}, u32[]{:S(2)}, u32[]{:S(2)}) %collective-permute-start.61) | collective-permute-done | bytes 12320 | tf_op jit(solution)/shard_map/ppermute | solution.py:191
  471.0 5.4 %collective-permute-done.58 = bf16[2,2,64,768]{3,2,0,1:T(8,128)(2,1)S(1)} collective-permute-done((bf16[2,2,64,768]{3,2,0,1:T(8,128)(2,1)S(1)}, bf16[2,2,64,768]{3,2,0,1:T(8,128)(2,1)S(1)}, u32[]{:S(2)}, u32[]{:S(2)}) %collective-permute-start.58) | collective-permute-done | bytes 393248 | tf_op jit(solution)/shard_map/ppermute | solution.py:204
  476.8 10.6 %collective-permute-done.59 = bf16[2,64,768]{2,1,0:T(8,128)(2,1)S(1)} collective-permute-done((bf16[2,64,768]{2,1,0:T(8,128)(2,1)S(1)}, bf16[2,64,768]{2,1,0:T(8,128)(2,1)S(1)}, u32[]{:S(2)}, u32[]{:S(2)}) %collective-permute-start.59) | collective-permute-done | bytes 196640 | tf_op jit(solution)/shard_map/ppermute | solution.py:204
  (506 shorter events, 246.0 us)
Async XLA Ops:
  41.9 27.5 %collective-permute-start.10 = (bf16[2,2,64,768]{3,2,1,0:T(8,128)(2,1)}, bf16[2,2,64,768]{3,2,1,0:T(8,128)(2,1)S(1)}, u32[]{:S(2)}, u32[]{:S(2)}) collective-permute-start(bf16[2,2,64,768]{3,2,1,0:T(8,128)(2,1)} %get-tuple-element.272), channel_id=1, source_target_pairs={{0,4},{4,0},{8,12},{12,8},{16,20},{20,16},{24,28},{28,24},{1,5},{5... | collective-permute-start | bytes 1179656 | tf_op jit(solution)/shard_map/ppermute | solution.py:204
  43.1 26.3 %collective-permute-start.11 = (bf16[2,2,64,768]{3,2,1,0:T(8,128)(2,1)}, bf16[2,2,64,768]{3,2,1,0:T(8,128)(2,1)S(1)}, u32[]{:S(2)}, u32[]{:S(2)}) collective-permute-start(bf16[2,2,64,768]{3,2,1,0:T(8,128)(2,1)} %get-tuple-element.275), channel_id=1, source_target_pairs={{0,1},{1,0},{2,3},{3,2},{4,5},{5,4},{6,7},{7,6},{8,9},{9,8},{10,11... | collective-permute-start | bytes 1179656 | tf_op jit(solution)/shard_map/ppermute | solution.py:199
  43.1 22.5 %collective-permute-start.8 = (bf16[2,64,1280]{2,1,0:T(8,128)(2,1)}, bf16[2,64,1280]{2,1,0:T(8,128)(2,1)}, u32[]{:S(2)}, u32[]{:S(2)}) collective-permute-start(bf16[2,64,1280]{2,1,0:T(8,128)(2,1)} %get-tuple-element.290), channel_id=1, source_target_pairs={{0,16},{4,20},{8,24},{12,28},{16,0},{20,4},{24,8},{28,12},{1,17},{... | collective-permute-start | bytes 983048 | tf_op jit(solution)/shard_map/ppermute | solution.py:204
  45.7 58.9 %collective-permute-start.7 = (bf16[2,64,1024]{2,1,0:T(8,128)(2,1)}, bf16[2,64,1024]{2,1,0:T(8,128)(2,1)S(1)}, u32[]{:S(2)}, u32[]{:S(2)}) collective-permute-start(bf16[2,64,1024]{2,1,0:T(8,128)(2,1)} %get-tuple-element.287), channel_id=1, source_target_pairs={{0,16},{4,20},{8,24},{12,28},{16,0},{20,4},{24,8},{28,12},{1,17},{... | collective-permute-start | bytes 786440 | tf_op jit(solution)/shard_map/ppermute | solution.py:204
  66.8 21.4 %collective-permute-start.9 = (bf16[2,2,64,1280]{3,2,1,0:T(8,128)(2,1)S(1)}, bf16[2,2,64,1280]{3,2,1,0:T(8,128)(2,1)S(1)}, u32[]{:S(2)}, u32[]{:S(2)}) collective-permute-start(bf16[2,2,64,1280]{3,2,1,0:T(8,128)(2,1)S(1)} %maximum_select_fusion.19), channel_id=1, source_target_pairs={{0,8},{4,12},{8,0},{12,4},{16,24},{20,28},{24,16},{28,20},{1,9},{5... | collective-permute-start | bytes 1966088 | tf_op jit(solution)/shard_map/ppermute | solution.py:204
  104.8 27.4 %collective-permute-start.18 = (bf16[2,2,2,64,1280]{4,3,1,0,2:T(8,128)(2,1)S(1)}, bf16[2,2,2,64,1280]{4,3,1,0,2:T(8,128)(2,1)S(1)}, u32[]{:S(2)}, u32[]{:S(2)}) collective-permute-start(bf16[2,2,2,64,1280]{4,3,1,0,2:T(8,128)(2,1)S(1)} %maximum_select_fusion.8), channel_id=1, source_target_pairs={{0,4},{4,0},{8,12},{12,8},{16,20},{20,16},{24,28},{28,24},{1,5},{5... | collective-permute-start | bytes 3932168 | tf_op jit(solution)/shard_map/ppermute | solution.py:204
  105.3 27.2 %collective-permute-start.17 = (bf16[2,2,2,64,1280]{4,3,2,1,0:T(8,128)(2,1)S(1)}, bf16[2,2,2,64,1280]{4,3,2,1,0:T(8,128)(2,1)S(1)}, u32[]{:S(2)}, u32[]{:S(2)}) collective-permute-start(bf16[2,2,2,64,1280]{4,3,2,1,0:T(8,128)(2,1)S(1)} %maximum_select_fusion.7), channel_id=1, source_target_pairs={{0,1},{1,0},{2,3},{3,2},{4,5},{5,4},{6,7},{7,6},{8,9},{9,8},{10,11... | collective-permute-start | bytes 3932168 | tf_op jit(solution)/shard_map/ppermute | solution.py:199
  107.7 25.4 %collective-permute-start.16 = (bf16[2,2,64,1024]{3,2,0,1:T(8,128)(2,1)}, bf16[2,2,64,1024]{3,2,0,1:T(8,128)(2,1)S(1)}, u32[]{:S(2)}, u32[]{:S(2)}) collective-permute-start(bf16[2,2,64,1024]{3,2,0,1:T(8,128)(2,1)} %maximum_select_fusion.20), channel_id=1, source_target_pairs={{0,8},{4,12},{8,0},{12,4},{16,24},{20,28},{24,16},{28,20},{1,9},{5... | collective-permute-start | bytes 1572872 | tf_op jit(solution)/shard_map/ppermute | solution.py:204
  158.2 29.0 %collective-permute-start.25 = (bf16[2,2,2,64,1024]{4,3,1,0,2:T(8,128)(2,1)S(1)}, bf16[2,2,2,64,1024]{4,3,1,0,2:T(8,128)(2,1)S(1)}, u32[]{:S(2)}, u32[]{:S(2)}) collective-permute-start(bf16[2,2,2,64,1024]{4,3,1,0,2:T(8,128)(2,1)S(1)} %maximum_select_fusion.13), channel_id=1, source_target_pairs={{0,4},{4,0},{8,12},{12,8},{16,20},{20,16},{24,28},{28,24},{1,5},{5... | collective-permute-start | bytes 3145736 | tf_op jit(solution)/shard_map/ppermute | solution.py:204
  158.7 28.5 %collective-permute-start.24 = (bf16[2,2,2,64,1024]{4,3,1,0,2:T(8,128)(2,1)S(1)}, bf16[2,2,2,64,1024]{4,3,1,0,2:T(8,128)(2,1)S(1)}, u32[]{:S(2)}, u32[]{:S(2)}) collective-permute-start(bf16[2,2,2,64,1024]{4,3,1,0,2:T(8,128)(2,1)S(1)} %maximum_select_fusion.12), channel_id=1, source_target_pairs={{0,1},{1,0},{2,3},{3,2},{4,5},{5,4},{6,7},{7,6},{8,9},{9,8},{10,11... | collective-permute-start | bytes 3145736 | tf_op jit(solution)/shard_map/ppermute | solution.py:199
  229.1 24.6 %collective-permute-start.29 = (bf16[2,2,2,64,1024]{4,3,0,1,2:T(8,128)(2,1)S(1)}, bf16[2,2,2,64,1024]{4,3,0,1,2:T(8,128)(2,1)S(1)}, u32[]{:S(2)}, u32[]{:S(2)}) collective-permute-start(bf16[2,2,2,64,1024]{4,3,0,1,2:T(8,128)(2,1)S(1)} %bitcast.379), channel_id=1, source_target_pairs={{0,4},{4,0},{8,12},{12,8},{16,20},{20,16},{24,28},{28,24},{1,5},{5... | collective-permute-start | bytes 3145736 | tf_op jit(solution)/shard_map/ppermute | solution.py:204
  231.6 24.4 %collective-permute-start.28 = (bf16[2,2,2,64,1024]{4,3,0,1,2:T(8,128)(2,1)S(1)}, bf16[2,2,2,64,1024]{4,3,0,1,2:T(8,128)(2,1)S(1)}, u32[]{:S(2)}, u32[]{:S(2)}) collective-permute-start(bf16[2,2,2,64,1024]{4,3,0,1,2:T(8,128)(2,1)S(1)} %bitcast.380), channel_id=1, source_target_pairs={{0,1},{1,0},{2,3},{3,2},{4,5},{5,4},{6,7},{7,6},{8,9},{9,8},{10,11... | collective-permute-start | bytes 3145736 | tf_op jit(solution)/shard_map/ppermute | solution.py:199
  291.5 19.3 %collective-permute-start.36 = (bf16[2,2,64,1024]{3,2,0,1:T(8,128)(2,1)S(1)}, bf16[2,2,64,1024]{3,2,0,1:T(8,128)(2,1)S(1)}, u32[]{:S(2)}, u32[]{:S(2)}) collective-permute-start(bf16[2,2,64,1024]{3,2,0,1:T(8,128)(2,1)S(1)} %fusion.76), channel_id=1, source_target_pairs={{0,8},{4,12},{8,0},{12,4},{16,24},{20,28},{24,16},{28,20},{1,9},{5... | collective-permute-start | bytes 1572872 | tf_op jit(solution)/shard_map/ppermute | solution.py:204
  292.7 81.6 %collective-permute-start.35 = (bf16[2,2,2,64,1280]{4,3,0,1,2:T(8,128)(2,1)}, bf16[2,2,2,64,1280]{4,3,0,1,2:T(8,128)(2,1)}, u32[]{:S(2)}, u32[]{:S(2)}) collective-permute-start(bf16[2,2,2,64,1280]{4,3,0,1,2:T(8,128)(2,1)} %copy_bitcast_fusion), channel_id=1, source_target_pairs={{0,4},{4,0},{8,12},{12,8},{16,20},{20,16},{24,28},{28,24},{1,5},{5... | collective-permute-start | bytes 3932168 | tf_op jit(solution)/shard_map/ppermute | solution.py:204
  313.5 60.9 %collective-permute-start.34 = (bf16[2,2,2,64,1280]{4,3,0,1,2:T(8,128)(2,1)}, bf16[2,2,2,64,1280]{4,3,0,1,2:T(8,128)(2,1)}, u32[]{:S(2)}, u32[]{:S(2)}) collective-permute-start(bf16[2,2,2,64,1280]{4,3,0,1,2:T(8,128)(2,1)} %copy_bitcast_fusion.1), channel_id=1, source_target_pairs={{0,1},{1,0},{2,3},{3,2},{4,5},{5,4},{6,7},{7,6},{8,9},{9,8},{10,11... | collective-permute-start | bytes 3932168 | tf_op jit(solution)/shard_map/ppermute | solution.py:199
  315.0 29.8 %collective-permute-start.41 = (f32[8192]{0:T(1024)S(1)}, f32[8192]{0:T(1024)S(1)}, u32[]{:S(2)}, u32[]{:S(2)}) collective-permute-start(f32[8192]{0:T(1024)S(1)} %pad_maximum_fusion.18), channel_id=1, source_target_pairs={{0,1},{1,0},{2,3},{3,2},{4,5},{5,4},{6,7},{7,6},{8,9},{9,8},{10,11... | collective-permute-start | bytes 98312 | tf_op jit(solution)/shard_map/ppermute | solution.py:199
  346.0 28.4 %collective-permute-start.39 = (bf16[2,64,1024]{2,1,0:T(8,128)(2,1)S(1)}, bf16[2,64,1024]{2,1,0:T(8,128)(2,1)S(1)}, u32[]{:S(2)}, u32[]{:S(2)}) collective-permute-start(bf16[2,64,1024]{2,1,0:T(8,128)(2,1)S(1)} %dynamic-slice_bitcast_fusion.7), channel_id=1, source_target_pairs={{0,16},{4,20},{8,24},{12,28},{16,0},{20,4},{24,8},{28,12},{1,17},{... | collective-permute-start | bytes 786440 | tf_op jit(solution)/shard_map/ppermute | solution.py:204
  350.0 20.5 %collective-permute-start.43 = (f32[8192]{0:T(1024)S(1)}, f32[8192]{0:T(1024)S(1)}, u32[]{:S(2)}, u32[]{:S(2)}) collective-permute-start(f32[8192]{0:T(1024)S(1)} %add.402), channel_id=1, source_target_pairs={{0,8},{4,12},{8,0},{12,4},{16,24},{20,28},{24,16},{28,20},{1,9},{5... | collective-permute-start | bytes 98312 | tf_op jit(solution)/shard_map/ppermute | solution.py:204
  387.5 24.4 %collective-permute-start.48 = (bf16[512,1024]{1,0:T(8,128)(2,1)S(1)}, bf16[512,1024]{1,0:T(8,128)(2,1)S(1)}, u32[]{:S(2)}, u32[]{:S(2)}) collective-permute-start(bf16[512,1024]{1,0:T(8,128)(2,1)S(1)} %add_convert_fusion.3), channel_id=1, source_target_pairs={{0,2},{2,0},{1,3},{3,1},{4,6},{6,4},{5,7},{7,5},{8,10},{10,8},{9,1... | collective-permute-start | bytes 3145736 | tf_op jit(solution)/shard_map/ppermute | solution.py:195
  423.3 25.2 %collective-permute-start.50 = (bf16[2,64,1280]{2,1,0:T(8,128)(2,1)S(1)}, bf16[2,64,1280]{2,1,0:T(8,128)(2,1)S(1)}, u32[]{:S(2)}, u32[]{:S(2)}) collective-permute-start(bf16[2,64,1280]{2,1,0:T(8,128)(2,1)S(1)} %dynamic-slice_bitcast_fusion.6), channel_id=1, source_target_pairs={{0,16},{4,20},{8,24},{12,28},{16,0},{20,4},{24,8},{28,12},{1,17},{... | collective-permute-start | bytes 983048 | tf_op jit(solution)/shard_map/ppermute | solution.py:204
  431.0 35.2 %collective-permute-start.57 = (bf16[2,2,64,768]{3,2,0,1:T(8,128)(2,1)S(1)}, bf16[2,2,64,768]{3,2,0,1:T(8,128)(2,1)S(1)}, u32[]{:S(2)}, u32[]{:S(2)}) collective-permute-start(bf16[2,2,64,768]{3,2,0,1:T(8,128)(2,1)S(1)} %dynamic-slice_bitcast_fusion.4), channel_id=1, source_target_pairs={{0,1},{1,0},{2,3},{3,2},{4,5},{5,4},{6,7},{7,6},{8,9},{9,8},{10,11... | collective-permute-start | bytes 1179656 | tf_op jit(solution)/shard_map/ppermute | solution.py:199
  438.4 27.7 %collective-permute-start.56 = (bf16[2,2,64,768]{3,2,0,1:T(8,128)(2,1)}, bf16[2,2,64,768]{3,2,0,1:T(8,128)(2,1)}, u32[]{:S(2)}, u32[]{:S(2)}) collective-permute-start(bf16[2,2,64,768]{3,2,0,1:T(8,128)(2,1)} %dynamic-slice_bitcast_fusion.5), channel_id=1, source_target_pairs={{0,4},{4,0},{8,12},{12,8},{16,20},{20,16},{24,28},{28,24},{1,5},{5... | collective-permute-start | bytes 1179656 | tf_op jit(solution)/shard_map/ppermute | solution.py:204
  439.9 50.3 %collective-permute-start.49 = (bf16[512,1024]{1,0:T(8,128)(2,1)}, bf16[512,1024]{1,0:T(8,128)(2,1)S(1)}, u32[]{:S(2)}, u32[]{:S(2)}) collective-permute-start(bf16[512,1024]{1,0:T(8,128)(2,1)} %get-tuple-element.191), channel_id=1, source_target_pairs={{0,0},{1,2},{2,1},{3,3},{4,4},{5,6},{6,5},{7,7},{8,8},{9,10},{10,9... | collective-permute-start | bytes 3145736 | tf_op jit(solution)/shard_map/ppermute | solution.py:191
  461.3 34.5 %collective-permute-start.55 = (bf16[512,1024]{1,0:T(8,128)(2,1)}, bf16[512,1024]{1,0:T(8,128)(2,1)}, u32[]{:S(2)}, u32[]{:S(2)}) collective-permute-start(bf16[512,1024]{1,0:T(8,128)(2,1)} %add_convert_fusion.2), channel_id=1, source_target_pairs={{0,0},{1,2},{2,1},{3,3},{4,4},{5,6},{6,5},{7,7},{8,8},{9,10},{10,9... | collective-permute-start | bytes 3145736 | tf_op jit(solution)/shard_map/ppermute | solution.py:191
  (141 other events, 1366.3 us)

commit v4 on v3

--- a/solution.py
+++ b/solution.py
@@ -183,12 +183,16 @@
     )(packed, packed, packed, grad, context, lse, seg_col)
 
 
-SWAP = [(core * 2 + side, side * 2 + core) for core in range(2) for side in range(2)]
+CROSS = [(1, 2), (2, 1)]
 FLIP = [(0, 1), (1, 0)]
 
 
-def swap(values):
-    return lax.ppermute(values, ("core", "tensor"), SWAP)
+def cross(values):
+    return lax.ppermute(values, ("core", "tensor"), CROSS)
+
+
+def settle(mine, other):
+    return jnp.where(lax.axis_index("core") == lax.axis_index("tensor"), mine, other)
 
 
 def core_exchange(values):
@@ -218,22 +222,24 @@
 Y, X, Z1, Z2 = range(4)
 
 
-def tie(*values):
-    return lax.optimization_barrier(values)
-
-
 def join(mine, other, stage, axis):
     first = bits()[stage] == 0
     return jnp.where(first, jnp.stack([mine, other], axis), jnp.stack([other, mine], axis))
 
 
 class Gather:
-    def __init__(self, both):
-        self.rows, self.width = both.shape[1:]
+    def __init__(self, held, step=0):
+        self.rows, self.width = held[0].shape[-2:]
         self.native = lax.axis_size("chip") != 8
         self.flight = ()
-        self.held = (both,)
-        self.step = 0
+        self.held = held
+        self.step = step
+
+    def fork(self, width):
+        return (
+            Gather(tuple(part[..., :width] for part in self.held), self.step),
+            Gather(tuple(part[..., width:] for part in self.held), self.step),
+        )
 
     def start(self):
         if self.native:
@@ -315,34 +321,41 @@
             )
         else:
             both = self.held[0]
-        return swap(both)
-
-
-def arrive(stream, *values):
-    count = len(stream.flight)
-    out = tie(*stream.flight, *values) if count + len(values) else ()
-    stream.flight = out[:count]
-    stream.finish()
-    return out[count:]
-
-
-def follow(stream, *values):
-    out = tie(*stream.held, *values)
-    count = len(stream.held)
-    stream.held = out[:count]
-    return out[count:]
-
-
-def sum_all(values):
-    if lax.axis_size("chip") != 8:
-        return lax.psum(values, ("chip", "tensor"))
-    for stage in (Y, X, Z1, Z2):
-        values = values + STAGES[stage](values)
-    return values
-
-
-def halves(values, width):
-    return (values[:, :width], values[:, width:])
+        return both
+
+
+class Sum:
+    def __init__(self, values):
+        self.native = lax.axis_size("chip") != 8
+        if self.native:
+            values = lax.psum(values, ("chip", "tensor"))
+        self.held, self.flight, self.step = (values,), (), 0
+
+    def start(self):
+        if not self.native:
+            self.flight = (STAGES[(Z2, Z1, X, Y)[self.step]](self.held[0]),)
+
+    def finish(self):
+        if not self.native:
+            self.held = (self.held[0] + self.flight[0],)
+            self.flight = ()
+            self.step += 1
+
+
+class Order:
+    def __init__(self):
+        self.now = jnp.zeros((8, 128), jnp.float32)
+
+    def at(self, *values):
+        self.now, *values = lax.optimization_barrier((self.now, *values))
+        return values
+
+    def arrive(self, stream, *values):
+        count = len(stream.flight)
+        out = self.at(*stream.flight, *values)
+        stream.flight = tuple(out[:count])
+        stream.finish()
+        return out[count:]
 
 
 def body(
@@ -379,16 +392,25 @@
     half = dev_width // 2
     unit_half = unit_width // 2
     sides = range(2)
+    order = Order()
+
+    def pair_dot(lefts, rights, form):
+        return sum(jnp.einsum(form, left, right, preferred_element_type=f32) for left, right in zip(lefts, rights))
+
+    def summed(lefts, rights, form):
+        away = pair_dot([left[rows:] for left in lefts], rights, form)
+        other = core_exchange(away.astype(bf16))
+        return pair_dot([left[:rows] for left in lefts], rights, form) + other.astype(f32)
 
     def full(values):
         return jnp.concatenate([values, core_exchange(values)])
 
     qkv_shard = w_qkv.astype(bf16)
-    qkv_both = swap(
-        jnp.stack([jnp.concatenate([qkv_shard[k, :, h * half : (h + 1) * half] for k in range(3)], 1) for h in sides])
+    qkv_own = jnp.stack(
+        [jnp.concatenate([qkv_shard[k, :, h * half : (h + 1) * half] for k in range(3)], 1) for h in sides]
     )
-    tokens, qkv_order = tie(tokens, qkv_both)
-    tokens = swap(tokens)
+    qkv_own, tokens, cotangent = order.at(qkv_own, tokens, cotangent)
+    qkv_other = cross(qkv_own)
     out_shard, up_shard, down_shard = w_out.T.astype(bf16), w_up.astype(bf16), w_down.T.astype(bf16)
     rest = jnp.stack(
         [
@@ -404,31 +426,36 @@
         ]
     )
     small = jnp.concatenate([w_bqv.reshape(-1), w_bup, segment_ids.reshape(-1).astype(f32)])
-
-    qkv = Gather(qkv_order)
+    qkv_other, rest = order.at(qkv_other, rest)
+    qkv = Gather((settle(qkv_own, qkv_other),))
     qkv.start()
-    tokens, rest, small = arrive(qkv, tokens, rest, small)
+    rest_other = cross(rest)
+    (tokens, small) = order.arrive(qkv, tokens, small)
     qkv.start()
-    rest, small = swap(rest), swap(small)
-    tok_full = full(tokens)
-    (rest, small, tok_full) = arrive(qkv, rest, small, tok_full)
+    tok_other = cross(tokens)
+    (small,) = order.arrive(qkv, small)
     qkv.start()
+    small_other = cross(small)
+    (rest_other,) = order.at(rest_other)
+    wide = Gather((settle(rest, rest_other),))
+    wide.start()
+    order.arrive(qkv)
+    qkv.start()
+    (tok_other,) = order.at(tok_other)
+    tokens = settle(tokens, tok_other)
+    tok_far = core_exchange(tokens)
+    order.arrive(wide)
+    wide.start()
+    tok_far, small_other = order.at(tok_far, small_other)
+    small = settle(small, small_other)
     b_qv = small[: 2 * dev_width].reshape(2, dev_width)
     b_up = small[2 * dev_width : 2 * dev_width + unit_width]
     segments = small[2 * dev_width + unit_width :].astype(jnp.int32).reshape(1, -1)
     segments = jnp.where(core == 1, jnp.roll(segments, rows, axis=1), segments)
     seg_col = segments.reshape(-1, 1)
-    upo = Gather(rest[:, :, : half + unit_half])
-    down = Gather(rest[:, :, half + unit_half :])
-    upo.start()
-    arrive(qkv)
-    qkv.start()
-    (tok_full,) = arrive(upo, tok_full)
-    upo.start()
-    (tok_full,) = arrive(qkv, tok_full)
-    (tok_full,) = arrive(upo, tok_full)
-    upo.start()
-    down.start()
+    tok_full = jnp.concatenate([tokens, tok_far])
+    (tok_full, cotangent, seg_col) = order.arrive(qkv, tok_full, cotangent, seg_col)
+    cot_other = cross(cotangent)
     qkv_w = qkv.result()
 
     packed, context, logsum = [], [], []
@@ -442,27 +469,21 @@
         context.append(ctx)
         logsum.append(lse)
         if h == 0:
-            (packed[1],) = arrive(upo, packed[1])
+            (context[0], packed[1]) = order.arrive(wide, context[0], packed[1])
+            upo, down = wide.fork(half + unit_half)
             upo.start()
-            (packed[1],) = arrive(down, packed[1])
-            down.start()
-    (context[1],) = arrive(upo, context[1])
+    (cot_other, *context) = order.arrive(upo, cot_other, *context)
+    upo.start()
+    down.start()
+    cotangent = settle(cotangent, cot_other)
+    context = order.arrive(upo, *context)
     uo_w = upo.result()
     out_w = [part[:, :half] for part in uo_w]
     up_w = [part[:, half:] for part in uo_w]
-    (context[1],) = arrive(down, context[1])
+
+    attended = summed(context, out_w, "ne,de->nd")
+    (attended,) = order.arrive(down, attended)
     down.start()
-    cotangent, _ = tie(cotangent, context[1])
-
-    def pair_dot(lefts, rights, form):
-        return sum(jnp.einsum(form, left, right, preferred_element_type=f32) for left, right in zip(lefts, rights))
-
-    def summed(lefts, rights, form):
-        away = pair_dot([left[rows:] for left in lefts], rights, form)
-        other = core_exchange(away.astype(bf16))
-        return pair_dot([left[:rows] for left in lefts], rights, form) + other.astype(f32)
-
-    attended = summed(context, out_w, "ne,de->nd")
     first_sum = tokens.astype(f32) + attended + w_vec[0]
     hidden, first_pull = jax.vjp(layer_norm, first_sum, w_vec[2], w_vec[3])
     hidden_full = full(hidden.astype(bf16))
@@ -472,20 +493,19 @@
         active, pull = jax.vjp(gelu_exact, upper)
         active16.append(active.astype(bf16))
         gelu_pulls.append(pull)
-        if h == 0:
-            (hidden_full,) = arrive(down, hidden_full)
-            down.start()
-    (active16[1],) = arrive(down, active16[1])
+    active16 = order.arrive(down, *active16)
     down_w = down.result()
-    cotangent = swap(cotangent)
     mixed = summed(active16, down_w, "nf,df->nd")
     second_sum = hidden + mixed + w_vec[1]
     normed, second_pull = jax.vjp(layer_norm, second_sum, w_vec[4], w_vec[5])
     layer_out = normed.astype(bf16)
     second_grad, gain2_grad, shift2_grad = second_pull(cotangent.astype(f32))
-    second_full = full(second_grad.astype(bf16))
+    second_far = core_exchange(second_grad.astype(bf16))
+    (second_far, layer_out) = order.at(second_far, layer_out)
+    out_other = cross(layer_out)
+    second_full = jnp.concatenate([second_grad.astype(bf16), second_far])
     down_grads = [jnp.einsum("nd,nf->df", second_full, active16[h], preferred_element_type=f32).astype(bf16) for h in sides]
-    (second_full, *down_grads) = tie(second_full, *down_grads)
+    (second_full, *down_grads) = order.at(second_full, *down_grads)
     down_sum = Reduce(*down_grads)
     down_sum.start()
     upper_grads, upper16, up_grads = [], [], []
@@ -495,20 +515,28 @@
         upper16.append(upper_grads[h].astype(bf16))
     for h in sides:
         up_grads.append(jnp.einsum("nd,nf->df", hidden_full, upper16[h], preferred_element_type=f32).astype(bf16))
-    (upper16[0], upper16[1], *up_grads) = arrive(down_sum, *upper16, *up_grads)
+    (upper16[0], upper16[1], *up_grads) = order.arrive(down_sum, *upper16, *up_grads)
     down_sum.start()
     hidden_grad = second_grad + summed(upper16, up_w, "nf,df->nd")
     first_grad, gain1_grad, shift1_grad = first_pull(hidden_grad)
     first_full = full(first_grad.astype(bf16))
     out_grads = [jnp.einsum("nd,ne->de", first_full, context[h], preferred_element_type=f32).astype(bf16) for h in sides]
-    (first_full, *out_grads) = arrive(down_sum, first_full, *out_grads)
-    upo_sum = Reduce(*(jnp.concatenate([out_grads[h], up_grads[h]], 1) for h in sides))
-    (first_full,) = follow(upo_sum, first_full)
+    uo_grads = [jnp.concatenate([out_grads[h], up_grads[h]], 1) for h in sides]
+    (first_full, *uo_grads) = order.at(first_full, *uo_grads)
+    upo_sum = Reduce(*uo_grads)
     upo_sum.start()
-    down_sum.start()
     context_grads = [
         jnp.einsum("nd,de->ne", first_full, out_w[h], preferred_element_type=f32).astype(bf16) for h in sides
     ]
+    context_grads = order.arrive(down_sum, *context_grads)
+    down_sum.start()
+    packed16, bias_sums = [None, None], [None, None]
+    packed16[0], bias_sums[0] = attend_backward(packed[0], context_grads[0], context[0], logsum[0], seg_col)
+    (out_other, context_grads[1], packed16[0]) = order.arrive(down_sum, out_other, context_grads[1], packed16[0])
+    layer_out = settle(layer_out, out_other)
+    down_sum.start()
+    (context_grads[1], packed16[0]) = order.arrive(upo_sum, context_grads[1], packed16[0])
+    upo_sum.start()
     vec_local = jnp.stack(
         [
             jnp.sum(first_grad, axis=0),
@@ -520,53 +548,61 @@
         ]
     )
     bup_local = jnp.concatenate([jnp.sum(part, axis=0) for part in upper_grads])
-    packed16, bias_sums = [None, None], [None, None]
-    packed16[0], bias_sums[0] = attend_backward(packed[0], context_grads[0], context[0], logsum[0], seg_col)
-    (context_grads[1], packed16[0], vec_local, layer_out) = arrive(
-        down_sum, context_grads[1], packed16[0], vec_local, layer_out
-    )
-    down_sum.start()
-    vec_local = vec_local + core_exchange(vec_local)
-    early = sum_all(jnp.concatenate([vec_local.reshape(-1), bup_local]))
-    vec_grad = early[: vec_local.size].reshape(vec_local.shape)
+    vec_far = core_exchange(vec_local)
     packed16[1], bias_sums[1] = attend_backward(packed[1], context_grads[1], context[1], logsum[1], seg_col)
-    (packed16[1],) = arrive(upo_sum, packed16[1])
+    vec_far, *packed16 = order.at(vec_far, *packed16)
+    packed16 = order.arrive(down_sum, *packed16)
+    packed16 = order.arrive(upo_sum, *packed16)
     upo_sum.start()
-    (packed16[1], vec_grad) = arrive(down_sum, packed16[1], vec_grad)
-
-    qkv_grads = [
-        jnp.dot(tok_full.T, packed16[h], preferred_element_type=f32).astype(bf16) for h in sides
-    ]
-    layer_out, vec_grad, *qkv_grads = arrive(upo_sum, layer_out, vec_grad, *qkv_grads)
+    bqv_local = jnp.concatenate(bias_sums, 1)
+    totals = Sum(jnp.concatenate([(vec_local + vec_far).reshape(-1), bqv_local.reshape(-1), bup_local]))
+    totals.start()
+    down_own = down_sum.result()
+    down_other = cross(down_own)
+
+    qkv_grads = [jnp.einsum("nd,ne->de", tok_full, packed16[h], preferred_element_type=f32).astype(bf16) for h in sides]
+    (packed16[0], packed16[1], *qkv_grads) = order.arrive(totals, *packed16, *qkv_grads)
     qkv_sum = Reduce(*qkv_grads)
     qkv_sum.start()
+    totals.start()
+    away = pair_dot([part[rows:] for part in packed16], qkv_w, "ne,de->nd")
+    grad_far = core_exchange(away.astype(bf16))
+    near = pair_dot([part[:rows] for part in packed16], qkv_w, "ne,de->nd")
+    grad_tokens = (first_grad + near + grad_far.astype(f32)).astype(bf16)
+    (grad_tokens, down_other) = order.arrive(upo_sum, grad_tokens, down_other)
     upo_sum.start()
-    bup_grad = early[vec_local.size :]
-    away = pair_dot([part[rows:] for part in packed16], qkv_w, "ne,de->nd")
-    other = core_exchange(away.astype(bf16))
-    near = pair_dot([part[:rows] for part in packed16], qkv_w, "ne,de->nd")
-    grad_tokens = (first_grad + near + other.astype(f32)).astype(bf16)
-    bqv_local = jnp.concatenate(bias_sums, 1)
-    (grad_tokens,) = arrive(upo_sum, grad_tokens)
-    upo_sum.start()
-    (grad_tokens, bqv_local, bup_grad, layer_out) = arrive(qkv_sum, grad_tokens, bqv_local, bup_grad, layer_out)
+    order.arrive(totals)
+    totals.start()
+    order.arrive(totals)
+    (grad_tokens,) = order.arrive(qkv_sum, grad_tokens)
+    totals.start()
     qkv_sum.start()
-    layer_out = swap(layer_out)
-    bqv_grad = sum_all(bqv_local)
-    down_both = down_sum.result()
-    (grad_tokens, bqv_grad) = arrive(upo_sum, grad_tokens, bqv_grad)
-    arrive(qkv_sum)
+    order.arrive(upo_sum)
+    upo_own = upo_sum.result()
+    order.arrive(totals)
+    vectors = totals.held[0]
+    count = vec_local.size
+    vec_grad = vectors[:count].reshape(vec_local.shape)
+    tail = vectors[count:]
+    (upo_own, grad_tokens, tail) = order.arrive(qkv_sum, upo_own, grad_tokens, tail)
     qkv_sum.start()
-    grad_tokens = swap(grad_tokens)
-    upo_both = upo_sum.result()
-    arrive(qkv_sum)
+    tail_other = cross(tail)
+    upo_other = cross(upo_own)
+    grad_other = cross(grad_tokens)
+    order.arrive(qkv_sum)
     qkv_sum.start()
-    tail = swap(jnp.concatenate([bqv_grad.reshape(-1), bup_grad]))
-    bqv_grad = tail[: bqv_grad.size].reshape(bqv_grad.shape)
-    bup_grad = tail[bqv_grad.size :]
-    arrive(qkv_sum)
-    qkv_both = qkv_sum.result().astype(f32)
-    upo_both, down_both = upo_both.astype(f32), down_both.astype(f32)
+    (tail_other, upo_other, grad_other) = order.at(tail_other, upo_other, grad_other)
+    order.arrive(qkv_sum)
+    qkv_own = qkv_sum.result()
+    qkv_other = cross(qkv_own)
+    tail = settle(tail, tail_other)
+    bqv_grad = tail[: bqv_local.size].reshape(bqv_local.shape)
+    bup_grad = tail[bqv_local.size :]
+    grad_tokens = settle(grad_tokens, grad_other)
+    upo_both, down_both = settle(upo_own, upo_other).astype(f32), settle(down_own, down_other).astype(f32)
+    qkv_both = settle(qkv_own, qkv_other).astype(f32)
+    (vec_grad,) = order.at(vec_grad)
+    vec_grad = vec_grad + order.now[0, 0]
     qkv_part = jnp.stack(
         [jnp.concatenate([qkv_both[h, :, k * half : (k + 1) * half] for h in sides], 1) for k in range(3)]
     )

time: 506 us -> 453 us (0.90)
  waiting for transfers between devices: 196 us -> 147 us
  starting transfers between devices: 96.8 us -> 79.5 us
  other arithmetic: 43.7 us -> 59.5 us
    ppermute x14 -> x13, waiting for transfers between devices: 51.3 us -> 30.3 us  [y_exchange(): return lax.ppermute(values, 'tensor', FLIP)]
    ppermute x11, waiting for transfers between devices: 32.1 us -> 13.3 us  [cross(): return lax.ppermute(values, ('core', 'tensor'), CROSS)]
    ppermute x30 -> x25, waiting for transfers between devices: 108 us -> 97.9 us  [chip_exchange(): return lax.ppermute(values, 'chip', [(k, k ^ mask) for k in range(count)])]
    reduce_sum x0 -> x1, other arithmetic: none -> 7.3 us  [body(): bup_local = jnp.concatenate([jnp.sum(part, axis=0) for part in upper_grads])]
    ppermute x11, starting transfers between devices: 42.1 us -> 35.7 us  [cross(): return lax.ppermute(values, ('core', 'tensor'), CROSS)]
    select_n x27 -> x24, other arithmetic: 6.55 us -> 11.8 us  [join(): jnp.where(first, jnp.stack([mine, other], axis), jnp.stack([other, mine],...]
    ppermute x30 -> x25, starting transfers between devices: 32.4 us -> 28 us  [chip_exchange(): return lax.ppermute(values, 'chip', [(k, k ^ mask) for k in range(count)])]
    ppermute x14 -> x13, starting transfers between devices: 12.2 us -> 8.86 us  [y_exchange(): return lax.ppermute(values, 'tensor', FLIP)]
  transfers between devices with their start and end apart: 64 -> 58, of which waited for: 35 -> 29; matrix products, arithmetic and copies ran while one was open for 21% -> 28% of each run, Pallas kernels for 8% -> 9%
where the time goes in v4:
time: 453 us; the launch traced here: 447 us
  waiting for transfers between devices  147 us (32%)
  matrix products  89 us (20%)
  starting transfers between devices  79.5 us (18%)
  other arithmetic  59.5 us (13%)
  Pallas kernels  41.5 us (9%)
  local copies, waits for them, and re-layouts  27.9 us (6%)
    ppermute x25, waiting for transfers between devices, chip_exchange(): return lax.ppermute(values, 'chip', [(k, k ^ mask) for k in range(count)])  97.9 us
    ppermute x11, starting transfers between devices, cross(): return lax.ppermute(values, ('core', 'tensor'), CROSS)  35.7 us
    ppermute x13, waiting for transfers between devices, y_exchange(): return lax.ppermute(values, 'tensor', FLIP)  30.3 us
    ppermute x25, starting transfers between devices, chip_exchange(): return lax.ppermute(values, 'chip', [(k, k ^ mask) for k in range(count)])  28 us
    dot_general x2, matrix products, body(): jnp.dot(hidden_full, up_w[h], preferred_element_type=f32)  27.8 us
    pallas_call x2, Pallas kernels, attend_backward(): pl.pallas_call(functools.partial(backward_kernel, block=block), grid=(pai...  27.4 us
    dot_general x16, matrix products, pair_dot(): jnp.einsum(form, left, right, preferred_element_type=f32)  17.5 us
    pallas_call x2, Pallas kernels, attend_forward(): pl.pallas_call(functools.partial(forward_kernel, block=block), grid=(pair...  14 us
  transfers between devices with their start and end apart: 58, of which 29 were waited for; matrix products, arithmetic and copies ran while one was open for 28% of the time, Pallas kernels for 9%

profile of v4, /device:TPU:1, one launch (start us, length us, event | category | flops | bytes accessed | tf_op | source)
XLA Modules:
  0.0 447.3 jit_solution(5015395600636725911)
XLA Ops:
  1.9 4.5 %collective-permute-start = (bf16[2,64,768]{2,1,0:T(8,128)(2,1)S(1)}, bf16[2,64,768]{2,1,0:T(8,128)(2,1)S(1)}, u32[]{:S(2)}, u32[]{:S(2)}) collective-permute-start(bf16[2,64,768]{2,1,0:T(8,128)(2,1)S(1)} %pad_maximum_fusion.17), channel_id=1, source_target_pairs={{1,2},{2,1},{5,6},{6,5},{9,10},{10,9},{13,14},{14,13},{17,18},{18,... | collective-permute-start | bytes 589832 | tf_op jit(solution)/shard_map/ppermute | solution.py:191
  12.5 5.3 %collective-permute-done.1 = bf16[2,64,768]{2,1,0:T(8,128)(2,1)S(1)} collective-permute-done((bf16[2,64,768]{2,1,0:T(8,128)(2,1)S(1)}, bf16[2,64,768]{2,1,0:T(8,128)(2,1)S(1)}, u32[]{:S(2)}, u32[]{:S(2)}) %collective-permute-start.1) | collective-permute-done | bytes 196640 | tf_op jit(solution)/shard_map/ppermute | solution.py:208
  19.2 4.4 collective-permute-start.3
  27.7 4.7 %collective-permute-done.3 = bf16[2,64,2304]{2,1,0:T(8,128)(2,1)S(1)} collective-permute-done((bf16[2,64,2304]{2,1,0:T(8,128)(2,1)S(1)}, bf16[2,64,2304]{2,1,0:T(8,128)(2,1)S(1)}, u32[]{:S(2)}, u32[]{:S(2)}) %collective-permute-start.3) | collective-permute-done | bytes 589856 | tf_op jit(solution)/shard_map/ppermute | solution.py:191
  38.5 11.6 %collective-permute-done.5 = bf16[2,2,64,768]{3,2,1,0:T(8,128)(2,1)S(1)} collective-permute-done((bf16[2,2,64,768]{3,2,1,0:T(8,128)(2,1)S(1)}, bf16[2,2,64,768]{3,2,1,0:T(8,128)(2,1)S(1)}, u32[]{:S(2)}, u32[]{:S(2)}) %collective-permute-start.5) | collective-permute-done | bytes 393248 | tf_op jit(solution)/shard_map/ppermute | solution.py:203
  55.5 5.1 %collective-permute-done.7 = bf16[2,64,2304]{2,1,0:T(8,128)(2,1)S(1)} collective-permute-done((bf16[2,64,2304]{2,1,0:T(8,128)(2,1)S(1)}, bf16[2,64,2304]{2,1,0:T(8,128)(2,1)S(1)}, u32[]{:S(2)}, u32[]{:S(2)}) %collective-permute-start.7) | collective-permute-done | bytes 589856 | tf_op jit(solution)/shard_map/ppermute | solution.py:208
  72.7 4.4 collective-permute-start.15
  81.1 7.1 %attend_forward.2 = (bf16[1024,256]{1,0:T(8,128)(2,1)S(1)}, f32[1024,256]{1,0:T(8,128)S(1)}) custom-call(bf16[1024,768]{1,0:T(8,128)(2,1)S(1)} %add_convert_fusion.1.q_ref.k_ref.v_ref, bf16[1024,768]{1,0:T(8,128)(2,1)S(1)} %add_convert_fusion.1.q_ref.k_ref.v_ref, bf16[1024,768]{1,0:T(8,128)(2,1)S(1)} %add_convert_fusion.1.q_ref.k_ref.v_ref, ...), custom_call_target="tpu_custom_call" | custom-call | tf_op jit(solution)/shard_map/attend_forward/pallas_call | solution.py:151
  93.9 6.9 %attend_forward.3 = (bf16[1024,256]{1,0:T(8,128)(2,1)S(1)}, f32[1024,256]{1,0:T(8,128)S(1)}) custom-call(bf16[1024,768]{1,0:T(8,128)(2,1)S(1)} %add_convert_fusion.q_ref.k_ref.v_ref, bf16[1024,768]{1,0:T(8,128)(2,1)S(1)} %add_convert_fusion.q_ref.k_ref.v_ref, bf16[1024,768]{1,0:T(8,128)(2,1)S(1)} %add_convert_fusion.q_ref.k_ref.v_ref, ...), custom_call_target="tpu_custom_call" | custom-call | tf_op jit(solution)/shard_map/attend_forward/pallas_call | solution.py:151
  100.8 8.6 %collective-permute-done.13 = bf16[2,2,64,1280]{3,2,1,0:T(8,128)(2,1)S(1)} collective-permute-done((bf16[2,2,64,1280]{3,2,1,0:T(8,128)(2,1)S(1)}, bf16[2,2,64,1280]{3,2,1,0:T(8,128)(2,1)S(1)}, u32[]{:S(2)}, u32[]{:S(2)}) %collective-permute-start.13) | collective-permute-done | bytes 655392 | tf_op jit(solution)/shard_map/ppermute | solution.py:208
  113.0 28.1 %collective-permute-done.17 = bf16[2,2,2,64,1280]{4,3,1,0,2:T(8,128)(2,1)S(1)} collective-permute-done((bf16[2,2,2,64,1280]{4,3,1,0,2:T(8,128)(2,1)S(1)}, bf16[2,2,2,64,1280]{4,3,1,0,2:T(8,128)(2,1)S(1)}, u32[]{:S(2)}, u32[]{:S(2)}) %collective-permute-start.17) | collective-permute-done | bytes 1310752 | tf_op jit(solution)/shard_map/ppermute | solution.py:208
  149.4 11.2 %collective-permute-done.18 = bf16[2,2,64,1024]{3,2,1,0:T(8,128)(2,1)S(1)} collective-permute-done((bf16[2,2,64,1024]{3,2,1,0:T(8,128)(2,1)S(1)}, bf16[2,2,64,1024]{3,2,1,0:T(8,128)(2,1)S(1)}, u32[]{:S(2)}, u32[]{:S(2)}) %collective-permute-start.18) | collective-permute-done | bytes 524320 | tf_op jit(solution)/shard_map/ppermute | solution.py:208
  166.3 13.8 %multiply_convert_fusion = (bf16[1024,1024]{1,0:T(8,128)(2,1)S(1)}, f32[1024,1024]{1,0:T(8,128)}, f32[1024,1024]{1,0:T(8,128)}) fusion(f32[1024]{0:T(1024)S(1)} %get-tuple-element.436, bf16[1024,1280]{1,0:T(8,128)(2,1)S(1)} %bitcast.335, bf16[512,1024]{1,0:T(8,128)(2,1)S(1)} %collective-permute-done.23, bf16[512,1024]{1,0:T(8,128)(2,1)S(1)} %fusion.20), kind=kOutput, calls=%fused_computation.6 | convolution fusion | flops 2220883968 | bytes 14684160 | tf_op jit(solution)/shard_map/dot_general | solution.py:492
  180.1 13.9 %multiply_convert_fusion.1 = (bf16[1024,1024]{1,0:T(8,128)(2,1)S(1)}, f32[1024,1024]{1,0:T(8,128)}, f32[1024,1024]{1,0:T(8,128)}) fusion(f32[1024]{0:T(1024)S(1)} %get-tuple-element.437, bf16[1024,1280]{1,0:T(8,128)(2,1)S(1)} %bitcast.329, bf16[512,1024]{1,0:T(8,128)(2,1)S(1)} %collective-permute-done.23, bf16[512,1024]{1,0:T(8,128)(2,1)S(1)} %fusion.20), kind=kOutput, calls=%fused_computation.19 | convolution fusion | flops 2220883968 | bytes 14684160 | tf_op jit(solution)/shard_map/dot_general | solution.py:492
  211.2 4.4 convolution_convert_fusion.2
  234.1 7.3 %fusion.102 = (f32[1024]{0:T(1024)S(1)}, bf16[1024,1024]{1,0:T(8,128)(2,1)}, f32[1024]{0:T(1024)S(1)}, bf16[1024,1024]{1,0:T(8,128)(2,1)}) fusion(f32[1024,1024]{1,0:T(8,128)} %fusion.117, f32[1024,1024]{1,0:T(8,128)S(1)} %copy-done.39, f32[1024,1024]{1,0:T(8,128)S(1)} %copy-done.40, f32[1024]{0:T(1024)S(1)} %get-tuple-element.437, ...), kind=kLoop, calls=%fused_computation.353 | loop fusion | flops 33552384 | bytes 29376512 | tf_op jit(solution)/shard_map/reduce_sum | solution.py:550
  241.4 6.1 %convolution_convert_fusion = bf16[1024,1024]{1,0:T(8,128)(2,1)} fusion(bf16[1024,1024]{1,0:T(8,128)(2,1)} %get-tuple-element.238, bf16[512,1024]{1,0:T(8,128)(2,1)} %copy-done.96, bf16[512,1024]{1,0:T(8,128)(2,1)} %copy-done.69), kind=kOutput, calls=%fused_computation.79 | convolution fusion | flops 2152726528 | bytes 6291456 | tf_op jit(solution)/shard_map/nd,nf->df/dot_general | solution.py:517
  288.2 6.7 %collective-permute-done.31 = bf16[2,2,64,1024]{3,2,0,1:T(8,128)(2,1)S(1)} collective-permute-done((bf16[2,2,64,1024]{3,2,0,1:T(8,128)(2,1)S(1)}, bf16[2,2,64,1024]{3,2,0,1:T(8,128)(2,1)S(1)}, u32[]{:S(2)}, u32[]{:S(2)}) %collective-permute-start.31) | collective-permute-done | bytes 524320 | tf_op jit(solution)/shard_map/ppermute | solution.py:203
  308.7 13.7 %attend_backward.2 = (bf16[1024,768]{1,0:T(8,128)(2,1)S(1)}, f32[2,256]{1,0:T(2,128)S(1)}) custom-call(bf16[1024,768]{1,0:T(8,128)(2,1)S(1)} %copy-done.3, bf16[1024,768]{1,0:T(8,128)(2,1)S(1)} %copy-done.3, bf16[1024,768]{1,0:T(8,128)(2,1)S(1)} %copy-done.3, bf16[1024,256]{1,0:T(8,128)(2,1)S(1)} %copy-done.15, bf16[1024,256]{1,0:T(8,128)(2,1)S(1)} %copy-done.9, ...), custom_call_target="tpu_custom_call" | custom-call | tf_op jit(solution)/shard_map/attend_backward/pallas_call | solution.py:169
  341.4 13.7 %attend_backward.3 = (bf16[1024,768]{1,0:T(8,128)(2,1)S(1)}, f32[2,256]{1,0:T(2,128)S(1)}) custom-call(bf16[1024,768]{1,0:T(8,128)(2,1)S(1)} %copy-done.1, bf16[1024,768]{1,0:T(8,128)(2,1)S(1)} %copy-done.1, bf16[1024,768]{1,0:T(8,128)(2,1)S(1)} %copy-done.1, bf16[1024,256]{1,0:T(8,128)(2,1)S(1)} %copy-done.14, bf16[1024,256]{1,0:T(8,128)(2,1)S(1)} %copy-done.7, ...), custom_call_target="tpu_custom_call" | custom-call | tf_op jit(solution)/shard_map/attend_backward/pallas_call | solution.py:169
  380.6 9.8 %collective-permute-done.41 = bf16[2,2,64,1280]{3,2,0,1:T(8,128)(2,1)S(1)} collective-permute-done((bf16[2,2,64,1280]{3,2,0,1:T(8,128)(2,1)S(1)}, bf16[2,2,64,1280]{3,2,0,1:T(8,128)(2,1)S(1)}, u32[]{:S(2)}, u32[]{:S(2)}) %collective-permute-start.41) | collective-permute-done | bytes 655392 | tf_op jit(solution)/shard_map/ppermute | solution.py:208
  398.2 10.2 %collective-permute-done.48 = bf16[2,64,1280]{2,1,0:T(8,128)(2,1)S(1)} collective-permute-done((bf16[2,64,1280]{2,1,0:T(8,128)(2,1)S(1)}, bf16[2,64,1280]{2,1,0:T(8,128)(2,1)S(1)}, u32[]{:S(2)}, u32[]{:S(2)}) %collective-permute-start.48) | collective-permute-done | bytes 327712 | tf_op jit(solution)/shard_map/ppermute | solution.py:208
  423.2 5.3 %collective-permute-done.53 = f32[3072]{0:T(1024)S(1)} collective-permute-done((f32[3072]{0:T(1024)S(1)}, f32[3072]{0:T(1024)S(1)}, u32[]{:S(2)}, u32[]{:S(2)}) %collective-permute-start.53) | collective-permute-done | bytes 12320 | tf_op jit(solution)/shard_map/ppermute | solution.py:191
  428.8 6.3 %collective-permute-done.56 = bf16[2,64,768]{2,1,0:T(8,128)(2,1)S(1)} collective-permute-done((bf16[2,64,768]{2,1,0:T(8,128)(2,1)S(1)}, bf16[2,64,768]{2,1,0:T(8,128)(2,1)S(1)}, u32[]{:S(2)}, u32[]{:S(2)}) %collective-permute-start.56) | collective-permute-done | bytes 196640 | tf_op jit(solution)/shard_map/ppermute | solution.py:208
  (500 shorter events, 230.7 us)
Async XLA Ops:
  23.6 31.5 %collective-permute-start.6 = (bf16[512,1024]{1,0:T(8,128)(2,1)S(1)}, bf16[512,1024]{1,0:T(8,128)(2,1)S(1)}, u32[]{:S(2)}, u32[]{:S(2)}) collective-permute-start(bf16[512,1024]{1,0:T(8,128)(2,1)S(1)} %copy-done.67), channel_id=1, source_target_pairs={{1,2},{2,1},{5,6},{6,5},{9,10},{10,9},{13,14},{14,13},{17,18},{18,... | collective-permute-start | bytes 3145736 | tf_op jit(solution)/shard_map/ppermute | solution.py:191
  27.7 22.3 %collective-permute-start.5 = (bf16[2,2,64,768]{3,2,1,0:T(8,128)(2,1)S(1)}, bf16[2,2,64,768]{3,2,1,0:T(8,128)(2,1)S(1)}, u32[]{:S(2)}, u32[]{:S(2)}) collective-permute-start(bf16[2,2,64,768]{3,2,1,0:T(8,128)(2,1)S(1)} %get-tuple-element.400), channel_id=1, source_target_pairs={{0,1},{1,0},{2,3},{3,2},{4,5},{5,4},{6,7},{7,6},{8,9},{9,8},{10,11... | collective-permute-start | bytes 1179656 | tf_op jit(solution)/shard_map/ppermute | solution.py:203
  32.5 28.1 %collective-permute-start.7 = (bf16[2,64,2304]{2,1,0:T(8,128)(2,1)S(1)}, bf16[2,64,2304]{2,1,0:T(8,128)(2,1)S(1)}, u32[]{:S(2)}, u32[]{:S(2)}) collective-permute-start(bf16[2,64,2304]{2,1,0:T(8,128)(2,1)S(1)} %broadcast_select_fusion.4), channel_id=1, source_target_pairs={{0,16},{4,20},{8,24},{12,28},{16,0},{20,4},{24,8},{28,12},{1,17},{... | collective-permute-start | bytes 1769480 | tf_op jit(solution)/shard_map/ppermute | solution.py:208
  36.0 26.8 %collective-permute-start.9 = (f32[4096]{0:T(1024)S(1)}, f32[4096]{0:T(1024)S(1)}, u32[]{:S(2)}, u32[]{:S(2)}) collective-permute-start(f32[4096]{0:T(1024)S(1)} %pad_maximum_fusion.19), channel_id=1, source_target_pairs={{1,2},{2,1},{5,6},{6,5},{9,10},{10,9},{13,14},{14,13},{17,18},{18,... | collective-permute-start | bytes 49160 | tf_op jit(solution)/shard_map/ppermute | solution.py:191
  61.8 28.3 %collective-permute-start.12 = (bf16[2,2,64,2304]{3,2,1,0:T(8,128)(2,1)}, bf16[2,2,64,2304]{3,2,1,0:T(8,128)(2,1)}, u32[]{:S(2)}, u32[]{:S(2)}) collective-permute-start(bf16[2,2,64,2304]{3,2,1,0:T(8,128)(2,1)} %maximum_select_fusion.10), channel_id=1, source_target_pairs={{0,8},{4,12},{8,0},{12,4},{16,24},{20,28},{24,16},{28,20},{1,9},{5... | collective-permute-start | bytes 3538952 | tf_op jit(solution)/shard_map/ppermute | solution.py:208
  72.7 37.6 %collective-permute-start.15 = (bf16[512,1024]{1,0:T(8,128)(2,1)}, bf16[512,1024]{1,0:T(8,128)(2,1)S(1)}, u32[]{:S(2)}, u32[]{:S(2)}) collective-permute-start(bf16[512,1024]{1,0:T(8,128)(2,1)} %param.25), channel_id=1, source_target_pairs={{1,2},{2,1},{5,6},{6,5},{9,10},{10,9},{13,14},{14,13},{17,18},{18,... | collective-permute-start | bytes 3145736 | tf_op jit(solution)/shard_map/ppermute | solution.py:191
  111.5 29.7 %collective-permute-start.17 = (bf16[2,2,2,64,1280]{4,3,1,0,2:T(8,128)(2,1)S(1)}, bf16[2,2,2,64,1280]{4,3,1,0,2:T(8,128)(2,1)S(1)}, u32[]{:S(2)}, u32[]{:S(2)}) collective-permute-start(bf16[2,2,2,64,1280]{4,3,1,0,2:T(8,128)(2,1)S(1)} %maximum_select_fusion.8), channel_id=1, source_target_pairs={{0,4},{4,0},{8,12},{12,8},{16,20},{20,16},{24,28},{28,24},{1,5},{5... | collective-permute-start | bytes 3932168 | tf_op jit(solution)/shard_map/ppermute | solution.py:208
  112.3 29.1 %collective-permute-start.16 = (bf16[2,2,2,64,1280]{4,3,2,1,0:T(8,128)(2,1)S(1)}, bf16[2,2,2,64,1280]{4,3,2,1,0:T(8,128)(2,1)S(1)}, u32[]{:S(2)}, u32[]{:S(2)}) collective-permute-start(bf16[2,2,2,64,1280]{4,3,2,1,0:T(8,128)(2,1)S(1)} %maximum_select_fusion.7), channel_id=1, source_target_pairs={{0,1},{1,0},{2,3},{3,2},{4,5},{5,4},{6,7},{7,6},{8,9},{9,8},{10,11... | collective-permute-start | bytes 3932168 | tf_op jit(solution)/shard_map/ppermute | solution.py:203
  164.2 29.9 %collective-permute-start.22 = (bf16[2,2,2,64,1024]{4,3,1,0,2:T(8,128)(2,1)S(1)}, bf16[2,2,2,64,1024]{4,3,1,0,2:T(8,128)(2,1)S(1)}, u32[]{:S(2)}, u32[]{:S(2)}) collective-permute-start(bf16[2,2,2,64,1024]{4,3,1,0,2:T(8,128)(2,1)S(1)} %maximum_select_fusion.12), channel_id=1, source_target_pairs={{0,4},{4,0},{8,12},{12,8},{16,20},{20,16},{24,28},{28,24},{1,5},{5... | collective-permute-start | bytes 3145736 | tf_op jit(solution)/shard_map/ppermute | solution.py:208
  165.0 29.0 %collective-permute-start.21 = (bf16[2,2,2,64,1024]{4,3,1,0,2:T(8,128)(2,1)S(1)}, bf16[2,2,2,64,1024]{4,3,1,0,2:T(8,128)(2,1)S(1)}, u32[]{:S(2)}, u32[]{:S(2)}) collective-permute-start(bf16[2,2,2,64,1024]{4,3,1,0,2:T(8,128)(2,1)S(1)} %maximum_select_fusion.11), channel_id=1, source_target_pairs={{0,1},{1,0},{2,3},{3,2},{4,5},{5,4},{6,7},{7,6},{8,9},{9,8},{10,11... | collective-permute-start | bytes 3145736 | tf_op jit(solution)/shard_map/ppermute | solution.py:203
  229.5 24.7 %collective-permute-start.27 = (bf16[2,2,2,64,1024]{4,3,0,1,2:T(8,128)(2,1)}, bf16[2,2,2,64,1024]{4,3,0,1,2:T(8,128)(2,1)}, u32[]{:S(2)}, u32[]{:S(2)}) collective-permute-start(bf16[2,2,2,64,1024]{4,3,0,1,2:T(8,128)(2,1)} %bitcast.319), channel_id=1, source_target_pairs={{0,4},{4,0},{8,12},{12,8},{16,20},{20,16},{24,28},{28,24},{1,5},{5... | collective-permute-start | bytes 3145736 | tf_op jit(solution)/shard_map/ppermute | solution.py:208
  232.4 24.3 %collective-permute-start.26 = (bf16[2,2,2,64,1024]{4,3,0,1,2:T(8,128)(2,1)}, bf16[2,2,2,64,1024]{4,3,0,1,2:T(8,128)(2,1)S(1)}, u32[]{:S(2)}, u32[]{:S(2)}) collective-permute-start(bf16[2,2,2,64,1024]{4,3,0,1,2:T(8,128)(2,1)} %bitcast.320), channel_id=1, source_target_pairs={{0,1},{1,0},{2,3},{3,2},{4,5},{5,4},{6,7},{7,6},{8,9},{9,8},{10,11... | collective-permute-start | bytes 3145736 | tf_op jit(solution)/shard_map/ppermute | solution.py:203
  268.7 53.7 %collective-permute-start.33 = (bf16[512,1024]{1,0:T(8,128)(2,1)}, bf16[512,1024]{1,0:T(8,128)(2,1)}, u32[]{:S(2)}, u32[]{:S(2)}) collective-permute-start(bf16[512,1024]{1,0:T(8,128)(2,1)} %get-tuple-element.229), channel_id=1, source_target_pairs={{1,2},{2,1},{5,6},{6,5},{9,10},{10,9},{13,14},{14,13},{17,18},{18,... | collective-permute-start | bytes 3145736 | tf_op jit(solution)/shard_map/ppermute | solution.py:191
  274.0 20.9 %collective-permute-start.31 = (bf16[2,2,64,1024]{3,2,0,1:T(8,128)(2,1)S(1)}, bf16[2,2,64,1024]{3,2,0,1:T(8,128)(2,1)S(1)}, u32[]{:S(2)}, u32[]{:S(2)}) collective-permute-start(bf16[2,2,64,1024]{3,2,0,1:T(8,128)(2,1)S(1)} %dynamic-slice_bitcast_fusion.2), channel_id=1, source_target_pairs={{0,1},{1,0},{2,3},{3,2},{4,5},{5,4},{6,7},{7,6},{8,9},{9,8},{10,11... | collective-permute-start | bytes 1572872 | tf_op jit(solution)/shard_map/ppermute | solution.py:203
  274.6 20.3 %collective-permute-start.30 = (bf16[2,2,64,1024]{3,2,0,1:T(8,128)(2,1)S(1)}, bf16[2,2,64,1024]{3,2,0,1:T(8,128)(2,1)S(1)}, u32[]{:S(2)}, u32[]{:S(2)}) collective-permute-start(bf16[2,2,64,1024]{3,2,0,1:T(8,128)(2,1)S(1)} %dynamic-slice_bitcast_fusion.3), channel_id=1, source_target_pairs={{0,4},{4,0},{8,12},{12,8},{16,20},{20,16},{24,28},{28,24},{1,5},{5... | collective-permute-start | bytes 1572872 | tf_op jit(solution)/shard_map/ppermute | solution.py:208
  297.3 29.1 %collective-permute-start.35 = (bf16[2,2,2,64,1280]{4,3,0,1,2:T(8,128)(2,1)}, bf16[2,2,2,64,1280]{4,3,0,1,2:T(8,128)(2,1)}, u32[]{:S(2)}, u32[]{:S(2)}) collective-permute-start(bf16[2,2,2,64,1280]{4,3,0,1,2:T(8,128)(2,1)} %bitcast.317), channel_id=1, source_target_pairs={{0,4},{4,0},{8,12},{12,8},{16,20},{20,16},{24,28},{28,24},{1,5},{5... | collective-permute-start | bytes 3932168 | tf_op jit(solution)/shard_map/ppermute | solution.py:208
  300.5 30.1 %collective-permute-start.34 = (bf16[2,2,2,64,1280]{4,3,0,1,2:T(8,128)(2,1)}, bf16[2,2,2,64,1280]{4,3,0,1,2:T(8,128)(2,1)}, u32[]{:S(2)}, u32[]{:S(2)}) collective-permute-start(bf16[2,2,2,64,1280]{4,3,0,1,2:T(8,128)(2,1)} %bitcast.318), channel_id=1, source_target_pairs={{0,1},{1,0},{2,3},{3,2},{4,5},{5,4},{6,7},{7,6},{8,9},{9,8},{10,11... | collective-permute-start | bytes 3932168 | tf_op jit(solution)/shard_map/ppermute | solution.py:203
  306.0 49.2 %collective-permute-start.36 = (f32[6,1024]{1,0:T(8,128)S(1)}, f32[6,1024]{1,0:T(8,128)S(1)}, u32[]{:S(2)}, u32[]{:S(2)}) collective-permute-start(f32[6,1024]{1,0:T(8,128)S(1)} %stack.431), channel_id=1, source_target_pairs={{0,2},{2,0},{1,3},{3,1},{4,6},{6,4},{5,7},{7,5},{8,10},{10,8},{9,1... | collective-permute-start | bytes 73736 | tf_op jit(solution)/shard_map/ppermute | solution.py:199
  324.3 30.8 %collective-permute-start.37 = (bf16[2,64,1024]{2,1,0:T(8,128)(2,1)S(1)}, bf16[2,64,1024]{2,1,0:T(8,128)(2,1)S(1)}, u32[]{:S(2)}, u32[]{:S(2)}) collective-permute-start(bf16[2,64,1024]{2,1,0:T(8,128)(2,1)S(1)} %dynamic-slice_bitcast_fusion.7), channel_id=1, source_target_pairs={{0,16},{4,20},{8,24},{12,28},{16,0},{20,4},{24,8},{28,12},{1,17},{... | collective-permute-start | bytes 786440 | tf_op jit(solution)/shard_map/ppermute | solution.py:208
  333.3 30.0 %collective-permute-start.39 = (bf16[2,2,64,1280]{3,2,0,1:T(8,128)(2,1)}, bf16[2,2,64,1280]{3,2,0,1:T(8,128)(2,1)}, u32[]{:S(2)}, u32[]{:S(2)}) collective-permute-start(bf16[2,2,64,1280]{3,2,0,1:T(8,128)(2,1)} %dynamic-slice_bitcast_fusion), channel_id=1, source_target_pairs={{0,1},{1,0},{2,3},{3,2},{4,5},{5,4},{6,7},{7,6},{8,9},{9,8},{10,11... | collective-permute-start | bytes 1966088 | tf_op jit(solution)/shard_map/ppermute | solution.py:203
  338.1 25.2 %collective-permute-start.38 = (bf16[2,2,64,1280]{3,2,0,1:T(8,128)(2,1)}, bf16[2,2,64,1280]{3,2,0,1:T(8,128)(2,1)}, u32[]{:S(2)}, u32[]{:S(2)}) collective-permute-start(bf16[2,2,64,1280]{3,2,0,1:T(8,128)(2,1)} %dynamic-slice_bitcast_fusion.1), channel_id=1, source_target_pairs={{0,4},{4,0},{8,12},{12,8},{16,20},{20,16},{24,28},{28,24},{1,5},{5... | collective-permute-start | bytes 1966088 | tf_op jit(solution)/shard_map/ppermute | solution.py:208
  359.6 21.0 %collective-permute-start.43 = (bf16[2,64,1024]{2,1,0:T(8,128)(2,1)S(1)}, bf16[2,64,1024]{2,1,0:T(8,128)(2,1)S(1)}, u32[]{:S(2)}, u32[]{:S(2)}) collective-permute-start(bf16[2,64,1024]{2,1,0:T(8,128)(2,1)S(1)} %fusion.77), channel_id=1, source_target_pairs={{1,2},{2,1},{5,6},{6,5},{9,10},{10,9},{13,14},{14,13},{17,18},{18,... | collective-permute-start | bytes 786440 | tf_op jit(solution)/shard_map/ppermute | solution.py:191
  368.8 21.7 %collective-permute-start.44 = (f32[9216]{0:T(1024)S(1)}, f32[9216]{0:T(1024)S(1)}, u32[]{:S(2)}, u32[]{:S(2)}) collective-permute-start(f32[9216]{0:T(1024)S(1)} %fusion.101), channel_id=1, source_target_pairs={{0,8},{4,12},{8,0},{12,4},{16,24},{20,28},{24,16},{28,20},{1,9},{5... | collective-permute-start | bytes 110600 | tf_op jit(solution)/shard_map/ppermute | solution.py:208
  375.6 19.9 %collective-permute-start.47 = (bf16[2,2,2,64,768]{4,3,0,1,2:T(8,128)(2,1)S(1)}, bf16[2,2,2,64,768]{4,3,0,1,2:T(8,128)(2,1)S(1)}, u32[]{:S(2)}, u32[]{:S(2)}) collective-permute-start(bf16[2,2,2,64,768]{4,3,0,1,2:T(8,128)(2,1)S(1)} %bitcast.375), channel_id=1, source_target_pairs={{0,4},{4,0},{8,12},{12,8},{16,20},{20,16},{24,28},{28,24},{1,5},{5... | collective-permute-start | bytes 2359304 | tf_op jit(solution)/shard_map/ppermute | solution.py:208
  (135 other events, 1110.9 us)

commit v5 on v4

--- a/solution.py
+++ b/solution.py
@@ -191,6 +191,15 @@
     return lax.ppermute(values, ("core", "tensor"), CROSS)
 
 
+def cross_far(values):
+    pairs = []
+    for chip in range(lax.axis_size("chip")):
+        for core in range(2):
+            for side in range(2):
+                pairs.append((chip * 4 + core * 2 + side, (chip ^ 4) * 4 + side * 2 + core))
+    return lax.ppermute(values, ("chip", "core", "tensor"), pairs)
+
+
 def settle(mine, other):
     return jnp.where(lax.axis_index("core") == lax.axis_index("tensor"), mine, other)
 
@@ -228,7 +237,8 @@
 
 
 class Gather:
-    def __init__(self, held, step=0):
+    def __init__(self, held, step=0, mirrored=False):
+        self.mirrored = mirrored
         self.rows, self.width = held[0].shape[-2:]
         self.native = lax.axis_size("chip") != 8
         self.flight = ()
@@ -242,9 +252,12 @@
         )
 
     def start(self):
-        if self.native:
+        if self.mirrored:
+            far = () if self.native else (cross_far(self.held[0]),)
+            self.flight = (cross(self.held[0]),) + far
+        elif self.native:
             return
-        if self.step == 0:
+        elif self.step == 0:
             self.flight = (STAGES[Z2](self.held[0]),)
         elif self.step == 1:
             self.flight = (STAGES[Z1](self.held[0]),)
@@ -254,13 +267,15 @@
             self.flight = (STAGES[Y](self.held[0]), STAGES[X](self.held[1]))
 
     def finish(self):
+        if self.mirrored:
+            self.held = (settle(self.held[0], self.flight[0]),)
+            self.mirrored, self.flight = False, self.flight[1:]
         if self.native:
             return
         if self.step == 0:
             self.held = (join(self.held[0], self.flight[0], Z2, 1),)
         elif self.step == 1:
-            both = join(self.held[0], self.flight[0], Z1, 2)
-            self.held = (both[0], both[1])
+            self.held = tuple(join(self.held[0][h], self.flight[0][h], Z1, 1) for h in range(2))
         elif self.step == 2:
             left, right = self.held
             self.held = (join(left, self.flight[0], X, 2), join(right, self.flight[1], Y, 2))
@@ -278,7 +293,7 @@
 
 class Reduce:
     def __init__(self, left, right):
-        self.width = left.shape[1]
+        self.width = left.shape[-1]
         self.native = lax.axis_size("chip") != 8
         self.held, self.flight = (left, right), ()
         self.step = 0
@@ -293,18 +308,26 @@
         elif self.step == 1:
             plan = ((X, 2), (Y, 2))
         elif self.step == 2:
-            plan = ((Z1, 2),)
+            plan = ((Z1, self.held[0].ndim - 3),)
         else:
-            plan = ((Z2, 1),)
+            plan = ((Z2, self.held[0].ndim - 3),)
         self.keep, self.flight = [], []
         for part, (stage, axis) in zip(self.held, plan):
             bit = bits()[stage]
             self.keep.append(lax.dynamic_index_in_dim(part, bit, axis, keepdims=False))
-            self.flight.append(STAGES[stage](lax.dynamic_index_in_dim(part, 1 - bit, axis, keepdims=False)))
+            send = lax.dynamic_index_in_dim(part, 1 - bit, axis, keepdims=False)
+            if self.step < 3:
+                self.flight.append(STAGES[stage](send))
+        if self.step == 3:
+            self.flight = [cross_far(send), cross(self.keep[0])]
         self.flight = tuple(self.flight)
 
     def finish(self):
         if self.native:
+            return
+        if self.step == 3:
+            mine = settle(self.keep[0], self.flight[1])
+            self.held, self.flight = (mine.astype(jnp.float32) + self.flight[0].astype(jnp.float32),), ()
             return
         total = tuple(
             (mine.astype(jnp.float32) + other.astype(jnp.float32)).astype(jnp.bfloat16)
@@ -317,11 +340,13 @@
     def result(self):
         if self.native:
             both = jnp.stack(
-                [lax.psum_scatter(p, ("chip", "tensor"), scatter_dimension=0, tiled=True) for p in self.held]
+                [
+                    lax.psum_scatter(p, ("chip", "tensor"), scatter_dimension=p.ndim - 2, tiled=True)
+                    for p in self.held
+                ]
             )
-        else:
-            both = self.held[0]
-        return both
+            return settle(both, cross(both)).astype(jnp.float32)
+        return self.held[0]
 
 
 class Sum:
@@ -350,12 +375,21 @@
         self.now, *values = lax.optimization_barrier((self.now, *values))
         return values
 
-    def arrive(self, stream, *values):
-        count = len(stream.flight)
-        out = self.at(*stream.flight, *values)
-        stream.flight = tuple(out[:count])
-        stream.finish()
+    def follow(self, stream, *values):
+        count = len(stream.held)
+        out = self.at(*stream.held, *values)
+        stream.held = tuple(out[:count])
         return out[count:]
+
+    def arrive(self, streams, *values):
+        if not isinstance(streams, tuple):
+            streams = (streams,)
+        out = self.at(*(part for stream in streams for part in stream.flight), *values)
+        for stream in streams:
+            count = len(stream.flight)
+            stream.flight, out = tuple(out[:count]), out[count:]
+            stream.finish()
+        return out
 
 
 def body(
@@ -410,7 +444,8 @@
         [jnp.concatenate([qkv_shard[k, :, h * half : (h + 1) * half] for k in range(3)], 1) for h in sides]
     )
     qkv_own, tokens, cotangent = order.at(qkv_own, tokens, cotangent)
-    qkv_other = cross(qkv_own)
+    qkv = Gather((qkv_own,), mirrored=True)
+    qkv.start()
     out_shard, up_shard, down_shard = w_out.T.astype(bf16), w_up.astype(bf16), w_down.T.astype(bf16)
     rest = jnp.stack(
         [
@@ -426,26 +461,21 @@
         ]
     )
     small = jnp.concatenate([w_bqv.reshape(-1), w_bup, segment_ids.reshape(-1).astype(f32)])
-    qkv_other, rest = order.at(qkv_other, rest)
-    qkv = Gather((settle(qkv_own, qkv_other),))
-    qkv.start()
+    rest, tokens = order.at(rest, tokens)
     rest_other = cross(rest)
     (tokens, small) = order.arrive(qkv, tokens, small)
     qkv.start()
     tok_other = cross(tokens)
-    (small,) = order.arrive(qkv, small)
+    (rest_other, small) = order.arrive(qkv, rest_other, small)
     qkv.start()
     small_other = cross(small)
-    (rest_other,) = order.at(rest_other)
-    wide = Gather((settle(rest, rest_other),))
-    wide.start()
-    order.arrive(qkv)
+    upo, down = Gather((settle(rest, rest_other),)).fork(half + unit_half)
+    upo.start()
+    (tok_other,) = order.arrive((qkv, upo), tok_other)
     qkv.start()
-    (tok_other,) = order.at(tok_other)
+    upo.start()
     tokens = settle(tokens, tok_other)
     tok_far = core_exchange(tokens)
-    order.arrive(wide)
-    wide.start()
     tok_far, small_other = order.at(tok_far, small_other)
     small = settle(small, small_other)
     b_qv = small[: 2 * dev_width].reshape(2, dev_width)
@@ -454,7 +484,10 @@
     segments = jnp.where(core == 1, jnp.roll(segments, rows, axis=1), segments)
     seg_col = segments.reshape(-1, 1)
     tok_full = jnp.concatenate([tokens, tok_far])
-    (tok_full, cotangent, seg_col) = order.arrive(qkv, tok_full, cotangent, seg_col)
+    (tok_full, seg_col, cotangent, *down.held) = order.arrive((upo, qkv), tok_full, seg_col, cotangent, *down.held)
+    (tok_full,) = order.follow(upo, tok_full)
+    upo.start()
+    down.start()
     cot_other = cross(cotangent)
     qkv_w = qkv.result()
 
@@ -469,21 +502,22 @@
         context.append(ctx)
         logsum.append(lse)
         if h == 0:
-            (context[0], packed[1]) = order.arrive(wide, context[0], packed[1])
-            upo, down = wide.fork(half + unit_half)
+            (context[0], packed[1]) = order.arrive(upo, context[0], packed[1])
+            (packed[1],) = order.follow(upo, packed[1])
             upo.start()
-    (cot_other, *context) = order.arrive(upo, cot_other, *context)
-    upo.start()
+    (cot_other, *context) = order.arrive(down, cot_other, *context)
     down.start()
     cotangent = settle(cotangent, cot_other)
-    context = order.arrive(upo, *context)
+    order.arrive(down)
+    down.start()
+    context = order.arrive((upo, down), *context)
+    context = order.follow(down, *context)
+    down.start()
     uo_w = upo.result()
     out_w = [part[:, :half] for part in uo_w]
     up_w = [part[:, half:] for part in uo_w]
 
     attended = summed(context, out_w, "ne,de->nd")
-    (attended,) = order.arrive(down, attended)
-    down.start()
     first_sum = tokens.astype(f32) + attended + w_vec[0]
     hidden, first_pull = jax.vjp(layer_norm, first_sum, w_vec[2], w_vec[3])
     hidden_full = full(hidden.astype(bf16))
@@ -505,7 +539,7 @@
     out_other = cross(layer_out)
     second_full = jnp.concatenate([second_grad.astype(bf16), second_far])
     down_grads = [jnp.einsum("nd,nf->df", second_full, active16[h], preferred_element_type=f32).astype(bf16) for h in sides]
-    (second_full, *down_grads) = order.at(second_full, *down_grads)
+    (second_full, out_other, *down_grads) = order.at(second_full, out_other, *down_grads)
     down_sum = Reduce(*down_grads)
     down_sum.start()
     upper_grads, upper16, up_grads = [], [], []
@@ -532,7 +566,7 @@
     down_sum.start()
     packed16, bias_sums = [None, None], [None, None]
     packed16[0], bias_sums[0] = attend_backward(packed[0], context_grads[0], context[0], logsum[0], seg_col)
-    (out_other, context_grads[1], packed16[0]) = order.arrive(down_sum, out_other, context_grads[1], packed16[0])
+    (context_grads[1], packed16[0]) = order.arrive(down_sum, context_grads[1], packed16[0])
     layer_out = settle(layer_out, out_other)
     down_sum.start()
     (context_grads[1], packed16[0]) = order.arrive(upo_sum, context_grads[1], packed16[0])
@@ -550,57 +584,49 @@
     bup_local = jnp.concatenate([jnp.sum(part, axis=0) for part in upper_grads])
     vec_far = core_exchange(vec_local)
     packed16[1], bias_sums[1] = attend_backward(packed[1], context_grads[1], context[1], logsum[1], seg_col)
-    vec_far, *packed16 = order.at(vec_far, *packed16)
-    packed16 = order.arrive(down_sum, *packed16)
-    packed16 = order.arrive(upo_sum, *packed16)
+    qkv_grads = [jnp.einsum("nd,ne->de", tok_full, packed16[h], preferred_element_type=f32).astype(bf16) for h in sides]
+    out = order.arrive((down_sum, upo_sum), vec_far, *packed16, *qkv_grads)
+    vec_far, packed16, qkv_grads = out[0], out[1:3], out[3:]
+    qkv_sum = Reduce(*qkv_grads)
+    qkv_sum.start()
+    packed16 = order.follow(upo_sum, *packed16)
     upo_sum.start()
     bqv_local = jnp.concatenate(bias_sums, 1)
     totals = Sum(jnp.concatenate([(vec_local + vec_far).reshape(-1), bqv_local.reshape(-1), bup_local]))
     totals.start()
-    down_own = down_sum.result()
-    down_other = cross(down_own)
-
-    qkv_grads = [jnp.einsum("nd,ne->de", tok_full, packed16[h], preferred_element_type=f32).astype(bf16) for h in sides]
-    (packed16[0], packed16[1], *qkv_grads) = order.arrive(totals, *packed16, *qkv_grads)
-    qkv_sum = Reduce(*qkv_grads)
-    qkv_sum.start()
-    totals.start()
+    down_both = down_sum.result()
     away = pair_dot([part[rows:] for part in packed16], qkv_w, "ne,de->nd")
     grad_far = core_exchange(away.astype(bf16))
+    packed16 = order.arrive((upo_sum, totals), *packed16)
+    upo_sum.start()
+    totals.start()
     near = pair_dot([part[:rows] for part in packed16], qkv_w, "ne,de->nd")
     grad_tokens = (first_grad + near + grad_far.astype(f32)).astype(bf16)
-    (grad_tokens, down_other) = order.arrive(upo_sum, grad_tokens, down_other)
-    upo_sum.start()
-    order.arrive(totals)
+    (grad_tokens, down_both) = order.arrive(totals, grad_tokens, down_both)
     totals.start()
-    order.arrive(totals)
-    (grad_tokens,) = order.arrive(qkv_sum, grad_tokens)
+    order.arrive(qkv_sum)
+    qkv_sum.start()
+    order.arrive((upo_sum, totals))
     totals.start()
+    upo_both = upo_sum.result()
+    (upo_both, grad_tokens) = order.arrive(qkv_sum, upo_both, grad_tokens)
     qkv_sum.start()
-    order.arrive(upo_sum)
-    upo_own = upo_sum.result()
+    grad_other = cross(grad_tokens)
     order.arrive(totals)
     vectors = totals.held[0]
     count = vec_local.size
     vec_grad = vectors[:count].reshape(vec_local.shape)
     tail = vectors[count:]
-    (upo_own, grad_tokens, tail) = order.arrive(qkv_sum, upo_own, grad_tokens, tail)
-    qkv_sum.start()
     tail_other = cross(tail)
-    upo_other = cross(upo_own)
-    grad_other = cross(grad_tokens)
     order.arrive(qkv_sum)
     qkv_sum.start()
-    (tail_other, upo_other, grad_other) = order.at(tail_other, upo_other, grad_other)
+    (tail_other, grad_other) = order.at(tail_other, grad_other)
     order.arrive(qkv_sum)
-    qkv_own = qkv_sum.result()
-    qkv_other = cross(qkv_own)
+    qkv_both = qkv_sum.result()
     tail = settle(tail, tail_other)
     bqv_grad = tail[: bqv_local.size].reshape(bqv_local.shape)
     bup_grad = tail[bqv_local.size :]
     grad_tokens = settle(grad_tokens, grad_other)
-    upo_both, down_both = settle(upo_own, upo_other).astype(f32), settle(down_own, down_other).astype(f32)
-    qkv_both = settle(qkv_own, qkv_other).astype(f32)
     (vec_grad,) = order.at(vec_grad)
     vec_grad = vec_grad + order.now[0, 0]
     qkv_part = jnp.stack(

time: 453 us -> 424 us (0.936)
  waiting for transfers between devices: 147 us -> 117 us
  starting transfers between devices: 79.5 us -> 90.6 us
  other arithmetic: 59.5 us -> 51.2 us
    ppermute x25 -> x23, waiting for transfers between devices: 97.9 us -> 49.1 us  [chip_exchange(): return lax.ppermute(values, 'chip', [(k, k ^ mask) for k in range(count)])]
    ppermute x0 -> x4, starting transfers between devices: none -> 15.3 us  [cross_far(): return lax.ppermute(values, ('chip', 'core', 'tensor'), pairs)]
    ppermute x13, waiting for transfers between devices: 30.3 us -> 41.3 us  [y_exchange(): return lax.ppermute(values, 'tensor', FLIP)]
    ppermute x25 -> x23, starting transfers between devices: 28 us -> 19.3 us  [chip_exchange(): return lax.ppermute(values, 'chip', [(k, k ^ mask) for k in range(count)])]
    reduce_sum x1 -> x0, other arithmetic: 7.3 us -> none  [body(): bup_local = jnp.concatenate([jnp.sum(part, axis=0) for part in upper_grads])]
    unnamed x204 -> x222, local copies, waits for them, and re-layouts: 11.7 us -> 14.4 us
    convert_element_type x12 -> x9, other arithmetic: 9.15 us -> 8.14 us  [finish(): (mine.astype(jnp.float32) + other.astype(jnp.float32)).astype(jnp.bfloat16)]
    select_n x24 -> x26, other arithmetic: 11.8 us -> 11.3 us  [join(): jnp.where(first, jnp.stack([mine, other], axis), jnp.stack([other, mine],...]
  transfers between devices with their start and end apart: 58 -> 60, of which waited for: 29 -> 24; matrix products, arithmetic and copies ran while one was open for 28% -> 28% of each run, Pallas kernels for 9% -> 10%
where the time goes in v5:
time: 424 us; the launch traced here: 418 us
  waiting for transfers between devices  117 us (28%)
  starting transfers between devices  90.6 us (21%)
  matrix products  90 us (21%)
  other arithmetic  51.2 us (12%)
  Pallas kernels  41.4 us (10%)
  local copies, waits for them, and re-layouts  24.4 us (6%)
    ppermute x23, waiting for transfers between devices, chip_exchange(): return lax.ppermute(values, 'chip', [(k, k ^ mask) for k in range(count)])  49.1 us
    ppermute x13, waiting for transfers between devices, y_exchange(): return lax.ppermute(values, 'tensor', FLIP)  41.3 us
    ppermute x11, starting transfers between devices, cross(): return lax.ppermute(values, ('core', 'tensor'), CROSS)  38.1 us
    dot_general x2, matrix products, body(): jnp.dot(hidden_full, up_w[h], preferred_element_type=f32)  28.3 us
    pallas_call x2, Pallas kernels, attend_backward(): pl.pallas_call(functools.partial(backward_kernel, block=block), grid=(pai...  27.3 us
    ppermute x23, starting transfers between devices, chip_exchange(): return lax.ppermute(values, 'chip', [(k, k ^ mask) for k in range(count)])  19.3 us
    dot_general x16, matrix products, pair_dot(): jnp.einsum(form, left, right, preferred_element_type=f32)  18.1 us
    ppermute x11, waiting for transfers between devices, cross(): return lax.ppermute(values, ('core', 'tensor'), CROSS)  16 us
  transfers between devices with their start and end apart: 60, of which 24 were waited for; matrix products, arithmetic and copies ran while one was open for 28% of the time, Pallas kernels for 10%

profile of v5, /device:TPU:1, one launch (start us, length us, event | category | flops | bytes accessed | tf_op | source)
XLA Modules:
  0.0 418.2 jit_solution(4327511452203011480)
XLA Ops:
  1.9 4.5 %collective-permute-start = (bf16[2,64,768]{2,1,0:T(8,128)(2,1)S(1)}, bf16[2,64,768]{2,1,0:T(8,128)(2,1)S(1)}, u32[]{:S(2)}, u32[]{:S(2)}) collective-permute-start(bf16[2,64,768]{2,1,0:T(8,128)(2,1)S(1)} %pad_maximum_fusion.15), channel_id=1, source_target_pairs={{1,2},{2,1},{5,6},{6,5},{9,10},{10,9},{13,14},{14,13},{17,18},{18,... | collective-permute-start | bytes 589832 | tf_op jit(solution)/shard_map/ppermute | solution.py:191
  20.0 7.1 %collective-permute-done.2 = bf16[2,2,64,768]{3,2,1,0:T(8,128)(2,1)S(1)} collective-permute-done((bf16[2,2,64,768]{3,2,1,0:T(8,128)(2,1)S(1)}, bf16[2,2,64,768]{3,2,1,0:T(8,128)(2,1)S(1)}, u32[]{:S(2)}, u32[]{:S(2)}) %collective-permute-start.2) | collective-permute-done | bytes 393248 | tf_op jit(solution)/shard_map/ppermute | solution.py:217
  30.5 5.3 %collective-permute-start.9 = (f32[4096]{0:T(1024)S(1)}, f32[4096]{0:T(1024)S(1)}, u32[]{:S(2)}, u32[]{:S(2)}) collective-permute-start(f32[4096]{0:T(1024)S(1)} %pad_maximum_fusion.17), channel_id=1, source_target_pairs={{1,2},{2,1},{5,6},{6,5},{9,10},{10,9},{13,14},{14,13},{17,18},{18,... | collective-permute-start | bytes 49160 | tf_op jit(solution)/shard_map/ppermute | solution.py:191
  36.0 10.8 %collective-permute-done.6 = bf16[2,64,1280]{2,1,0:T(8,128)(2,1)S(1)} collective-permute-done((bf16[2,64,1280]{2,1,0:T(8,128)(2,1)S(1)}, bf16[2,64,1280]{2,1,0:T(8,128)(2,1)S(1)}, u32[]{:S(2)}, u32[]{:S(2)}) %collective-permute-start.6) | collective-permute-done | bytes 327712 | tf_op jit(solution)/shard_map/ppermute | solution.py:217
  53.2 12.5 %collective-permute-done.10 = bf16[2,2,64,1280]{3,2,1,0:T(8,128)(2,1)S(1)} collective-permute-done((bf16[2,2,64,1280]{3,2,1,0:T(8,128)(2,1)S(1)}, bf16[2,2,64,1280]{3,2,1,0:T(8,128)(2,1)S(1)}, u32[]{:S(2)}, u32[]{:S(2)}) %collective-permute-start.10) | collective-permute-done | bytes 655392 | tf_op jit(solution)/shard_map/ppermute | solution.py:217
  74.5 4.5 %collective-permute-start.16 = (bf16[512,1024]{1,0:T(8,128)(2,1)}, bf16[512,1024]{1,0:T(8,128)(2,1)}, u32[]{:S(2)}, u32[]{:S(2)}) collective-permute-start(bf16[512,1024]{1,0:T(8,128)(2,1)} %param.25), channel_id=1, source_target_pairs={{1,2},{2,1},{5,6},{6,5},{9,10},{10,9},{13,14},{14,13},{17,18},{18,... | collective-permute-start | bytes 3145736 | tf_op jit(solution)/shard_map/ppermute | solution.py:191
  82.6 7.1 %attend_forward.2 = (bf16[1024,256]{1,0:T(8,128)(2,1)S(1)}, f32[1024,256]{1,0:T(8,128)S(1)}) custom-call(bf16[1024,768]{1,0:T(8,128)(2,1)S(1)} %add_convert_fusion.1.q_ref.k_ref.v_ref, bf16[1024,768]{1,0:T(8,128)(2,1)S(1)} %add_convert_fusion.1.q_ref.k_ref.v_ref, bf16[1024,768]{1,0:T(8,128)(2,1)S(1)} %add_convert_fusion.1.q_ref.k_ref.v_ref, ...), custom_call_target="tpu_custom_call" | custom-call | tf_op jit(solution)/shard_map/attend_forward/pallas_call | solution.py:151
  96.9 6.9 %attend_forward.3 = (bf16[1024,256]{1,0:T(8,128)(2,1)S(1)}, f32[1024,256]{1,0:T(8,128)S(1)}) custom-call(bf16[1024,768]{1,0:T(8,128)(2,1)S(1)} %add_convert_fusion.q_ref.k_ref.v_ref, bf16[1024,768]{1,0:T(8,128)(2,1)S(1)} %add_convert_fusion.q_ref.k_ref.v_ref, bf16[1024,768]{1,0:T(8,128)(2,1)S(1)} %add_convert_fusion.q_ref.k_ref.v_ref, ...), custom_call_target="tpu_custom_call" | custom-call | tf_op jit(solution)/shard_map/attend_forward/pallas_call | solution.py:151
  109.4 10.9 %collective-permute-done.17 = bf16[2,2,64,1024]{3,2,1,0:T(8,128)(2,1)S(1)} collective-permute-done((bf16[2,2,64,1024]{3,2,1,0:T(8,128)(2,1)S(1)}, bf16[2,2,64,1024]{3,2,1,0:T(8,128)(2,1)S(1)}, u32[]{:S(2)}, u32[]{:S(2)}) %collective-permute-start.17) | collective-permute-done | bytes 524320 | tf_op jit(solution)/shard_map/ppermute | solution.py:217
  121.1 17.3 %collective-permute-done.18 = bf16[2,2,2,64,1280]{4,3,2,1,0:T(8,128)(2,1)S(1)} collective-permute-done((bf16[2,2,2,64,1280]{4,3,2,1,0:T(8,128)(2,1)S(1)}, bf16[2,2,2,64,1280]{4,3,2,1,0:T(8,128)(2,1)S(1)}, u32[]{:S(2)}, u32[]{:S(2)}) %collective-permute-start.18) | collective-permute-done | bytes 1310752 | tf_op jit(solution)/shard_map/ppermute | solution.py:212
  138.4 11.2 %collective-permute-done.21 = bf16[2,2,64,1024]{3,2,0,1:T(8,128)(2,1)S(1)} collective-permute-done((bf16[2,2,64,1024]{3,2,0,1:T(8,128)(2,1)S(1)}, bf16[2,2,64,1024]{3,2,0,1:T(8,128)(2,1)S(1)}, u32[]{:S(2)}, u32[]{:S(2)}) %collective-permute-start.21) | collective-permute-done | bytes 524320 | tf_op jit(solution)/shard_map/ppermute | solution.py:212
  159.7 13.8 %multiply_convert_fusion = (bf16[1024,1024]{1,0:T(8,128)(2,1)S(1)}, f32[1024,1024]{1,0:T(8,128)}, f32[1024,1024]{1,0:T(8,128)}) fusion(f32[1024]{0:T(1024)S(1)} %get-tuple-element.452, bf16[1024,1280]{1,0:T(8,128)(2,1)S(1)} %bitcast.335, bf16[512,1024]{1,0:T(8,128)(2,1)S(1)} %collective-permute-done.25, bf16[512,1024]{1,0:T(8,128)(2,1)S(1)} %fusion.20), kind=kOutput, calls=%fused_computation.6 | convolution fusion | flops 2220883968 | bytes 14684160 | tf_op jit(solution)/shard_map/dot_general | solution.py:526
  173.6 14.5 %multiply_convert_fusion.1 = (bf16[1024,1024]{1,0:T(8,128)(2,1)S(1)}, f32[1024,1024]{1,0:T(8,128)}, f32[1024,1024]{1,0:T(8,128)}) fusion(f32[1024]{0:T(1024)S(1)} %get-tuple-element.453, bf16[1024,1280]{1,0:T(8,128)(2,1)S(1)} %bitcast.341, bf16[512,1024]{1,0:T(8,128)(2,1)S(1)} %collective-permute-done.25, bf16[512,1024]{1,0:T(8,128)(2,1)S(1)} %fusion.20), kind=kOutput, calls=%fused_computation.19 | convolution fusion | flops 2220883968 | bytes 14684160 | tf_op jit(solution)/shard_map/dot_general | solution.py:526
  211.2 4.1 convolution_convert_fusion.2
  233.1 4.2 %convolution_convert_fusion = bf16[1024,1024]{1,0:T(8,128)(2,1)} fusion(bf16[1024,1024]{1,0:T(8,128)(2,1)S(1)} %get-tuple-element.261, bf16[512,1024]{1,0:T(8,128)(2,1)S(1)} %copy-done.101, bf16[512,1024]{1,0:T(8,128)(2,1)S(1)} %copy-done.65), kind=kOutput, calls=%fused_computation.77 | convolution fusion | flops 2152726528 | bytes 6291456 | tf_op jit(solution)/shard_map/nd,nf->df/dot_general | solution.py:551
  243.0 5.4 %collective-permute-done.29 = bf16[2,2,2,64,1024]{4,3,2,1,0:T(8,128)(2,1)S(1)} collective-permute-done((bf16[2,2,2,64,1024]{4,3,2,1,0:T(8,128)(2,1)S(1)}, bf16[2,2,2,64,1024]{4,3,2,1,0:T(8,128)(2,1)S(1)}, u32[]{:S(2)}, u32[]{:S(2)}) %collective-permute-start.29) | collective-permute-done | bytes 1048608 | tf_op jit(solution)/shard_map/ppermute | solution.py:212
  290.7 13.5 %attend_backward.2 = (bf16[1024,768]{1,0:T(8,128)(2,1)S(1)}, f32[2,256]{1,0:T(2,128)S(1)}) custom-call(bf16[1024,768]{1,0:T(8,128)(2,1)S(1)} %add_convert_fusion.1.q_ref.k_ref.v_ref, bf16[1024,768]{1,0:T(8,128)(2,1)S(1)} %add_convert_fusion.1.q_ref.k_ref.v_ref, bf16[1024,768]{1,0:T(8,128)(2,1)S(1)} %add_convert_fusion.1.q_ref.k_ref.v_ref, ...), custom_call_target="tpu_custom_call" | custom-call | tf_op jit(solution)/shard_map/attend_backward/pallas_call | solution.py:169
  318.6 13.8 %attend_backward.3 = (bf16[1024,768]{1,0:T(8,128)(2,1)S(1)}, f32[2,256]{1,0:T(2,128)S(1)}) custom-call(bf16[1024,768]{1,0:T(8,128)(2,1)S(1)} %copy-done.1, bf16[1024,768]{1,0:T(8,128)(2,1)S(1)} %copy-done.1, bf16[1024,768]{1,0:T(8,128)(2,1)S(1)} %copy-done.1, bf16[1024,256]{1,0:T(8,128)(2,1)S(1)} %copy-done.10, bf16[1024,256]{1,0:T(8,128)(2,1)S(1)} %copy-done.3, ...), custom_call_target="tpu_custom_call" | custom-call | tf_op jit(solution)/shard_map/attend_backward/pallas_call | solution.py:169
  346.2 4.9 %collective-permute-start.46 = (bf16[512,1024]{1,0:T(8,128)(2,1)S(1)}, bf16[512,1024]{1,0:T(8,128)(2,1)S(1)}, u32[]{:S(2)}, u32[]{:S(2)}) collective-permute-start(bf16[512,1024]{1,0:T(8,128)(2,1)S(1)} %add_convert_fusion.3), channel_id=1, source_target_pairs={{0,2},{2,0},{1,3},{3,1},{4,6},{6,4},{5,7},{7,5},{8,10},{10,8},{9,1... | collective-permute-start | bytes 3145736 | tf_op jit(solution)/shard_map/ppermute | solution.py:208
  356.7 6.4 %collective-permute-start.49 = (bf16[2,64,1280]{2,1,0:T(8,128)(2,1)S(1)}, bf16[2,64,1280]{2,1,0:T(8,128)(2,1)S(1)}, u32[]{:S(2)}, u32[]{:S(2)}) collective-permute-start(bf16[2,64,1280]{2,1,0:T(8,128)(2,1)S(1)} %get-tuple-element.395), channel_id=1, source_target_pairs={{0,16},{1,18},{2,17},{3,19},{4,20},{5,22},{6,21},{7,23},{8,24},{9,... | collective-permute-start | bytes 983048 | tf_op jit(solution)/shard_map/ppermute | solution.py:200
  376.7 4.8 %collective-permute-done.50 = bf16[2,64,1280]{2,1,0:T(8,128)(2,1)S(1)} collective-permute-done((bf16[2,64,1280]{2,1,0:T(8,128)(2,1)S(1)}, bf16[2,64,1280]{2,1,0:T(8,128)(2,1)S(1)}, u32[]{:S(2)}, u32[]{:S(2)}) %collective-permute-start.50) | collective-permute-done | bytes 327712 | tf_op jit(solution)/shard_map/ppermute | solution.py:191
  387.5 4.2 %collective-permute-start.56 = (f32[3072]{0:T(1024)S(1)}, f32[3072]{0:T(1024)S(1)}, u32[]{:S(2)}, u32[]{:S(2)}) collective-permute-start(f32[3072]{0:T(1024)S(1)} %slice.388), channel_id=1, source_target_pairs={{1,2},{2,1},{5,6},{6,5},{9,10},{10,9},{13,14},{14,13},{17,18},{18,... | collective-permute-start | bytes 36872 | tf_op jit(solution)/shard_map/ppermute | solution.py:191
  395.2 5.5 %collective-permute-start.58 = (bf16[2,64,768]{2,1,0:T(8,128)(2,1)S(1)}, bf16[2,64,768]{2,1,0:T(8,128)(2,1)S(1)}, u32[]{:S(2)}, u32[]{:S(2)}) collective-permute-start(bf16[2,64,768]{2,1,0:T(8,128)(2,1)S(1)} %get-tuple-element.421), channel_id=1, source_target_pairs={{0,16},{1,18},{2,17},{3,19},{4,20},{5,22},{6,21},{7,23},{8,24},{9,... | collective-permute-start | bytes 589832 | tf_op jit(solution)/shard_map/ppermute | solution.py:200
  403.4 6.6 %collective-permute-done.57 = bf16[512,1024]{1,0:T(8,128)(2,1)S(1)} collective-permute-done((bf16[512,1024]{1,0:T(8,128)(2,1)S(1)}, bf16[512,1024]{1,0:T(8,128)(2,1)S(1)}, u32[]{:S(2)}, u32[]{:S(2)}) %collective-permute-start.57) | collective-permute-done | bytes 1048608 | tf_op jit(solution)/shard_map/ppermute | solution.py:191
  (518 shorter events, 214.9 us)
Async XLA Ops:
  17.2 29.5 %collective-permute-start.7 = (bf16[512,1024]{1,0:T(8,128)(2,1)}, bf16[512,1024]{1,0:T(8,128)(2,1)S(1)}, u32[]{:S(2)}, u32[]{:S(2)}) collective-permute-start(bf16[512,1024]{1,0:T(8,128)(2,1)} %param.24), channel_id=1, source_target_pairs={{1,2},{2,1},{5,6},{6,5},{9,10},{10,9},{13,14},{14,13},{17,18},{18,... | collective-permute-start | bytes 3145736 | tf_op jit(solution)/shard_map/ppermute | solution.py:191
  27.3 19.5 %collective-permute-start.5 = (bf16[2,2,64,768]{3,2,0,1:T(8,128)(2,1)S(1)}, bf16[2,2,64,768]{3,2,0,1:T(8,128)(2,1)S(1)}, u32[]{:S(2)}, u32[]{:S(2)}) collective-permute-start(bf16[2,2,64,768]{3,2,0,1:T(8,128)(2,1)S(1)} %maximum_select_fusion.23), channel_id=1, source_target_pairs={{0,1},{1,0},{2,3},{3,2},{4,5},{5,4},{6,7},{7,6},{8,9},{9,8},{10,11... | collective-permute-start | bytes 1179656 | tf_op jit(solution)/shard_map/ppermute | solution.py:212
  30.5 21.0 %collective-permute-start.9 = (f32[4096]{0:T(1024)S(1)}, f32[4096]{0:T(1024)S(1)}, u32[]{:S(2)}, u32[]{:S(2)}) collective-permute-start(f32[4096]{0:T(1024)S(1)} %pad_maximum_fusion.17), channel_id=1, source_target_pairs={{1,2},{2,1},{5,6},{6,5},{9,10},{10,9},{13,14},{14,13},{17,18},{18,... | collective-permute-start | bytes 49160 | tf_op jit(solution)/shard_map/ppermute | solution.py:191
  72.6 19.9 %collective-permute-start.13 = (bf16[2,2,64,1280]{3,2,1,0:T(8,128)(2,1)}, bf16[2,2,64,1280]{3,2,1,0:T(8,128)(2,1)}, u32[]{:S(2)}, u32[]{:S(2)}) collective-permute-start(bf16[2,2,64,1280]{3,2,1,0:T(8,128)(2,1)} %maximum_select_fusion.14), channel_id=1, source_target_pairs={{0,4},{4,0},{8,12},{12,8},{16,20},{20,16},{24,28},{28,24},{1,5},{5... | collective-permute-start | bytes 1966088 | tf_op jit(solution)/shard_map/ppermute | solution.py:217
  74.5 29.4 %collective-permute-start.16 = (bf16[512,1024]{1,0:T(8,128)(2,1)}, bf16[512,1024]{1,0:T(8,128)(2,1)}, u32[]{:S(2)}, u32[]{:S(2)}) collective-permute-start(bf16[512,1024]{1,0:T(8,128)(2,1)} %param.25), channel_id=1, source_target_pairs={{1,2},{2,1},{5,6},{6,5},{9,10},{10,9},{13,14},{14,13},{17,18},{18,... | collective-permute-start | bytes 3145736 | tf_op jit(solution)/shard_map/ppermute | solution.py:191
  79.0 24.9 %collective-permute-start.15 = (bf16[2,64,1024]{2,1,0:T(8,128)(2,1)S(1)}, bf16[2,64,1024]{2,1,0:T(8,128)(2,1)}, u32[]{:S(2)}, u32[]{:S(2)}) collective-permute-start(bf16[2,64,1024]{2,1,0:T(8,128)(2,1)S(1)} %slice.372), channel_id=1, source_target_pairs={{0,16},{4,20},{8,24},{12,28},{16,0},{20,4},{24,8},{28,12},{1,17},{... | collective-permute-start | bytes 786440 | tf_op jit(solution)/shard_map/ppermute | solution.py:217
  108.0 30.4 %collective-permute-start.18 = (bf16[2,2,2,64,1280]{4,3,2,1,0:T(8,128)(2,1)S(1)}, bf16[2,2,2,64,1280]{4,3,2,1,0:T(8,128)(2,1)S(1)}, u32[]{:S(2)}, u32[]{:S(2)}) collective-permute-start(bf16[2,2,2,64,1280]{4,3,2,1,0:T(8,128)(2,1)S(1)} %maximum_select_fusion.6), channel_id=1, source_target_pairs={{0,1},{1,0},{2,3},{3,2},{4,5},{5,4},{6,7},{7,6},{8,9},{9,8},{10,11... | collective-permute-start | bytes 3932168 | tf_op jit(solution)/shard_map/ppermute | solution.py:212
  108.0 30.4 %collective-permute-start.19 = (bf16[2,2,2,64,1280]{4,3,0,1,2:T(8,128)(2,1)S(1)}, bf16[2,2,2,64,1280]{4,3,0,1,2:T(8,128)(2,1)S(1)}, u32[]{:S(2)}, u32[]{:S(2)}) collective-permute-start(bf16[2,2,2,64,1280]{4,3,0,1,2:T(8,128)(2,1)S(1)} %maximum_select_fusion.7), channel_id=1, source_target_pairs={{0,4},{4,0},{8,12},{12,8},{16,20},{20,16},{24,28},{28,24},{1,5},{5... | collective-permute-start | bytes 3932168 | tf_op jit(solution)/shard_map/ppermute | solution.py:217
  120.5 29.2 %collective-permute-start.21 = (bf16[2,2,64,1024]{3,2,0,1:T(8,128)(2,1)S(1)}, bf16[2,2,64,1024]{3,2,0,1:T(8,128)(2,1)S(1)}, u32[]{:S(2)}, u32[]{:S(2)}) collective-permute-start(bf16[2,2,64,1024]{3,2,0,1:T(8,128)(2,1)S(1)} %maximum_select_fusion.18), channel_id=1, source_target_pairs={{0,1},{1,0},{2,3},{3,2},{4,5},{5,4},{6,7},{7,6},{8,9},{9,8},{10,11... | collective-permute-start | bytes 1572872 | tf_op jit(solution)/shard_map/ppermute | solution.py:212
  120.7 29.0 %collective-permute-start.20 = (bf16[2,2,64,1024]{3,2,0,1:T(8,128)(2,1)S(1)}, bf16[2,2,64,1024]{3,2,0,1:T(8,128)(2,1)S(1)}, u32[]{:S(2)}, u32[]{:S(2)}) collective-permute-start(bf16[2,2,64,1024]{3,2,0,1:T(8,128)(2,1)S(1)} %maximum_select_fusion.17), channel_id=1, source_target_pairs={{0,4},{4,0},{8,12},{12,8},{16,20},{20,16},{24,28},{28,24},{1,5},{5... | collective-permute-start | bytes 1572872 | tf_op jit(solution)/shard_map/ppermute | solution.py:217
  157.4 30.6 %collective-permute-start.22 = (bf16[2,2,2,64,1024]{4,3,0,2,1:T(8,128)(2,1)S(1)}, bf16[2,2,2,64,1024]{4,3,0,2,1:T(8,128)(2,1)S(1)}, u32[]{:S(2)}, u32[]{:S(2)}) collective-permute-start(bf16[2,2,2,64,1024]{4,3,0,2,1:T(8,128)(2,1)S(1)} %maximum_select_fusion.8), channel_id=1, source_target_pairs={{0,1},{1,0},{2,3},{3,2},{4,5},{5,4},{6,7},{7,6},{8,9},{9,8},{10,11... | collective-permute-start | bytes 3145736 | tf_op jit(solution)/shard_map/ppermute | solution.py:212
  158.9 29.2 %collective-permute-start.23 = (bf16[2,2,2,64,1024]{4,3,0,2,1:T(8,128)(2,1)S(1)}, bf16[2,2,2,64,1024]{4,3,0,2,1:T(8,128)(2,1)S(1)}, u32[]{:S(2)}, u32[]{:S(2)}) collective-permute-start(bf16[2,2,2,64,1024]{4,3,0,2,1:T(8,128)(2,1)S(1)} %maximum_select_fusion.9), channel_id=1, source_target_pairs={{0,4},{4,0},{8,12},{12,8},{16,20},{20,16},{24,28},{28,24},{1,5},{5... | collective-permute-start | bytes 3145736 | tf_op jit(solution)/shard_map/ppermute | solution.py:217
  222.3 20.7 %collective-permute-start.30 = (bf16[2,2,2,64,1024]{4,3,1,0,2:T(8,128)(2,1)S(1)}, bf16[2,2,2,64,1024]{4,3,1,0,2:T(8,128)(2,1)S(1)}, u32[]{:S(2)}, u32[]{:S(2)}) collective-permute-start(bf16[2,2,2,64,1024]{4,3,1,0,2:T(8,128)(2,1)S(1)} %bitcast.376), channel_id=1, source_target_pairs={{0,4},{4,0},{8,12},{12,8},{16,20},{20,16},{24,28},{28,24},{1,5},{5... | collective-permute-start | bytes 3145736 | tf_op jit(solution)/shard_map/ppermute | solution.py:217
  223.4 24.9 %collective-permute-start.29 = (bf16[2,2,2,64,1024]{4,3,2,1,0:T(8,128)(2,1)S(1)}, bf16[2,2,2,64,1024]{4,3,2,1,0:T(8,128)(2,1)S(1)}, u32[]{:S(2)}, u32[]{:S(2)}) collective-permute-start(bf16[2,2,2,64,1024]{4,3,2,1,0:T(8,128)(2,1)S(1)} %dynamic-slice_bitcast_fusion.1), channel_id=1, source_target_pairs={{0,1},{1,0},{2,3},{3,2},{4,5},{5,4},{6,7},{7,6},{8,9},{9,8},{10,11... | collective-permute-start | bytes 3145736 | tf_op jit(solution)/shard_map/ppermute | solution.py:212
  279.5 31.3 %collective-permute-start.37 = (bf16[2,2,2,64,1280]{4,3,1,0,2:T(8,128)(2,1)}, bf16[2,2,2,64,1280]{4,3,1,0,2:T(8,128)(2,1)}, u32[]{:S(2)}, u32[]{:S(2)}) collective-permute-start(bf16[2,2,2,64,1280]{4,3,1,0,2:T(8,128)(2,1)} %bitcast.323), channel_id=1, source_target_pairs={{0,4},{4,0},{8,12},{12,8},{16,20},{20,16},{24,28},{28,24},{1,5},{5... | collective-permute-start | bytes 3932168 | tf_op jit(solution)/shard_map/ppermute | solution.py:217
  281.3 29.7 %collective-permute-start.36 = (bf16[2,2,2,64,1280]{4,3,2,1,0:T(8,128)(2,1)}, bf16[2,2,2,64,1280]{4,3,2,1,0:T(8,128)(2,1)}, u32[]{:S(2)}, u32[]{:S(2)}) collective-permute-start(bf16[2,2,2,64,1280]{4,3,2,1,0:T(8,128)(2,1)} %dynamic-slice_bitcast_fusion), channel_id=1, source_target_pairs={{0,1},{1,0},{2,3},{3,2},{4,5},{5,4},{6,7},{7,6},{8,9},{9,8},{10,11... | collective-permute-start | bytes 3932168 | tf_op jit(solution)/shard_map/ppermute | solution.py:212
  284.4 19.8 %collective-permute-start.35 = (bf16[2,2,64,1024]{3,2,1,0:T(8,128)(2,1)}, bf16[2,2,64,1024]{3,2,1,0:T(8,128)(2,1)}, u32[]{:S(2)}, u32[]{:S(2)}) collective-permute-start(bf16[2,2,64,1024]{3,2,1,0:T(8,128)(2,1)} %fusion.71), channel_id=1, source_target_pairs={{0,8},{4,12},{8,0},{12,4},{16,24},{20,28},{24,16},{28,20},{1,9},{5... | collective-permute-start | bytes 1572872 | tf_op jit(solution)/shard_map/ppermute | solution.py:217
  286.9 51.8 %collective-permute-start.42 = (f32[6,1024]{1,0:T(8,128)S(1)}, f32[6,1024]{1,0:T(8,128)S(1)}, u32[]{:S(2)}, u32[]{:S(2)}) collective-permute-start(f32[6,1024]{1,0:T(8,128)S(1)} %stack.453), channel_id=1, source_target_pairs={{0,2},{2,0},{1,3},{3,1},{4,6},{6,4},{5,7},{7,5},{8,10},{10,8},{9,1... | collective-permute-start | bytes 73736 | tf_op jit(solution)/shard_map/ppermute | solution.py:208
  306.2 32.5 %collective-permute-start.38 = (bf16[2,64,1024]{2,1,0:T(8,128)(2,1)S(1)}, bf16[2,64,1024]{2,1,0:T(8,128)(2,1)S(1)}, u32[]{:S(2)}, u32[]{:S(2)}) collective-permute-start(bf16[2,64,1024]{2,1,0:T(8,128)(2,1)S(1)} %get-tuple-element.405), channel_id=1, source_target_pairs={{0,16},{1,18},{2,17},{3,19},{4,20},{5,22},{6,21},{7,23},{8,24},{9,... | collective-permute-start | bytes 786440 | tf_op jit(solution)/shard_map/ppermute | solution.py:200
  307.5 31.2 %collective-permute-start.39 = (bf16[2,64,1024]{2,1,0:T(8,128)(2,1)S(1)}, bf16[2,64,1024]{2,1,0:T(8,128)(2,1)S(1)}, u32[]{:S(2)}, u32[]{:S(2)}) collective-permute-start(bf16[2,64,1024]{2,1,0:T(8,128)(2,1)S(1)} %get-tuple-element.404), channel_id=1, source_target_pairs={{1,2},{2,1},{5,6},{6,5},{9,10},{10,9},{13,14},{14,13},{17,18},{18,... | collective-permute-start | bytes 786440 | tf_op jit(solution)/shard_map/ppermute | solution.py:191
  313.9 24.9 %collective-permute-start.41 = (bf16[2,2,64,1280]{3,2,1,0:T(8,128)(2,1)S(1)}, bf16[2,2,64,1280]{3,2,1,0:T(8,128)(2,1)}, u32[]{:S(2)}, u32[]{:S(2)}) collective-permute-start(bf16[2,2,64,1280]{3,2,1,0:T(8,128)(2,1)S(1)} %dynamic-slice_bitcast_fusion.4), channel_id=1, source_target_pairs={{0,1},{1,0},{2,3},{3,2},{4,5},{5,4},{6,7},{7,6},{8,9},{9,8},{10,11... | collective-permute-start | bytes 1966088 | tf_op jit(solution)/shard_map/ppermute | solution.py:212
  317.5 21.2 %collective-permute-start.40 = (bf16[2,2,64,1280]{3,2,1,0:T(8,128)(2,1)S(1)}, bf16[2,2,64,1280]{3,2,1,0:T(8,128)(2,1)}, u32[]{:S(2)}, u32[]{:S(2)}) collective-permute-start(bf16[2,2,64,1280]{3,2,1,0:T(8,128)(2,1)S(1)} %dynamic-slice_bitcast_fusion.5), channel_id=1, source_target_pairs={{0,4},{4,0},{8,12},{12,8},{16,20},{20,16},{24,28},{28,24},{1,5},{5... | collective-permute-start | bytes 1966088 | tf_op jit(solution)/shard_map/ppermute | solution.py:217
  352.5 21.3 %collective-permute-start.47 = (bf16[2,2,2,64,768]{4,3,2,1,0:T(8,128)(2,1)S(1)}, bf16[2,2,2,64,768]{4,3,2,1,0:T(8,128)(2,1)S(1)}, u32[]{:S(2)}, u32[]{:S(2)}) collective-permute-start(bf16[2,2,2,64,768]{4,3,2,1,0:T(8,128)(2,1)S(1)} %dynamic-slice_bitcast_fusion.2), channel_id=1, source_target_pairs={{0,1},{1,0},{2,3},{3,2},{4,5},{5,4},{6,7},{7,6},{8,9},{9,8},{10,11... | collective-permute-start | bytes 2359304 | tf_op jit(solution)/shard_map/ppermute | solution.py:212
  356.7 20.0 %collective-permute-start.49 = (bf16[2,64,1280]{2,1,0:T(8,128)(2,1)S(1)}, bf16[2,64,1280]{2,1,0:T(8,128)(2,1)S(1)}, u32[]{:S(2)}, u32[]{:S(2)}) collective-permute-start(bf16[2,64,1280]{2,1,0:T(8,128)(2,1)S(1)} %get-tuple-element.395), channel_id=1, source_target_pairs={{0,16},{1,18},{2,17},{3,19},{4,20},{5,22},{6,21},{7,23},{8,24},{9,... | collective-permute-start | bytes 983048 | tf_op jit(solution)/shard_map/ppermute | solution.py:200
  (146 other events, 1164.1 us)

commit v6 on v5

--- a/solution.py
+++ b/solution.py
@@ -300,9 +300,9 @@
         if not self.native:
             self.held = tuple(part.reshape(2, 2, 2, 2, -1, self.width) for part in self.held)
 
-    def start(self):
+    def start(self, order=None, *values):
         if self.native:
-            return
+            return values
         if self.step == 0:
             plan = ((Y, 3), (X, 2))
         elif self.step == 1:
@@ -311,16 +311,19 @@
             plan = ((Z1, self.held[0].ndim - 3),)
         else:
             plan = ((Z2, self.held[0].ndim - 3),)
-        self.keep, self.flight = [], []
+        self.keep, sends = [], []
         for part, (stage, axis) in zip(self.held, plan):
             bit = bits()[stage]
             self.keep.append(lax.dynamic_index_in_dim(part, bit, axis, keepdims=False))
-            send = lax.dynamic_index_in_dim(part, 1 - bit, axis, keepdims=False)
-            if self.step < 3:
-                self.flight.append(STAGES[stage](send))
+            sends.append(lax.dynamic_index_in_dim(part, 1 - bit, axis, keepdims=False))
+        if order is not None:
+            out = order.at(*sends, *values)
+            sends, values = out[: len(sends)], out[len(sends) :]
         if self.step == 3:
-            self.flight = [cross_far(send), cross(self.keep[0])]
-        self.flight = tuple(self.flight)
+            self.flight = (cross_far(sends[0]), cross(self.keep[0]))
+        else:
+            self.flight = tuple(STAGES[stage](send) for send, (stage, _) in zip(sends, plan))
+        return values
 
     def finish(self):
         if self.native:
@@ -510,14 +513,14 @@
     cotangent = settle(cotangent, cot_other)
     order.arrive(down)
     down.start()
-    context = order.arrive((upo, down), *context)
-    context = order.follow(down, *context)
-    down.start()
+    context = order.arrive(upo, *context)
     uo_w = upo.result()
     out_w = [part[:, :half] for part in uo_w]
     up_w = [part[:, half:] for part in uo_w]
 
     attended = summed(context, out_w, "ne,de->nd")
+    (attended,) = order.arrive(down, attended)
+    down.start()
     first_sum = tokens.astype(f32) + attended + w_vec[0]
     hidden, first_pull = jax.vjp(layer_norm, first_sum, w_vec[2], w_vec[3])
     hidden_full = full(hidden.astype(bf16))
@@ -558,7 +561,7 @@
     uo_grads = [jnp.concatenate([out_grads[h], up_grads[h]], 1) for h in sides]
     (first_full, *uo_grads) = order.at(first_full, *uo_grads)
     upo_sum = Reduce(*uo_grads)
-    upo_sum.start()
+    (first_full,) = upo_sum.start(order, first_full)
     context_grads = [
         jnp.einsum("nd,de->ne", first_full, out_w[h], preferred_element_type=f32).astype(bf16) for h in sides
     ]
@@ -567,7 +570,6 @@
     packed16, bias_sums = [None, None], [None, None]
     packed16[0], bias_sums[0] = attend_backward(packed[0], context_grads[0], context[0], logsum[0], seg_col)
     (context_grads[1], packed16[0]) = order.arrive(down_sum, context_grads[1], packed16[0])
-    layer_out = settle(layer_out, out_other)
     down_sum.start()
     (context_grads[1], packed16[0]) = order.arrive(upo_sum, context_grads[1], packed16[0])
     upo_sum.start()
@@ -604,8 +606,9 @@
     grad_tokens = (first_grad + near + grad_far.astype(f32)).astype(bf16)
     (grad_tokens, down_both) = order.arrive(totals, grad_tokens, down_both)
     totals.start()
-    order.arrive(qkv_sum)
+    (layer_out, out_other) = order.arrive(qkv_sum, layer_out, out_other)
     qkv_sum.start()
+    layer_out = settle(layer_out, out_other)
     order.arrive((upo_sum, totals))
     totals.start()
     upo_both = upo_sum.result()

time: 424 us -> 415 us (0.979)
    ppermute x13, waiting for transfers between devices: 41.3 us -> 25.5 us  [y_exchange(): return lax.ppermute(values, 'tensor', FLIP)]
    ppermute x23, waiting for transfers between devices: 49.1 us -> 61.9 us  [chip_exchange(): return lax.ppermute(values, 'chip', [(k, k ^ mask) for k in range(count)])]
    unnamed x222 -> x226, local copies, waits for them, and re-layouts: 14.4 us -> 14.1 us
  transfers between devices with their start and end apart: 60 -> 60, of which waited for: 24 -> 26; matrix products, arithmetic and copies ran while one was open for 28% -> 28% of each run, Pallas kernels for 10% -> 10%
where the time goes in v6:
time: 415 us; the launch traced here: 411 us
  waiting for transfers between devices  117 us (28%)
  matrix products  89.8 us (22%)
  starting transfers between devices  87 us (21%)
  other arithmetic  48.5 us (12%)
  Pallas kernels  41.2 us (10%)
  local copies, waits for them, and re-layouts  24 us (6%)
    ppermute x23, waiting for transfers between devices, chip_exchange(): return lax.ppermute(values, 'chip', [(k, k ^ mask) for k in range(count)])  61.9 us
    ppermute x11, starting transfers between devices, cross(): return lax.ppermute(values, ('core', 'tensor'), CROSS)  36.8 us
    dot_general x2, matrix products, body(): jnp.dot(hidden_full, up_w[h], preferred_element_type=f32)  28.2 us
    pallas_call x2, Pallas kernels, attend_backward(): pl.pallas_call(functools.partial(backward_kernel, block=block), grid=(pai...  27.3 us
    ppermute x13, waiting for transfers between devices, y_exchange(): return lax.ppermute(values, 'tensor', FLIP)  25.5 us
    ppermute x11, waiting for transfers between devices, cross(): return lax.ppermute(values, ('core', 'tensor'), CROSS)  17.9 us
    dot_general x16, matrix products, pair_dot(): jnp.einsum(form, left, right, preferred_element_type=f32)  17.8 us
    ppermute x23, starting transfers between devices, chip_exchange(): return lax.ppermute(values, 'chip', [(k, k ^ mask) for k in range(count)])  16.9 us
  transfers between devices with their start and end apart: 60, of which 26 were waited for; matrix products, arithmetic and copies ran while one was open for 28% of the time, Pallas kernels for 10%

profile of v6, /device:TPU:1, one launch (start us, length us, event | category | flops | bytes accessed | tf_op | source)
XLA Modules:
  0.0 410.6 jit_solution(8543099798227800282)
XLA Ops:
  1.9 4.5 %collective-permute-start = (bf16[2,64,768]{2,1,0:T(8,128)(2,1)S(1)}, bf16[2,64,768]{2,1,0:T(8,128)(2,1)S(1)}, u32[]{:S(2)}, u32[]{:S(2)}) collective-permute-start(bf16[2,64,768]{2,1,0:T(8,128)(2,1)S(1)} %pad_maximum_fusion.15), channel_id=1, source_target_pairs={{1,2},{2,1},{5,6},{6,5},{9,10},{10,9},{13,14},{14,13},{17,18},{18,... | collective-permute-start | bytes 589832 | tf_op jit(solution)/shard_map/ppermute | solution.py:191
  20.0 7.1 %collective-permute-done.2 = bf16[2,2,64,768]{3,2,1,0:T(8,128)(2,1)S(1)} collective-permute-done((bf16[2,2,64,768]{3,2,1,0:T(8,128)(2,1)S(1)}, bf16[2,2,64,768]{3,2,1,0:T(8,128)(2,1)S(1)}, u32[]{:S(2)}, u32[]{:S(2)}) %collective-permute-start.2) | collective-permute-done | bytes 393248 | tf_op jit(solution)/shard_map/ppermute | solution.py:217
  30.5 5.3 %collective-permute-start.9 = (f32[4096]{0:T(1024)S(1)}, f32[4096]{0:T(1024)S(1)}, u32[]{:S(2)}, u32[]{:S(2)}) collective-permute-start(f32[4096]{0:T(1024)S(1)} %pad_maximum_fusion.17), channel_id=1, source_target_pairs={{1,2},{2,1},{5,6},{6,5},{9,10},{10,9},{13,14},{14,13},{17,18},{18,... | collective-permute-start | bytes 49160 | tf_op jit(solution)/shard_map/ppermute | solution.py:191
  36.0 10.8 %collective-permute-done.6 = bf16[2,64,1280]{2,1,0:T(8,128)(2,1)S(1)} collective-permute-done((bf16[2,64,1280]{2,1,0:T(8,128)(2,1)S(1)}, bf16[2,64,1280]{2,1,0:T(8,128)(2,1)S(1)}, u32[]{:S(2)}, u32[]{:S(2)}) %collective-permute-start.6) | collective-permute-done | bytes 327712 | tf_op jit(solution)/shard_map/ppermute | solution.py:217
  53.2 12.5 %collective-permute-done.10 = bf16[2,2,64,1280]{3,2,1,0:T(8,128)(2,1)S(1)} collective-permute-done((bf16[2,2,64,1280]{3,2,1,0:T(8,128)(2,1)S(1)}, bf16[2,2,64,1280]{3,2,1,0:T(8,128)(2,1)S(1)}, u32[]{:S(2)}, u32[]{:S(2)}) %collective-permute-start.10) | collective-permute-done | bytes 655392 | tf_op jit(solution)/shard_map/ppermute | solution.py:217
  74.5 4.7 %collective-permute-start.16 = (bf16[512,1024]{1,0:T(8,128)(2,1)}, bf16[512,1024]{1,0:T(8,128)(2,1)}, u32[]{:S(2)}, u32[]{:S(2)}) collective-permute-start(bf16[512,1024]{1,0:T(8,128)(2,1)} %param.25), channel_id=1, source_target_pairs={{1,2},{2,1},{5,6},{6,5},{9,10},{10,9},{13,14},{14,13},{17,18},{18,... | collective-permute-start | bytes 3145736 | tf_op jit(solution)/shard_map/ppermute | solution.py:191
  82.6 6.9 %attend_forward.2 = (bf16[1024,256]{1,0:T(8,128)(2,1)S(1)}, f32[1024,256]{1,0:T(8,128)S(1)}) custom-call(bf16[1024,768]{1,0:T(8,128)(2,1)S(1)} %add_convert_fusion.1.q_ref.k_ref.v_ref, bf16[1024,768]{1,0:T(8,128)(2,1)S(1)} %add_convert_fusion.1.q_ref.k_ref.v_ref, bf16[1024,768]{1,0:T(8,128)(2,1)S(1)} %add_convert_fusion.1.q_ref.k_ref.v_ref, ...), custom_call_target="tpu_custom_call" | custom-call | tf_op jit(solution)/shard_map/attend_forward/pallas_call | solution.py:151
  97.1 6.9 %attend_forward.3 = (bf16[1024,256]{1,0:T(8,128)(2,1)S(1)}, f32[1024,256]{1,0:T(8,128)S(1)}) custom-call(bf16[1024,768]{1,0:T(8,128)(2,1)S(1)} %add_convert_fusion.q_ref.k_ref.v_ref, bf16[1024,768]{1,0:T(8,128)(2,1)S(1)} %add_convert_fusion.q_ref.k_ref.v_ref, bf16[1024,768]{1,0:T(8,128)(2,1)S(1)} %add_convert_fusion.q_ref.k_ref.v_ref, ...), custom_call_target="tpu_custom_call" | custom-call | tf_op jit(solution)/shard_map/attend_forward/pallas_call | solution.py:151
  104.1 7.7 %collective-permute-done.15 = bf16[2,64,1024]{2,1,0:T(8,128)(2,1)S(1)} collective-permute-done((bf16[2,64,1024]{2,1,0:T(8,128)(2,1)S(1)}, bf16[2,64,1024]{2,1,0:T(8,128)(2,1)S(1)}, u32[]{:S(2)}, u32[]{:S(2)}) %collective-permute-start.15) | collective-permute-done | bytes 262176 | tf_op jit(solution)/shard_map/ppermute | solution.py:217
  112.1 12.9 %collective-permute-done.17 = bf16[2,2,64,1024]{3,2,1,0:T(8,128)(2,1)S(1)} collective-permute-done((bf16[2,2,64,1024]{3,2,1,0:T(8,128)(2,1)S(1)}, bf16[2,2,64,1024]{3,2,1,0:T(8,128)(2,1)S(1)}, u32[]{:S(2)}, u32[]{:S(2)}) %collective-permute-start.17) | collective-permute-done | bytes 524320 | tf_op jit(solution)/shard_map/ppermute | solution.py:217
  135.7 11.0 %collective-permute-done.21 = bf16[2,2,64,1024]{3,2,0,1:T(8,128)(2,1)S(1)} collective-permute-done((bf16[2,2,64,1024]{3,2,0,1:T(8,128)(2,1)S(1)}, bf16[2,2,64,1024]{3,2,0,1:T(8,128)(2,1)S(1)}, u32[]{:S(2)}, u32[]{:S(2)}) %collective-permute-start.21) | collective-permute-done | bytes 524320 | tf_op jit(solution)/shard_map/ppermute | solution.py:212
  151.6 13.8 %multiply_convert_fusion = (bf16[1024,1024]{1,0:T(8,128)(2,1)S(1)}, f32[1024,1024]{1,0:T(8,128)}, f32[1024,1024]{1,0:T(8,128)}) fusion(f32[1024]{0:T(1024)S(1)} %get-tuple-element.464, bf16[1024,1280]{1,0:T(8,128)(2,1)S(1)} %bitcast.351, bf16[512,1024]{1,0:T(8,128)(2,1)S(1)} %collective-permute-done.25, bf16[512,1024]{1,0:T(8,128)(2,1)S(1)} %fusion.20), kind=kOutput, calls=%fused_computation.6 | convolution fusion | flops 2220883968 | bytes 14684160 | tf_op jit(solution)/shard_map/dot_general | solution.py:529
  165.5 14.4 %multiply_convert_fusion.1 = (bf16[1024,1024]{1,0:T(8,128)(2,1)S(1)}, f32[1024,1024]{1,0:T(8,128)}, f32[1024,1024]{1,0:T(8,128)}) fusion(f32[1024]{0:T(1024)S(1)} %get-tuple-element.465, bf16[1024,1280]{1,0:T(8,128)(2,1)S(1)} %bitcast.345, bf16[512,1024]{1,0:T(8,128)(2,1)S(1)} %collective-permute-done.25, bf16[512,1024]{1,0:T(8,128)(2,1)S(1)} %fusion.20), kind=kOutput, calls=%fused_computation.19 | convolution fusion | flops 2220883968 | bytes 14684160 | tf_op jit(solution)/shard_map/dot_general | solution.py:529
  202.8 4.1 %convolution_convert_fusion.2 = bf16[1024,1024]{1,0:T(8,128)(2,1)S(1)} fusion(bf16[1024,1024]{1,0:T(8,128)(2,1)S(1)} %copy-done.107, bf16[512,1024]{1,0:T(8,128)(2,1)} %collective-permute-done.27, bf16[512,1024]{1,0:T(8,128)(2,1)} %get-tuple-element.389), kind=kOutput, calls=%fused_computation.80 | convolution fusion | flops 2152726528 | bytes 6291456 | tf_op jit(solution)/shard_map/nd,nf->df/dot_general | solution.py:544
  207.0 4.1 %convolution_convert_fusion.3 = bf16[1024,1024]{1,0:T(8,128)(2,1)S(1)} fusion(bf16[1024,1024]{1,0:T(8,128)(2,1)S(1)} %copy-done.105, bf16[512,1024]{1,0:T(8,128)(2,1)} %collective-permute-done.27, bf16[512,1024]{1,0:T(8,128)(2,1)} %get-tuple-element.389), kind=kOutput, calls=%fused_computation.81 | convolution fusion | flops 2152726528 | bytes 6291456 | tf_op jit(solution)/shard_map/nd,nf->df/dot_general | solution.py:544
  226.1 4.2 %convolution_convert_fusion = bf16[1024,1024]{1,0:T(8,128)(2,1)} fusion(bf16[1024,1024]{1,0:T(8,128)(2,1)S(1)} %get-tuple-element.260, bf16[512,1024]{1,0:T(8,128)(2,1)S(1)} %copy-done.103, bf16[512,1024]{1,0:T(8,128)(2,1)S(1)} %copy-done.67), kind=kOutput, calls=%fused_computation.78 | convolution fusion | flops 2152726528 | bytes 6291456 | tf_op jit(solution)/shard_map/nd,nf->df/dot_general | solution.py:554
  236.4 4.9 %collective-permute-done.29 = bf16[2,2,2,64,1024]{4,3,2,1,0:T(8,128)(2,1)S(1)} collective-permute-done((bf16[2,2,2,64,1024]{4,3,2,1,0:T(8,128)(2,1)S(1)}, bf16[2,2,2,64,1024]{4,3,2,1,0:T(8,128)(2,1)S(1)}, u32[]{:S(2)}, u32[]{:S(2)}) %collective-permute-start.29) | collective-permute-done | bytes 1048608 | tf_op jit(solution)/shard_map/ppermute | solution.py:212
  280.9 13.5 %attend_backward.2 = (bf16[1024,768]{1,0:T(8,128)(2,1)S(1)}, f32[2,256]{1,0:T(2,128)S(1)}) custom-call(bf16[1024,768]{1,0:T(8,128)(2,1)S(1)} %add_convert_fusion.1.q_ref.k_ref.v_ref, bf16[1024,768]{1,0:T(8,128)(2,1)S(1)} %add_convert_fusion.1.q_ref.k_ref.v_ref, bf16[1024,768]{1,0:T(8,128)(2,1)S(1)} %add_convert_fusion.1.q_ref.k_ref.v_ref, ...), custom_call_target="tpu_custom_call" | custom-call | tf_op jit(solution)/shard_map/attend_backward/pallas_call | solution.py:169
  310.9 13.8 %attend_backward.3 = (bf16[1024,768]{1,0:T(8,128)(2,1)S(1)}, f32[2,256]{1,0:T(2,128)S(1)}) custom-call(bf16[1024,768]{1,0:T(8,128)(2,1)S(1)} %copy-done.1, bf16[1024,768]{1,0:T(8,128)(2,1)S(1)} %copy-done.1, bf16[1024,768]{1,0:T(8,128)(2,1)S(1)} %copy-done.1, bf16[1024,256]{1,0:T(8,128)(2,1)S(1)} %copy-done.10, bf16[1024,256]{1,0:T(8,128)(2,1)S(1)} %copy-done.3, ...), custom_call_target="tpu_custom_call" | custom-call | tf_op jit(solution)/shard_map/attend_backward/pallas_call | solution.py:169
  344.7 5.4 %collective-permute-done.43 = bf16[2,2,64,1280]{3,2,1,0:T(8,128)(2,1)S(1)} collective-permute-done((bf16[2,2,64,1280]{3,2,1,0:T(8,128)(2,1)S(1)}, bf16[2,2,64,1280]{3,2,1,0:T(8,128)(2,1)S(1)}, u32[]{:S(2)}, u32[]{:S(2)}) %collective-permute-start.43) | collective-permute-done | bytes 655392 | tf_op jit(solution)/shard_map/ppermute | solution.py:217
  350.8 5.5 %collective-permute-start.49 = (bf16[2,64,1280]{2,1,0:T(8,128)(2,1)S(1)}, bf16[2,64,1280]{2,1,0:T(8,128)(2,1)S(1)}, u32[]{:S(2)}, u32[]{:S(2)}) collective-permute-start(bf16[2,64,1280]{2,1,0:T(8,128)(2,1)S(1)} %get-tuple-element.403), channel_id=1, source_target_pairs={{0,16},{1,18},{2,17},{3,19},{4,20},{5,22},{6,21},{7,23},{8,24},{9,... | collective-permute-start | bytes 983048 | tf_op jit(solution)/shard_map/ppermute | solution.py:200
  369.5 4.4 %collective-permute-done.50 = bf16[2,64,1280]{2,1,0:T(8,128)(2,1)S(1)} collective-permute-done((bf16[2,64,1280]{2,1,0:T(8,128)(2,1)S(1)}, bf16[2,64,1280]{2,1,0:T(8,128)(2,1)S(1)}, u32[]{:S(2)}, u32[]{:S(2)}) %collective-permute-start.50) | collective-permute-done | bytes 327712 | tf_op jit(solution)/shard_map/ppermute | solution.py:191
  380.1 4.2 %collective-permute-start.56 = (f32[3072]{0:T(1024)S(1)}, f32[3072]{0:T(1024)S(1)}, u32[]{:S(2)}, u32[]{:S(2)}) collective-permute-start(f32[3072]{0:T(1024)S(1)} %slice.388), channel_id=1, source_target_pairs={{1,2},{2,1},{5,6},{6,5},{9,10},{10,9},{13,14},{14,13},{17,18},{18,... | collective-permute-start | bytes 36872 | tf_op jit(solution)/shard_map/ppermute | solution.py:191
  394.4 8.3 %collective-permute-done.57 = bf16[512,1024]{1,0:T(8,128)(2,1)S(1)} collective-permute-done((bf16[512,1024]{1,0:T(8,128)(2,1)S(1)}, bf16[512,1024]{1,0:T(8,128)(2,1)S(1)}, u32[]{:S(2)}, u32[]{:S(2)}) %collective-permute-start.57) | collective-permute-done | bytes 1048608 | tf_op jit(solution)/shard_map/ppermute | solution.py:191
  (525 shorter events, 216.2 us)
Async XLA Ops:
  17.2 29.5 %collective-permute-start.7 = (bf16[512,1024]{1,0:T(8,128)(2,1)}, bf16[512,1024]{1,0:T(8,128)(2,1)S(1)}, u32[]{:S(2)}, u32[]{:S(2)}) collective-permute-start(bf16[512,1024]{1,0:T(8,128)(2,1)} %param.24), channel_id=1, source_target_pairs={{1,2},{2,1},{5,6},{6,5},{9,10},{10,9},{13,14},{14,13},{17,18},{18,... | collective-permute-start | bytes 3145736 | tf_op jit(solution)/shard_map/ppermute | solution.py:191
  27.3 19.5 %collective-permute-start.5 = (bf16[2,2,64,768]{3,2,0,1:T(8,128)(2,1)S(1)}, bf16[2,2,64,768]{3,2,0,1:T(8,128)(2,1)S(1)}, u32[]{:S(2)}, u32[]{:S(2)}) collective-permute-start(bf16[2,2,64,768]{3,2,0,1:T(8,128)(2,1)S(1)} %maximum_select_fusion.25), channel_id=1, source_target_pairs={{0,1},{1,0},{2,3},{3,2},{4,5},{5,4},{6,7},{7,6},{8,9},{9,8},{10,11... | collective-permute-start | bytes 1179656 | tf_op jit(solution)/shard_map/ppermute | solution.py:212
  27.4 19.3 %collective-permute-start.4 = (bf16[2,2,64,768]{3,2,1,0:T(8,128)(2,1)S(1)}, bf16[2,2,64,768]{3,2,1,0:T(8,128)(2,1)S(1)}, u32[]{:S(2)}, u32[]{:S(2)}) collective-permute-start(bf16[2,2,64,768]{3,2,1,0:T(8,128)(2,1)S(1)} %maximum_select_fusion.24), channel_id=1, source_target_pairs={{0,4},{4,0},{8,12},{12,8},{16,20},{20,16},{24,28},{28,24},{1,5},{5... | collective-permute-start | bytes 1179656 | tf_op jit(solution)/shard_map/ppermute | solution.py:217
  30.5 21.0 %collective-permute-start.9 = (f32[4096]{0:T(1024)S(1)}, f32[4096]{0:T(1024)S(1)}, u32[]{:S(2)}, u32[]{:S(2)}) collective-permute-start(f32[4096]{0:T(1024)S(1)} %pad_maximum_fusion.17), channel_id=1, source_target_pairs={{1,2},{2,1},{5,6},{6,5},{9,10},{10,9},{13,14},{14,13},{17,18},{18,... | collective-permute-start | bytes 49160 | tf_op jit(solution)/shard_map/ppermute | solution.py:191
  48.8 19.1 %collective-permute-start.12 = (bf16[2,2,2,64,768]{4,3,0,1,2:T(8,128)(2,1)S(1)}, bf16[2,2,2,64,768]{4,3,0,1,2:T(8,128)(2,1)S(1)}, u32[]{:S(2)}, u32[]{:S(2)}) collective-permute-start(bf16[2,2,2,64,768]{4,3,0,1,2:T(8,128)(2,1)S(1)} %maximum_select_fusion.13), channel_id=1, source_target_pairs={{0,4},{4,0},{8,12},{12,8},{16,20},{20,16},{24,28},{28,24},{1,5},{5... | collective-permute-start | bytes 2359304 | tf_op jit(solution)/shard_map/ppermute | solution.py:217
  49.1 18.9 %collective-permute-start.11 = (bf16[2,2,2,64,768]{4,3,2,1,0:T(8,128)(2,1)S(1)}, bf16[2,2,2,64,768]{4,3,2,1,0:T(8,128)(2,1)S(1)}, u32[]{:S(2)}, u32[]{:S(2)}) collective-permute-start(bf16[2,2,2,64,768]{4,3,2,1,0:T(8,128)(2,1)S(1)} %maximum_select_fusion.12), channel_id=1, source_target_pairs={{0,1},{1,0},{2,3},{3,2},{4,5},{5,4},{6,7},{7,6},{8,9},{9,8},{10,11... | collective-permute-start | bytes 2359304 | tf_op jit(solution)/shard_map/ppermute | solution.py:212
  72.6 19.8 %collective-permute-start.13 = (bf16[2,2,64,1280]{3,2,1,0:T(8,128)(2,1)}, bf16[2,2,64,1280]{3,2,1,0:T(8,128)(2,1)}, u32[]{:S(2)}, u32[]{:S(2)}) collective-permute-start(bf16[2,2,64,1280]{3,2,1,0:T(8,128)(2,1)} %maximum_select_fusion.16), channel_id=1, source_target_pairs={{0,4},{4,0},{8,12},{12,8},{16,20},{20,16},{24,28},{28,24},{1,5},{5... | collective-permute-start | bytes 1966088 | tf_op jit(solution)/shard_map/ppermute | solution.py:217
  74.5 37.3 %collective-permute-start.16 = (bf16[512,1024]{1,0:T(8,128)(2,1)}, bf16[512,1024]{1,0:T(8,128)(2,1)}, u32[]{:S(2)}, u32[]{:S(2)}) collective-permute-start(bf16[512,1024]{1,0:T(8,128)(2,1)} %param.25), channel_id=1, source_target_pairs={{1,2},{2,1},{5,6},{6,5},{9,10},{10,9},{13,14},{14,13},{17,18},{18,... | collective-permute-start | bytes 3145736 | tf_op jit(solution)/shard_map/ppermute | solution.py:191
  96.8 31.8 %collective-permute-start.18 = (bf16[2,2,2,64,1280]{4,3,2,1,0:T(8,128)(2,1)S(1)}, bf16[2,2,2,64,1280]{4,3,2,1,0:T(8,128)(2,1)S(1)}, u32[]{:S(2)}, u32[]{:S(2)}) collective-permute-start(bf16[2,2,2,64,1280]{4,3,2,1,0:T(8,128)(2,1)S(1)} %maximum_select_fusion.6), channel_id=1, source_target_pairs={{0,1},{1,0},{2,3},{3,2},{4,5},{5,4},{6,7},{7,6},{8,9},{9,8},{10,11... | collective-permute-start | bytes 3932168 | tf_op jit(solution)/shard_map/ppermute | solution.py:212
  96.9 31.7 %collective-permute-start.19 = (bf16[2,2,2,64,1280]{4,3,0,1,2:T(8,128)(2,1)S(1)}, bf16[2,2,2,64,1280]{4,3,0,1,2:T(8,128)(2,1)S(1)}, u32[]{:S(2)}, u32[]{:S(2)}) collective-permute-start(bf16[2,2,2,64,1280]{4,3,0,1,2:T(8,128)(2,1)S(1)} %maximum_select_fusion.7), channel_id=1, source_target_pairs={{0,4},{4,0},{8,12},{12,8},{16,20},{20,16},{24,28},{28,24},{1,5},{5... | collective-permute-start | bytes 3932168 | tf_op jit(solution)/shard_map/ppermute | solution.py:217
  149.5 30.4 %collective-permute-start.24 = (bf16[2,2,2,64,1024]{4,3,0,1,2:T(8,128)(2,1)S(1)}, bf16[2,2,2,64,1024]{4,3,0,1,2:T(8,128)(2,1)S(1)}, u32[]{:S(2)}, u32[]{:S(2)}) collective-permute-start(bf16[2,2,2,64,1024]{4,3,0,1,2:T(8,128)(2,1)S(1)} %maximum_select_fusion.9), channel_id=1, source_target_pairs={{0,4},{4,0},{8,12},{12,8},{16,20},{20,16},{24,28},{28,24},{1,5},{5... | collective-permute-start | bytes 3145736 | tf_op jit(solution)/shard_map/ppermute | solution.py:217
  149.7 30.2 %collective-permute-start.23 = (bf16[2,2,2,64,1024]{4,3,0,1,2:T(8,128)(2,1)S(1)}, bf16[2,2,2,64,1024]{4,3,0,1,2:T(8,128)(2,1)S(1)}, u32[]{:S(2)}, u32[]{:S(2)}) collective-permute-start(bf16[2,2,2,64,1024]{4,3,0,1,2:T(8,128)(2,1)S(1)} %maximum_select_fusion.8), channel_id=1, source_target_pairs={{0,1},{1,0},{2,3},{3,2},{4,5},{5,4},{6,7},{7,6},{8,9},{9,8},{10,11... | collective-permute-start | bytes 3145736 | tf_op jit(solution)/shard_map/ppermute | solution.py:212
  215.6 20.7 %collective-permute-start.30 = (bf16[2,2,2,64,1024]{4,3,1,0,2:T(8,128)(2,1)S(1)}, bf16[2,2,2,64,1024]{4,3,1,0,2:T(8,128)(2,1)S(1)}, u32[]{:S(2)}, u32[]{:S(2)}) collective-permute-start(bf16[2,2,2,64,1024]{4,3,1,0,2:T(8,128)(2,1)S(1)} %bitcast.388), channel_id=1, source_target_pairs={{0,4},{4,0},{8,12},{12,8},{16,20},{20,16},{24,28},{28,24},{1,5},{5... | collective-permute-start | bytes 3145736 | tf_op jit(solution)/shard_map/ppermute | solution.py:217
  217.2 24.0 %collective-permute-start.29 = (bf16[2,2,2,64,1024]{4,3,2,1,0:T(8,128)(2,1)S(1)}, bf16[2,2,2,64,1024]{4,3,2,1,0:T(8,128)(2,1)S(1)}, u32[]{:S(2)}, u32[]{:S(2)}) collective-permute-start(bf16[2,2,2,64,1024]{4,3,2,1,0:T(8,128)(2,1)S(1)} %dynamic-slice_bitcast_fusion.1), channel_id=1, source_target_pairs={{0,1},{1,0},{2,3},{3,2},{4,5},{5,4},{6,7},{7,6},{8,9},{9,8},{10,11... | collective-permute-start | bytes 3145736 | tf_op jit(solution)/shard_map/ppermute | solution.py:212
  253.9 19.9 %collective-permute-start.34 = (bf16[2,2,64,1024]{3,2,1,0:T(8,128)(2,1)S(1)}, bf16[2,2,64,1024]{3,2,1,0:T(8,128)(2,1)S(1)}, u32[]{:S(2)}, u32[]{:S(2)}) collective-permute-start(bf16[2,2,64,1024]{3,2,1,0:T(8,128)(2,1)S(1)} %dynamic-slice_bitcast_fusion.6), channel_id=1, source_target_pairs={{0,1},{1,0},{2,3},{3,2},{4,5},{5,4},{6,7},{7,6},{8,9},{9,8},{10,11... | collective-permute-start | bytes 1572872 | tf_op jit(solution)/shard_map/ppermute | solution.py:212
  273.7 30.4 %collective-permute-start.36 = (bf16[2,2,2,64,1280]{4,3,2,1,0:T(8,128)(2,1)}, bf16[2,2,2,64,1280]{4,3,2,1,0:T(8,128)(2,1)}, u32[]{:S(2)}, u32[]{:S(2)}) collective-permute-start(bf16[2,2,2,64,1280]{4,3,2,1,0:T(8,128)(2,1)} %dynamic-slice_bitcast_fusion), channel_id=1, source_target_pairs={{0,1},{1,0},{2,3},{3,2},{4,5},{5,4},{6,7},{7,6},{8,9},{9,8},{10,11... | collective-permute-start | bytes 3932168 | tf_op jit(solution)/shard_map/ppermute | solution.py:212
  274.7 29.7 %collective-permute-start.37 = (bf16[2,2,2,64,1280]{4,3,1,0,2:T(8,128)(2,1)}, bf16[2,2,2,64,1280]{4,3,1,0,2:T(8,128)(2,1)}, u32[]{:S(2)}, u32[]{:S(2)}) collective-permute-start(bf16[2,2,2,64,1280]{4,3,1,0,2:T(8,128)(2,1)} %bitcast.333), channel_id=1, source_target_pairs={{0,4},{4,0},{8,12},{12,8},{16,20},{20,16},{24,28},{28,24},{1,5},{5... | collective-permute-start | bytes 3932168 | tf_op jit(solution)/shard_map/ppermute | solution.py:217
  277.3 53.6 %collective-permute-start.42 = (f32[6,1024]{1,0:T(8,128)S(1)}, f32[6,1024]{1,0:T(8,128)S(1)}, u32[]{:S(2)}, u32[]{:S(2)}) collective-permute-start(f32[6,1024]{1,0:T(8,128)S(1)} %stack.471), channel_id=1, source_target_pairs={{0,2},{2,0},{1,3},{3,1},{4,6},{6,4},{5,7},{7,5},{8,10},{10,8},{9,1... | collective-permute-start | bytes 73736 | tf_op jit(solution)/shard_map/ppermute | solution.py:208
  296.4 34.6 %collective-permute-start.38 = (bf16[2,64,1024]{2,1,0:T(8,128)(2,1)S(1)}, bf16[2,64,1024]{2,1,0:T(8,128)(2,1)S(1)}, u32[]{:S(2)}, u32[]{:S(2)}) collective-permute-start(bf16[2,64,1024]{2,1,0:T(8,128)(2,1)S(1)} %get-tuple-element.413), channel_id=1, source_target_pairs={{0,16},{1,18},{2,17},{3,19},{4,20},{5,22},{6,21},{7,23},{8,24},{9,... | collective-permute-start | bytes 786440 | tf_op jit(solution)/shard_map/ppermute | solution.py:200
  300.0 30.9 %collective-permute-start.39 = (bf16[2,64,1024]{2,1,0:T(8,128)(2,1)S(1)}, bf16[2,64,1024]{2,1,0:T(8,128)(2,1)S(1)}, u32[]{:S(2)}, u32[]{:S(2)}) collective-permute-start(bf16[2,64,1024]{2,1,0:T(8,128)(2,1)S(1)} %get-tuple-element.412), channel_id=1, source_target_pairs={{1,2},{2,1},{5,6},{6,5},{9,10},{10,9},{13,14},{14,13},{17,18},{18,... | collective-permute-start | bytes 786440 | tf_op jit(solution)/shard_map/ppermute | solution.py:191
  307.2 23.8 %collective-permute-start.41 = (bf16[2,2,64,1280]{3,2,1,0:T(8,128)(2,1)S(1)}, bf16[2,2,64,1280]{3,2,1,0:T(8,128)(2,1)}, u32[]{:S(2)}, u32[]{:S(2)}) collective-permute-start(bf16[2,2,64,1280]{3,2,1,0:T(8,128)(2,1)S(1)} %dynamic-slice_bitcast_fusion.4), channel_id=1, source_target_pairs={{0,1},{1,0},{2,3},{3,2},{4,5},{5,4},{6,7},{7,6},{8,9},{9,8},{10,11... | collective-permute-start | bytes 1966088 | tf_op jit(solution)/shard_map/ppermute | solution.py:212
  309.9 21.2 %collective-permute-start.40 = (bf16[2,2,64,1280]{3,2,1,0:T(8,128)(2,1)S(1)}, bf16[2,2,64,1280]{3,2,1,0:T(8,128)(2,1)}, u32[]{:S(2)}, u32[]{:S(2)}) collective-permute-start(bf16[2,2,64,1280]{3,2,1,0:T(8,128)(2,1)S(1)} %dynamic-slice_bitcast_fusion.5), channel_id=1, source_target_pairs={{0,4},{4,0},{8,12},{12,8},{16,20},{20,16},{24,28},{28,24},{1,5},{5... | collective-permute-start | bytes 1966088 | tf_op jit(solution)/shard_map/ppermute | solution.py:217
  343.2 18.9 %collective-permute-start.48 = (bf16[2,2,2,64,768]{4,3,1,0,2:T(8,128)(2,1)S(1)}, bf16[2,2,2,64,768]{4,3,1,0,2:T(8,128)(2,1)S(1)}, u32[]{:S(2)}, u32[]{:S(2)}) collective-permute-start(bf16[2,2,2,64,768]{4,3,1,0,2:T(8,128)(2,1)S(1)} %bitcast.391), channel_id=1, source_target_pairs={{0,4},{4,0},{8,12},{12,8},{16,20},{20,16},{24,28},{28,24},{1,5},{5... | collective-permute-start | bytes 2359304 | tf_op jit(solution)/shard_map/ppermute | solution.py:217
  344.4 19.3 %collective-permute-start.47 = (bf16[2,2,2,64,768]{4,3,2,1,0:T(8,128)(2,1)S(1)}, bf16[2,2,2,64,768]{4,3,2,1,0:T(8,128)(2,1)S(1)}, u32[]{:S(2)}, u32[]{:S(2)}) collective-permute-start(bf16[2,2,2,64,768]{4,3,2,1,0:T(8,128)(2,1)S(1)} %dynamic-slice_bitcast_fusion.2), channel_id=1, source_target_pairs={{0,1},{1,0},{2,3},{3,2},{4,5},{5,4},{6,7},{7,6},{8,9},{9,8},{10,11... | collective-permute-start | bytes 2359304 | tf_op jit(solution)/shard_map/ppermute | solution.py:212
  (148 other events, 1151.9 us)

commit v7 on v6

--- a/solution.py
+++ b/solution.py
@@ -491,7 +491,6 @@
     (tok_full,) = order.follow(upo, tok_full)
     upo.start()
     down.start()
-    cot_other = cross(cotangent)
     qkv_w = qkv.result()
 
     packed, context, logsum = [], [], []
@@ -505,13 +504,13 @@
         context.append(ctx)
         logsum.append(lse)
         if h == 0:
-            (context[0], packed[1]) = order.arrive(upo, context[0], packed[1])
+            (context[0], packed[1]) = order.arrive((upo, down), context[0], packed[1])
             (packed[1],) = order.follow(upo, packed[1])
+            (packed[1],) = order.follow(down, packed[1])
             upo.start()
-    (cot_other, *context) = order.arrive(down, cot_other, *context)
-    down.start()
-    cotangent = settle(cotangent, cot_other)
-    order.arrive(down)
+            down.start()
+    context = order.arrive(down, *context)
+    context = order.follow(down, *context)
     down.start()
     context = order.arrive(upo, *context)
     uo_w = upo.result()
@@ -519,8 +518,9 @@
     up_w = [part[:, half:] for part in uo_w]
 
     attended = summed(context, out_w, "ne,de->nd")
-    (attended,) = order.arrive(down, attended)
+    (attended, cotangent) = order.arrive(down, attended, cotangent)
     down.start()
+    cot_other = cross(cotangent)
     first_sum = tokens.astype(f32) + attended + w_vec[0]
     hidden, first_pull = jax.vjp(layer_norm, first_sum, w_vec[2], w_vec[3])
     hidden_full = full(hidden.astype(bf16))
@@ -532,7 +532,11 @@
         gelu_pulls.append(pull)
     active16 = order.arrive(down, *active16)
     down_w = down.result()
-    mixed = summed(active16, down_w, "nf,df->nd")
+    away = pair_dot([part[rows:] for part in active16], down_w, "nf,df->nd").astype(bf16)
+    (away, cot_other) = order.at(away, cot_other)
+    cotangent = settle(cotangent, cot_other)
+    other = core_exchange(away)
+    mixed = pair_dot([part[:rows] for part in active16], down_w, "nf,df->nd") + other.astype(f32)
     second_sum = hidden + mixed + w_vec[1]
     normed, second_pull = jax.vjp(layer_norm, second_sum, w_vec[4], w_vec[5])
     layer_out = normed.astype(bf16)
@@ -597,24 +601,25 @@
     totals = Sum(jnp.concatenate([(vec_local + vec_far).reshape(-1), bqv_local.reshape(-1), bup_local]))
     totals.start()
     down_both = down_sum.result()
-    away = pair_dot([part[rows:] for part in packed16], qkv_w, "ne,de->nd")
-    grad_far = core_exchange(away.astype(bf16))
     packed16 = order.arrive((upo_sum, totals), *packed16)
     upo_sum.start()
     totals.start()
+    (layer_out, out_other, down_both, *packed16) = order.arrive(
+        (qkv_sum, totals), layer_out, out_other, down_both, *packed16
+    )
+    totals.start()
+    packed16 = qkv_sum.start(order, *packed16)
+    away = pair_dot([part[rows:] for part in packed16], qkv_w, "ne,de->nd")
+    grad_far = core_exchange(away.astype(bf16))
     near = pair_dot([part[:rows] for part in packed16], qkv_w, "ne,de->nd")
     grad_tokens = (first_grad + near + grad_far.astype(f32)).astype(bf16)
-    (grad_tokens, down_both) = order.arrive(totals, grad_tokens, down_both)
+    layer_out = settle(layer_out, out_other)
+    (grad_tokens,) = order.arrive((qkv_sum, totals), grad_tokens)
+    qkv_sum.start()
     totals.start()
-    (layer_out, out_other) = order.arrive(qkv_sum, layer_out, out_other)
-    qkv_sum.start()
-    layer_out = settle(layer_out, out_other)
-    order.arrive((upo_sum, totals))
-    totals.start()
+    grad_other = cross(grad_tokens)
+    order.arrive(upo_sum)
     upo_both = upo_sum.result()
-    (upo_both, grad_tokens) = order.arrive(qkv_sum, upo_both, grad_tokens)
-    qkv_sum.start()
-    grad_other = cross(grad_tokens)
     order.arrive(totals)
     vectors = totals.held[0]
     count = vec_local.size

time: 415 us -> 412 us (level)
  waiting for transfers between devices: 117 us -> 109 us
    ppermute x11, waiting for transfers between devices: 17.9 us -> 5.97 us  [cross(): return lax.ppermute(values, ('core', 'tensor'), CROSS)]
    ppermute x13, starting transfers between devices: 6.82 us -> 11.6 us  [y_exchange(): return lax.ppermute(values, 'tensor', FLIP)]
    unnamed x226 -> x230, local copies, waits for them, and re-layouts: 14.1 us -> 17.5 us
  transfers between devices with their start and end apart: 60 -> 60, of which waited for: 26 -> 23; matrix products, arithmetic and copies ran while one was open for 28% -> 28% of each run, Pallas kernels for 10% -> 10%
where the time goes in v7:
time: 412 us; the launch traced here: 406 us
  waiting for transfers between devices  109 us (26%)
  matrix products  89.1 us (22%)
  starting transfers between devices  87.2 us (21%)
  other arithmetic  48.7 us (12%)
  Pallas kernels  41.4 us (10%)
  local copies, waits for them, and re-layouts  27.4 us (7%)
    ppermute x23, waiting for transfers between devices, chip_exchange(): return lax.ppermute(values, 'chip', [(k, k ^ mask) for k in range(count)])  63.7 us
    ppermute x11, starting transfers between devices, cross(): return lax.ppermute(values, ('core', 'tensor'), CROSS)  35.3 us
    dot_general x2, matrix products, body(): jnp.dot(hidden_full, up_w[h], preferred_element_type=f32)  28.2 us
    ppermute x13, waiting for transfers between devices, y_exchange(): return lax.ppermute(values, 'tensor', FLIP)  27.5 us
    pallas_call x2, Pallas kernels, attend_backward(): pl.pallas_call(functools.partial(backward_kernel, block=block), grid=(pai...  27.3 us
    ppermute x23, starting transfers between devices, chip_exchange(): return lax.ppermute(values, 'chip', [(k, k ^ mask) for k in range(count)])  19.9 us
    unnamed x230, local copies, waits for them, and re-layouts  17.5 us
    dot_general x16, matrix products, pair_dot(): jnp.einsum(form, left, right, preferred_element_type=f32)  17.4 us
  transfers between devices with their start and end apart: 60, of which 23 were waited for; matrix products, arithmetic and copies ran while one was open for 28% of the time, Pallas kernels for 10%

profile of v7, /device:TPU:1, one launch (start us, length us, event | category | flops | bytes accessed | tf_op | source)
XLA Modules:
  0.0 405.9 jit_solution(7465788451010544956)
XLA Ops:
  1.9 4.5 %collective-permute-start = (bf16[2,64,768]{2,1,0:T(8,128)(2,1)S(1)}, bf16[2,64,768]{2,1,0:T(8,128)(2,1)S(1)}, u32[]{:S(2)}, u32[]{:S(2)}) collective-permute-start(bf16[2,64,768]{2,1,0:T(8,128)(2,1)S(1)} %pad_maximum_fusion.15), channel_id=1, source_target_pairs={{1,2},{2,1},{5,6},{6,5},{9,10},{10,9},{13,14},{14,13},{17,18},{18,... | collective-permute-start | bytes 589832 | tf_op jit(solution)/shard_map/ppermute | solution.py:191
  8.9 3.8 collective-permute-start.3
  20.0 7.1 %collective-permute-done.2 = bf16[2,2,64,768]{3,2,1,0:T(8,128)(2,1)S(1)} collective-permute-done((bf16[2,2,64,768]{3,2,1,0:T(8,128)(2,1)S(1)}, bf16[2,2,64,768]{3,2,1,0:T(8,128)(2,1)S(1)}, u32[]{:S(2)}, u32[]{:S(2)}) %collective-permute-start.2) | collective-permute-done | bytes 393248 | tf_op jit(solution)/shard_map/ppermute | solution.py:217
  30.5 5.3 %collective-permute-start.9 = (f32[4096]{0:T(1024)S(1)}, f32[4096]{0:T(1024)S(1)}, u32[]{:S(2)}, u32[]{:S(2)}) collective-permute-start(f32[4096]{0:T(1024)S(1)} %pad_maximum_fusion.17), channel_id=1, source_target_pairs={{1,2},{2,1},{5,6},{6,5},{9,10},{10,9},{13,14},{14,13},{17,18},{18,... | collective-permute-start | bytes 49160 | tf_op jit(solution)/shard_map/ppermute | solution.py:191
  36.0 10.8 %collective-permute-done.6 = bf16[2,64,1280]{2,1,0:T(8,128)(2,1)S(1)} collective-permute-done((bf16[2,64,1280]{2,1,0:T(8,128)(2,1)S(1)}, bf16[2,64,1280]{2,1,0:T(8,128)(2,1)S(1)}, u32[]{:S(2)}, u32[]{:S(2)}) %collective-permute-start.6) | collective-permute-done | bytes 327712 | tf_op jit(solution)/shard_map/ppermute | solution.py:217
  52.5 12.8 %collective-permute-done.10 = bf16[2,2,64,1280]{3,2,1,0:T(8,128)(2,1)S(1)} collective-permute-done((bf16[2,2,64,1280]{3,2,1,0:T(8,128)(2,1)S(1)}, bf16[2,2,64,1280]{3,2,1,0:T(8,128)(2,1)S(1)}, u32[]{:S(2)}, u32[]{:S(2)}) %collective-permute-start.10) | collective-permute-done | bytes 655392 | tf_op jit(solution)/shard_map/ppermute | solution.py:217
  77.7 7.1 %attend_forward.2 = (bf16[1024,256]{1,0:T(8,128)(2,1)S(1)}, f32[1024,256]{1,0:T(8,128)S(1)}) custom-call(bf16[1024,768]{1,0:T(8,128)(2,1)S(1)} %add_convert_fusion.1.q_ref.k_ref.v_ref, bf16[1024,768]{1,0:T(8,128)(2,1)S(1)} %add_convert_fusion.1.q_ref.k_ref.v_ref, bf16[1024,768]{1,0:T(8,128)(2,1)S(1)} %add_convert_fusion.1.q_ref.k_ref.v_ref, ...), custom_call_target="tpu_custom_call" | custom-call | tf_op jit(solution)/shard_map/attend_forward/pallas_call | solution.py:151
  96.3 6.9 %attend_forward.3 = (bf16[1024,256]{1,0:T(8,128)(2,1)S(1)}, f32[1024,256]{1,0:T(8,128)S(1)}) custom-call(bf16[1024,768]{1,0:T(8,128)(2,1)S(1)} %add_convert_fusion.q_ref.k_ref.v_ref, bf16[1024,768]{1,0:T(8,128)(2,1)S(1)} %add_convert_fusion.q_ref.k_ref.v_ref, bf16[1024,768]{1,0:T(8,128)(2,1)S(1)} %add_convert_fusion.q_ref.k_ref.v_ref, ...), custom_call_target="tpu_custom_call" | custom-call | tf_op jit(solution)/shard_map/attend_forward/pallas_call | solution.py:151
  106.2 15.9 %collective-permute-done.17 = bf16[2,2,2,64,1280]{4,3,2,1,0:T(8,128)(2,1)S(1)} collective-permute-done((bf16[2,2,2,64,1280]{4,3,2,1,0:T(8,128)(2,1)S(1)}, bf16[2,2,2,64,1280]{4,3,2,1,0:T(8,128)(2,1)S(1)}, u32[]{:S(2)}, u32[]{:S(2)}) %collective-permute-start.17) | collective-permute-done | bytes 1310752 | tf_op jit(solution)/shard_map/ppermute | solution.py:212
  129.6 10.6 %collective-permute-done.19 = bf16[2,2,64,1024]{3,2,0,1:T(8,128)(2,1)S(1)} collective-permute-done((bf16[2,2,64,1024]{3,2,0,1:T(8,128)(2,1)S(1)}, bf16[2,2,64,1024]{3,2,0,1:T(8,128)(2,1)S(1)}, u32[]{:S(2)}, u32[]{:S(2)}) %collective-permute-start.19) | collective-permute-done | bytes 524320 | tf_op jit(solution)/shard_map/ppermute | solution.py:217
  148.8 14.2 %multiply_convert_fusion = (bf16[1024,1024]{1,0:T(8,128)(2,1)S(1)}, f32[1024,1024]{1,0:T(8,128)}, f32[1024,1024]{1,0:T(8,128)}) fusion(f32[1024]{0:T(1024)S(1)} %get-tuple-element.484, bf16[1024,1280]{1,0:T(8,128)(2,1)S(1)} %bitcast.337, bf16[512,1024]{1,0:T(8,128)(2,1)S(1)} %collective-permute-done.24, bf16[512,1024]{1,0:T(8,128)(2,1)S(1)} %fusion.20), kind=kOutput, calls=%fused_computation.6 | convolution fusion | flops 2220883968 | bytes 14684160 | tf_op jit(solution)/shard_map/dot_general | solution.py:529
  163.0 14.0 %multiply_convert_fusion.1 = (bf16[1024,1024]{1,0:T(8,128)(2,1)S(1)}, f32[1024,1024]{1,0:T(8,128)}, f32[1024,1024]{1,0:T(8,128)}) fusion(f32[1024]{0:T(1024)S(1)} %get-tuple-element.485, bf16[1024,1280]{1,0:T(8,128)(2,1)S(1)} %bitcast.331, bf16[512,1024]{1,0:T(8,128)(2,1)S(1)} %collective-permute-done.24, bf16[512,1024]{1,0:T(8,128)(2,1)S(1)} %fusion.20), kind=kOutput, calls=%fused_computation.19 | convolution fusion | flops 2220883968 | bytes 14684160 | tf_op jit(solution)/shard_map/dot_general | solution.py:529
  197.8 4.1 %convolution_convert_fusion.2 = bf16[1024,1024]{1,0:T(8,128)(2,1)S(1)} fusion(bf16[1024,1024]{1,0:T(8,128)(2,1)S(1)} %copy-done.109, bf16[512,1024]{1,0:T(8,128)(2,1)} %collective-permute-done.27, bf16[512,1024]{1,0:T(8,128)(2,1)} %get-tuple-element.419), kind=kOutput, calls=%fused_computation.80 | convolution fusion | flops 2152726528 | bytes 6291456 | tf_op jit(solution)/shard_map/nd,nf->df/dot_general | solution.py:548
  202.0 4.1 %convolution_convert_fusion.3 = bf16[1024,1024]{1,0:T(8,128)(2,1)S(1)} fusion(bf16[1024,1024]{1,0:T(8,128)(2,1)S(1)} %copy-done.107, bf16[512,1024]{1,0:T(8,128)(2,1)} %collective-permute-done.27, bf16[512,1024]{1,0:T(8,128)(2,1)} %get-tuple-element.419), kind=kOutput, calls=%fused_computation.81 | convolution fusion | flops 2152726528 | bytes 6291456 | tf_op jit(solution)/shard_map/nd,nf->df/dot_general | solution.py:548
  220.9 4.2 %convolution_convert_fusion = bf16[1024,1024]{1,0:T(8,128)(2,1)} fusion(bf16[1024,1024]{1,0:T(8,128)(2,1)S(1)} %get-tuple-element.284, bf16[512,1024]{1,0:T(8,128)(2,1)S(1)} %copy-done.105, bf16[512,1024]{1,0:T(8,128)(2,1)S(1)} %copy-done.68), kind=kOutput, calls=%fused_computation.78 | convolution fusion | flops 2152726528 | bytes 6291456 | tf_op jit(solution)/shard_map/nd,nf->df/dot_general | solution.py:558
  225.1 3.8 convolution_convert_fusion.1
  231.1 4.8 %collective-permute-done.29 = bf16[2,2,2,64,1024]{4,3,2,1,0:T(8,128)(2,1)S(1)} collective-permute-done((bf16[2,2,2,64,1024]{4,3,2,1,0:T(8,128)(2,1)S(1)}, bf16[2,2,2,64,1024]{4,3,2,1,0:T(8,128)(2,1)S(1)}, u32[]{:S(2)}, u32[]{:S(2)}) %collective-permute-start.29) | collective-permute-done | bytes 1048608 | tf_op jit(solution)/shard_map/ppermute | solution.py:212
  277.3 13.5 %attend_backward.2 = (bf16[1024,768]{1,0:T(8,128)(2,1)S(1)}, f32[2,256]{1,0:T(2,128)S(1)}) custom-call(bf16[1024,768]{1,0:T(8,128)(2,1)S(1)} %add_convert_fusion.1.q_ref.k_ref.v_ref, bf16[1024,768]{1,0:T(8,128)(2,1)S(1)} %add_convert_fusion.1.q_ref.k_ref.v_ref, bf16[1024,768]{1,0:T(8,128)(2,1)S(1)} %add_convert_fusion.1.q_ref.k_ref.v_ref, ...), custom_call_target="tpu_custom_call" | custom-call | tf_op jit(solution)/shard_map/attend_backward/pallas_call | solution.py:169
  306.0 13.8 %attend_backward.3 = (bf16[1024,768]{1,0:T(8,128)(2,1)S(1)}, f32[2,256]{1,0:T(2,128)S(1)}) custom-call(bf16[1024,768]{1,0:T(8,128)(2,1)S(1)} %copy-done.1, bf16[1024,768]{1,0:T(8,128)(2,1)S(1)} %copy-done.1, bf16[1024,768]{1,0:T(8,128)(2,1)S(1)} %copy-done.1, bf16[1024,256]{1,0:T(8,128)(2,1)S(1)} %copy-done.10, bf16[1024,256]{1,0:T(8,128)(2,1)S(1)} %copy-done.3, ...), custom_call_target="tpu_custom_call" | custom-call | tf_op jit(solution)/shard_map/attend_backward/pallas_call | solution.py:169
  335.8 9.5 %collective-permute-done.44 = f32[9216]{0:T(1024)S(1)} collective-permute-done((f32[9216]{0:T(1024)S(1)}, f32[9216]{0:T(1024)S(1)}, u32[]{:S(2)}, u32[]{:S(2)}) %collective-permute-start.44) | collective-permute-done | bytes 36896 | tf_op jit(solution)/shard_map/ppermute | solution.py:217
  347.0 6.4 %collective-permute-start.52 = (bf16[2,64,1280]{2,1,0:T(8,128)(2,1)S(1)}, bf16[2,64,1280]{2,1,0:T(8,128)(2,1)S(1)}, u32[]{:S(2)}, u32[]{:S(2)}) collective-permute-start(bf16[2,64,1280]{2,1,0:T(8,128)(2,1)S(1)} %get-tuple-element.433), channel_id=1, source_target_pairs={{0,16},{1,18},{2,17},{3,19},{4,20},{5,22},{6,21},{7,23},{8,24},{9,... | collective-permute-start | bytes 983048 | tf_op jit(solution)/shard_map/ppermute | solution.py:200
  371.5 4.4 %collective-permute-done.49 = bf16[2,2,64,768]{3,2,1,0:T(8,128)(2,1)S(1)} collective-permute-done((bf16[2,2,64,768]{3,2,1,0:T(8,128)(2,1)S(1)}, bf16[2,2,64,768]{3,2,1,0:T(8,128)(2,1)S(1)}, u32[]{:S(2)}, u32[]{:S(2)}) %collective-permute-start.49) | collective-permute-done | bytes 393248 | tf_op jit(solution)/shard_map/ppermute | solution.py:212
  379.2 3.9 collective-permute-start.57
  396.0 3.8 collective-permute-done.58
  (528 shorter events, 213.2 us)
Async XLA Ops:
  17.2 29.5 %collective-permute-start.7 = (bf16[512,1024]{1,0:T(8,128)(2,1)S(1)}, bf16[512,1024]{1,0:T(8,128)(2,1)S(1)}, u32[]{:S(2)}, u32[]{:S(2)}) collective-permute-start(bf16[512,1024]{1,0:T(8,128)(2,1)S(1)} %copy-done.63), channel_id=1, source_target_pairs={{1,2},{2,1},{5,6},{6,5},{9,10},{10,9},{13,14},{14,13},{17,18},{18,... | collective-permute-start | bytes 3145736 | tf_op jit(solution)/shard_map/ppermute | solution.py:191
  27.3 19.5 %collective-permute-start.5 = (bf16[2,2,64,768]{3,2,0,1:T(8,128)(2,1)S(1)}, bf16[2,2,64,768]{3,2,0,1:T(8,128)(2,1)S(1)}, u32[]{:S(2)}, u32[]{:S(2)}) collective-permute-start(bf16[2,2,64,768]{3,2,0,1:T(8,128)(2,1)S(1)} %maximum_select_fusion.23), channel_id=1, source_target_pairs={{0,1},{1,0},{2,3},{3,2},{4,5},{5,4},{6,7},{7,6},{8,9},{9,8},{10,11... | collective-permute-start | bytes 1179656 | tf_op jit(solution)/shard_map/ppermute | solution.py:212
  27.4 19.4 %collective-permute-start.4 = (bf16[2,2,64,768]{3,2,1,0:T(8,128)(2,1)S(1)}, bf16[2,2,64,768]{3,2,1,0:T(8,128)(2,1)S(1)}, u32[]{:S(2)}, u32[]{:S(2)}) collective-permute-start(bf16[2,2,64,768]{3,2,1,0:T(8,128)(2,1)S(1)} %maximum_select_fusion.22), channel_id=1, source_target_pairs={{0,4},{4,0},{8,12},{12,8},{16,20},{20,16},{24,28},{28,24},{1,5},{5... | collective-permute-start | bytes 1179656 | tf_op jit(solution)/shard_map/ppermute | solution.py:217
  30.5 20.2 %collective-permute-start.9 = (f32[4096]{0:T(1024)S(1)}, f32[4096]{0:T(1024)S(1)}, u32[]{:S(2)}, u32[]{:S(2)}) collective-permute-start(f32[4096]{0:T(1024)S(1)} %pad_maximum_fusion.17), channel_id=1, source_target_pairs={{1,2},{2,1},{5,6},{6,5},{9,10},{10,9},{13,14},{14,13},{17,18},{18,... | collective-permute-start | bytes 49160 | tf_op jit(solution)/shard_map/ppermute | solution.py:191
  47.6 19.1 %collective-permute-start.12 = (bf16[2,2,2,64,768]{4,3,0,1,2:T(8,128)(2,1)S(1)}, bf16[2,2,2,64,768]{4,3,0,1,2:T(8,128)(2,1)S(1)}, u32[]{:S(2)}, u32[]{:S(2)}) collective-permute-start(bf16[2,2,2,64,768]{4,3,0,1,2:T(8,128)(2,1)S(1)} %maximum_select_fusion.13), channel_id=1, source_target_pairs={{0,4},{4,0},{8,12},{12,8},{16,20},{20,16},{24,28},{28,24},{1,5},{5... | collective-permute-start | bytes 2359304 | tf_op jit(solution)/shard_map/ppermute | solution.py:217
  93.1 29.1 %collective-permute-start.17 = (bf16[2,2,2,64,1280]{4,3,2,1,0:T(8,128)(2,1)S(1)}, bf16[2,2,2,64,1280]{4,3,2,1,0:T(8,128)(2,1)S(1)}, u32[]{:S(2)}, u32[]{:S(2)}) collective-permute-start(bf16[2,2,2,64,1280]{4,3,2,1,0:T(8,128)(2,1)S(1)} %maximum_select_fusion.6), channel_id=1, source_target_pairs={{0,1},{1,0},{2,3},{3,2},{4,5},{5,4},{6,7},{7,6},{8,9},{9,8},{10,11... | collective-permute-start | bytes 3932168 | tf_op jit(solution)/shard_map/ppermute | solution.py:212
  93.6 28.5 %collective-permute-start.18 = (bf16[2,2,2,64,1280]{4,3,0,1,2:T(8,128)(2,1)S(1)}, bf16[2,2,2,64,1280]{4,3,0,1,2:T(8,128)(2,1)S(1)}, u32[]{:S(2)}, u32[]{:S(2)}) collective-permute-start(bf16[2,2,2,64,1280]{4,3,0,1,2:T(8,128)(2,1)S(1)} %maximum_select_fusion.7), channel_id=1, source_target_pairs={{0,4},{4,0},{8,12},{12,8},{16,20},{20,16},{24,28},{28,24},{1,5},{5... | collective-permute-start | bytes 3932168 | tf_op jit(solution)/shard_map/ppermute | solution.py:217
  143.0 34.0 %collective-permute-start.23 = (bf16[2,2,2,64,1024]{4,3,0,1,2:T(8,128)(2,1)S(1)}, bf16[2,2,2,64,1024]{4,3,0,1,2:T(8,128)(2,1)S(1)}, u32[]{:S(2)}, u32[]{:S(2)}) collective-permute-start(bf16[2,2,2,64,1024]{4,3,0,1,2:T(8,128)(2,1)S(1)} %maximum_select_fusion.9), channel_id=1, source_target_pairs={{0,4},{4,0},{8,12},{12,8},{16,20},{20,16},{24,28},{28,24},{1,5},{5... | collective-permute-start | bytes 3145736 | tf_op jit(solution)/shard_map/ppermute | solution.py:217
  144.4 32.6 %collective-permute-start.22 = (bf16[2,2,2,64,1024]{4,3,0,1,2:T(8,128)(2,1)S(1)}, bf16[2,2,2,64,1024]{4,3,0,1,2:T(8,128)(2,1)S(1)}, u32[]{:S(2)}, u32[]{:S(2)}) collective-permute-start(bf16[2,2,2,64,1024]{4,3,0,1,2:T(8,128)(2,1)S(1)} %maximum_select_fusion.8), channel_id=1, source_target_pairs={{0,1},{1,0},{2,3},{3,2},{4,5},{5,4},{6,7},{7,6},{8,9},{9,8},{10,11... | collective-permute-start | bytes 3145736 | tf_op jit(solution)/shard_map/ppermute | solution.py:212
  145.4 35.4 %collective-permute-start.25 = (bf16[512,1024]{1,0:T(8,128)(2,1)S(1)}, bf16[512,1024]{1,0:T(8,128)(2,1)S(1)}, u32[]{:S(2)}, u32[]{:S(2)}) collective-permute-start(bf16[512,1024]{1,0:T(8,128)(2,1)S(1)} %copy-done.71), channel_id=1, source_target_pairs={{1,2},{2,1},{5,6},{6,5},{9,10},{10,9},{13,14},{14,13},{17,18},{18,... | collective-permute-start | bytes 3145736 | tf_op jit(solution)/shard_map/ppermute | solution.py:191
  210.4 20.7 %collective-permute-start.30 = (bf16[2,2,2,64,1024]{4,3,1,0,2:T(8,128)(2,1)S(1)}, bf16[2,2,2,64,1024]{4,3,1,0,2:T(8,128)(2,1)S(1)}, u32[]{:S(2)}, u32[]{:S(2)}) collective-permute-start(bf16[2,2,2,64,1024]{4,3,1,0,2:T(8,128)(2,1)S(1)} %bitcast.376), channel_id=1, source_target_pairs={{0,4},{4,0},{8,12},{12,8},{16,20},{20,16},{24,28},{28,24},{1,5},{5... | collective-permute-start | bytes 3145736 | tf_op jit(solution)/shard_map/ppermute | solution.py:217
  210.8 25.1 %collective-permute-start.29 = (bf16[2,2,2,64,1024]{4,3,2,1,0:T(8,128)(2,1)S(1)}, bf16[2,2,2,64,1024]{4,3,2,1,0:T(8,128)(2,1)S(1)}, u32[]{:S(2)}, u32[]{:S(2)}) collective-permute-start(bf16[2,2,2,64,1024]{4,3,2,1,0:T(8,128)(2,1)S(1)} %dynamic-slice_bitcast_fusion.1), channel_id=1, source_target_pairs={{0,1},{1,0},{2,3},{3,2},{4,5},{5,4},{6,7},{7,6},{8,9},{9,8},{10,11... | collective-permute-start | bytes 3145736 | tf_op jit(solution)/shard_map/ppermute | solution.py:212
  248.9 19.9 %collective-permute-start.34 = (bf16[2,2,64,1024]{3,2,1,0:T(8,128)(2,1)S(1)}, bf16[2,2,64,1024]{3,2,1,0:T(8,128)(2,1)S(1)}, u32[]{:S(2)}, u32[]{:S(2)}) collective-permute-start(bf16[2,2,64,1024]{3,2,1,0:T(8,128)(2,1)S(1)} %dynamic-slice_bitcast_fusion.6), channel_id=1, source_target_pairs={{0,1},{1,0},{2,3},{3,2},{4,5},{5,4},{6,7},{7,6},{8,9},{9,8},{10,11... | collective-permute-start | bytes 1572872 | tf_op jit(solution)/shard_map/ppermute | solution.py:212
  268.7 30.2 %collective-permute-start.36 = (bf16[2,2,2,64,1280]{4,3,2,1,0:T(8,128)(2,1)}, bf16[2,2,2,64,1280]{4,3,2,1,0:T(8,128)(2,1)}, u32[]{:S(2)}, u32[]{:S(2)}) collective-permute-start(bf16[2,2,2,64,1280]{4,3,2,1,0:T(8,128)(2,1)} %dynamic-slice_bitcast_fusion), channel_id=1, source_target_pairs={{0,1},{1,0},{2,3},{3,2},{4,5},{5,4},{6,7},{7,6},{8,9},{9,8},{10,11... | collective-permute-start | bytes 3932168 | tf_op jit(solution)/shard_map/ppermute | solution.py:212
  270.0 29.7 %collective-permute-start.37 = (bf16[2,2,2,64,1280]{4,3,1,0,2:T(8,128)(2,1)}, bf16[2,2,2,64,1280]{4,3,1,0,2:T(8,128)(2,1)}, u32[]{:S(2)}, u32[]{:S(2)}) collective-permute-start(bf16[2,2,2,64,1280]{4,3,1,0,2:T(8,128)(2,1)} %bitcast.319), channel_id=1, source_target_pairs={{0,4},{4,0},{8,12},{12,8},{16,20},{20,16},{24,28},{28,24},{1,5},{5... | collective-permute-start | bytes 3932168 | tf_op jit(solution)/shard_map/ppermute | solution.py:217
  273.7 52.4 %collective-permute-start.42 = (f32[6,1024]{1,0:T(8,128)S(1)}, f32[6,1024]{1,0:T(8,128)S(1)}, u32[]{:S(2)}, u32[]{:S(2)}) collective-permute-start(f32[6,1024]{1,0:T(8,128)S(1)} %stack.453), channel_id=1, source_target_pairs={{0,2},{2,0},{1,3},{3,1},{4,6},{6,4},{5,7},{7,5},{8,10},{10,8},{9,1... | collective-permute-start | bytes 73736 | tf_op jit(solution)/shard_map/ppermute | solution.py:208
  292.8 33.3 %collective-permute-start.38 = (bf16[2,64,1024]{2,1,0:T(8,128)(2,1)S(1)}, bf16[2,64,1024]{2,1,0:T(8,128)(2,1)S(1)}, u32[]{:S(2)}, u32[]{:S(2)}) collective-permute-start(bf16[2,64,1024]{2,1,0:T(8,128)(2,1)S(1)} %get-tuple-element.443), channel_id=1, source_target_pairs={{0,16},{1,18},{2,17},{3,19},{4,20},{5,22},{6,21},{7,23},{8,24},{9,... | collective-permute-start | bytes 786440 | tf_op jit(solution)/shard_map/ppermute | solution.py:200
  293.8 32.3 %collective-permute-start.39 = (bf16[2,64,1024]{2,1,0:T(8,128)(2,1)S(1)}, bf16[2,64,1024]{2,1,0:T(8,128)(2,1)S(1)}, u32[]{:S(2)}, u32[]{:S(2)}) collective-permute-start(bf16[2,64,1024]{2,1,0:T(8,128)(2,1)S(1)} %get-tuple-element.442), channel_id=1, source_target_pairs={{1,2},{2,1},{5,6},{6,5},{9,10},{10,9},{13,14},{14,13},{17,18},{18,... | collective-permute-start | bytes 786440 | tf_op jit(solution)/shard_map/ppermute | solution.py:191
  302.5 23.6 %collective-permute-start.41 = (bf16[2,2,64,1280]{3,2,1,0:T(8,128)(2,1)S(1)}, bf16[2,2,64,1280]{3,2,1,0:T(8,128)(2,1)}, u32[]{:S(2)}, u32[]{:S(2)}) collective-permute-start(bf16[2,2,64,1280]{3,2,1,0:T(8,128)(2,1)S(1)} %dynamic-slice_bitcast_fusion.4), channel_id=1, source_target_pairs={{0,1},{1,0},{2,3},{3,2},{4,5},{5,4},{6,7},{7,6},{8,9},{9,8},{10,11... | collective-permute-start | bytes 1966088 | tf_op jit(solution)/shard_map/ppermute | solution.py:212
  305.0 21.2 %collective-permute-start.40 = (bf16[2,2,64,1280]{3,2,1,0:T(8,128)(2,1)S(1)}, bf16[2,2,64,1280]{3,2,1,0:T(8,128)(2,1)}, u32[]{:S(2)}, u32[]{:S(2)}) collective-permute-start(bf16[2,2,64,1280]{3,2,1,0:T(8,128)(2,1)S(1)} %dynamic-slice_bitcast_fusion.5), channel_id=1, source_target_pairs={{0,4},{4,0},{8,12},{12,8},{16,20},{20,16},{24,28},{28,24},{1,5},{5... | collective-permute-start | bytes 1966088 | tf_op jit(solution)/shard_map/ppermute | solution.py:217
  333.7 21.6 %collective-permute-start.46 = (bf16[2,2,2,64,768]{4,3,1,0,2:T(8,128)(2,1)S(1)}, bf16[2,2,2,64,768]{4,3,1,0,2:T(8,128)(2,1)S(1)}, u32[]{:S(2)}, u32[]{:S(2)}) collective-permute-start(bf16[2,2,2,64,768]{4,3,1,0,2:T(8,128)(2,1)S(1)} %bitcast.378), channel_id=1, source_target_pairs={{0,4},{4,0},{8,12},{12,8},{16,20},{20,16},{24,28},{28,24},{1,5},{5... | collective-permute-start | bytes 2359304 | tf_op jit(solution)/shard_map/ppermute | solution.py:217
  334.9 20.4 %collective-permute-start.45 = (bf16[2,2,2,64,768]{4,3,2,1,0:T(8,128)(2,1)S(1)}, bf16[2,2,2,64,768]{4,3,2,1,0:T(8,128)(2,1)S(1)}, u32[]{:S(2)}, u32[]{:S(2)}) collective-permute-start(bf16[2,2,2,64,768]{4,3,2,1,0:T(8,128)(2,1)S(1)} %dynamic-slice_bitcast_fusion.2), channel_id=1, source_target_pairs={{0,1},{1,0},{2,3},{3,2},{4,5},{5,4},{6,7},{7,6},{8,9},{9,8},{10,11... | collective-permute-start | bytes 2359304 | tf_op jit(solution)/shard_map/ppermute | solution.py:212
  347.0 32.2 %collective-permute-start.52 = (bf16[2,64,1280]{2,1,0:T(8,128)(2,1)S(1)}, bf16[2,64,1280]{2,1,0:T(8,128)(2,1)S(1)}, u32[]{:S(2)}, u32[]{:S(2)}) collective-permute-start(bf16[2,64,1280]{2,1,0:T(8,128)(2,1)S(1)} %get-tuple-element.433), channel_id=1, source_target_pairs={{0,16},{1,18},{2,17},{3,19},{4,20},{5,22},{6,21},{7,23},{8,24},{9,... | collective-permute-start | bytes 983048 | tf_op jit(solution)/shard_map/ppermute | solution.py:200
  353.4 25.8 %collective-permute-start.53 = (bf16[2,64,1280]{2,1,0:T(8,128)(2,1)S(1)}, bf16[2,64,1280]{2,1,0:T(8,128)(2,1)S(1)}, u32[]{:S(2)}, u32[]{:S(2)}) collective-permute-start(bf16[2,64,1280]{2,1,0:T(8,128)(2,1)S(1)} %get-tuple-element.432), channel_id=1, source_target_pairs={{1,2},{2,1},{5,6},{6,5},{9,10},{10,9},{13,14},{14,13},{17,18},{18,... | collective-permute-start | bytes 983048 | tf_op jit(solution)/shard_map/ppermute | solution.py:191
  (150 other events, 1103.1 us)
